TPU v7x, 32 devices: a whole 2x2x4 slice. The times are simulated.
32 devices in a mesh: seq: 4 (over y, x), ctx: 8 (over z, core).
Axes of the slice: x: 2, y: 2, z: 4, core: 2. Of those that a mesh axis runs over, the one named last changes fastest.
Arguments:
- states: bfloat16 [4096, 1280], P(('seq', 'ctx')), may hold values from -0.15625 to 0.15625
- cotangent: bfloat16 [4096, 1280], P(('seq', 'ctx')), may hold values from -6 to 6
- attn_weights: float32 [1280, 5120], P(('seq', 'ctx')), may hold values from -0.15625 to 0.15625
- mlp_weights: float32 [1280, 15360], P(('seq', 'ctx')), may hold values from -0.15625 to 0.15625
- feature_gains: float32 [1280, 3], replicated, may hold values from 0.5 to 2
- unit_gains: float32 [5120, 2], replicated, may hold values from 0.5 to 2
- block_place: int32 [4, 8], P('seq'), may hold values from 0 to 7, each once within a row
Outputs:
- out_states: bfloat16 [4096, 1280], P(('seq', 'ctx'))
- grad_states: bfloat16 [4096, 1280], P(('seq', 'ctx'))
- grad_attn: float32 [1280, 5120], P(('seq', 'ctx'))
- grad_mlp: float32 [1280, 15360], P(('seq', 'ctx'))
- grad_feature_gains: float32 [1280, 3], P(('seq', 'ctx'))
- grad_unit_gains: float32 [5120, 2], P(('seq', 'ctx'))
Inputs may be any that keep to these rules, and one draw needn't show every extreme that they name: Each row of block_place is a permutation of 0 to 7.
All inputs are finite; a program needn't handle non-finite values.
Results may differ from a plain program's by a relative error of at most 0.02.
The roundings to bfloat16 on the way count: a program that leaves them out, or rounds other values in their place, can miss the bound.
Values may be sent and summed in bfloat16 or wider, within the bound.
A program may use at most 384 MiB of HBM per device.

v0:
```python
import math

import jax
import jax.numpy as jnp
from jax import lax
from jax.sharding import PartitionSpec as P

D = 1280
HEADS = 20
HEAD_DIM = 64


EPSILON = 1e-06
NEG_LARGE = -1e30


def unit_rows(values_in):
    factor = lax.rsqrt(jnp.sum(values_in * values_in, axis=-1, keepdims=True) + EPSILON)
    return (values_in * factor, factor)


def unit_back(normed, factor, upstream):
    return factor * (upstream - normed * jnp.sum(upstream * normed, axis=-1, keepdims=True))


def contract_rows(left_mat, right_mat):
    return lax.dot_general(
        left_mat, right_mat, (((0,), (0,)), ((), ())), preferred_element_type=jnp.float32
    )


def contract_cols(left_mat, right_mat):
    return lax.dot_general(
        left_mat, right_mat, (((1,), (1,)), ((), ())), preferred_element_type=jnp.float32
    )


def shards(states, cotangent, attn_weights, mlp_weights, feature_gains, unit_gains, block_place):
    tok_rows = states.shape[0]
    model_width = states.shape[1]
    ff_width = unit_gains.shape[0]
    score_scale = math.sqrt(HEAD_DIM)
    gate_factor = unit_gains[:, 1] * math.sqrt(D)
    w_attn = lax.all_gather(attn_weights.astype(jnp.bfloat16), ("seq", "ctx"), axis=0, tiled=True)
    w_mlp = lax.all_gather(mlp_weights.astype(jnp.bfloat16), ("seq", "ctx"), axis=0, tiled=True)
    states_full = states.astype(jnp.float32)
    projected = jnp.dot(states, w_attn[:, : 3 * model_width], preferred_element_type=jnp.float32)
    head_shape = (tok_rows, HEADS, HEAD_DIM)
    qk_gain = feature_gains[:, 0].reshape(HEADS, HEAD_DIM)
    query_unit, query_factor = unit_rows(projected[:, :model_width].reshape(head_shape))
    key_unit, key_factor = unit_rows(
        projected[:, model_width : 2 * model_width].reshape(head_shape)
    )
    query_low = (query_unit * qk_gain).astype(jnp.bfloat16)
    key_low = (key_unit * qk_gain).astype(jnp.bfloat16).reshape(tok_rows, model_width)
    value_low = projected[:, 2 * model_width :].astype(jnp.bfloat16)
    keys_all, values_all = (
        lax.all_gather(key_low, "ctx", axis=0, tiled=True),
        lax.all_gather(value_low, "ctx", axis=0, tiled=True),
    )
    seq_len = keys_all.shape[0]
    ctx_lanes = jnp.arange(lax.axis_size("ctx"), dtype=jnp.int32)
    places = block_place[0]
    own_block = jnp.sum(jnp.where(ctx_lanes == lax.axis_index("ctx"), places, 0))
    query_pos = own_block * tok_rows + jnp.arange(tok_rows, dtype=jnp.int32)
    key_index = jnp.arange(seq_len, dtype=jnp.int32)
    key_owner = key_index // tok_rows
    key_pos = (
        jnp.sum(jnp.where(key_owner[:, None] == ctx_lanes[None, :], places[None, :], 0), axis=1)
        * tok_rows
        + key_index % tok_rows
    )
    kblock = min(512, seq_len)
    nblocks = seq_len // kblock
    key_blocks = keys_all.reshape(nblocks, kblock, HEADS, HEAD_DIM)
    value_blocks = values_all.reshape(nblocks, kblock, HEADS, HEAD_DIM)
    pos_blocks = key_pos.reshape(nblocks, kblock)

    def block_scores(key_rows, key_places):
        raw_scores = score_scale * jnp.einsum(
            "qhd,khd->hqk", query_low, key_rows, preferred_element_type=jnp.float32
        )
        allowed = key_places[None, None, :] <= query_pos[None, :, None]
        return (raw_scores, allowed)

    def max_step(running, inputs):
        running_max, running_sum = running
        key_rows, key_places = inputs
        raw_scores, allowed = block_scores(key_rows, key_places)
        masked = jnp.where(allowed, raw_scores, NEG_LARGE)
        new_max = jnp.maximum(running_max, jnp.max(masked, axis=-1))
        powered = jnp.where(allowed, jnp.exp(masked - new_max[..., None]), 0.0)
        running_sum = running_sum * jnp.exp(running_max - new_max) + jnp.sum(powered, axis=-1)
        return ((new_max, running_sum), None)

    start_max = jnp.full((HEADS, tok_rows), NEG_LARGE, jnp.float32)
    start_sum = jnp.zeros((HEADS, tok_rows), jnp.float32)
    (final_max, final_sum), _ = lax.scan(max_step, (start_max, start_sum), (key_blocks, pos_blocks))
    log_total = final_max + jnp.log(final_sum)

    def value_step(accumulated, inputs):
        key_rows, value_rows, key_places = inputs
        raw_scores, allowed = block_scores(key_rows, key_places)
        weights_low = jnp.where(allowed, jnp.exp(raw_scores - log_total[..., None]), 0.0).astype(
            jnp.bfloat16
        )
        accumulated = accumulated + jnp.einsum(
            "hqk,khd->qhd", weights_low, value_rows, preferred_element_type=jnp.float32
        )
        return (accumulated, None)

    attended, _ = lax.scan(
        value_step, jnp.zeros(head_shape, jnp.float32), (key_blocks, value_blocks, pos_blocks)
    )
    attended_low = attended.reshape(tok_rows, model_width).astype(jnp.bfloat16)
    branch_attn = jnp.dot(
        attended_low, w_attn[:, 3 * model_width :], preferred_element_type=jnp.float32
    )
    attn_unit, attn_factor = unit_rows(branch_attn)
    alpha_attn = feature_gains[:, 1]
    mixed_one, mix_factor = unit_rows(states_full + alpha_attn * (attn_unit - states_full))
    mixed_low = mixed_one.astype(jnp.bfloat16)
    up_gate = jnp.dot(mixed_low, w_mlp[:, : 2 * ff_width], preferred_element_type=jnp.float32)
    up_scaled = up_gate[:, :ff_width] * unit_gains[:, 0]
    gate_scaled = up_gate[:, ff_width:] * gate_factor
    sigmoid_gate = jax.nn.sigmoid(gate_scaled)
    activated = gate_scaled * sigmoid_gate
    hidden = (activated * up_scaled).astype(jnp.bfloat16)
    branch_mlp = contract_cols(hidden, w_mlp[:, 2 * ff_width :])
    mlp_unit, mlp_factor = unit_rows(branch_mlp)
    alpha_mlp = feature_gains[:, 2]
    out_full, out_factor = unit_rows(mixed_one + alpha_mlp * (mlp_unit - mixed_one))
    grad_mix_two = unit_back(out_full, out_factor, cotangent.astype(jnp.float32))
    grad_alpha_m = jnp.sum(grad_mix_two * (mlp_unit - mixed_one), axis=0)
    grad_branch_mlp = unit_back(mlp_unit, mlp_factor, grad_mix_two * alpha_mlp).astype(jnp.bfloat16)
    grad_hidden = jnp.dot(
        grad_branch_mlp, w_mlp[:, 2 * ff_width :], preferred_element_type=jnp.float32
    )
    grad_up_scaled = grad_hidden * activated
    grad_gate_scaled = (
        grad_hidden * up_scaled * sigmoid_gate * (1.0 + gate_scaled * (1.0 - sigmoid_gate))
    )
    grad_s_u = jnp.sum(grad_up_scaled * up_gate[:, :ff_width], axis=0)
    grad_s_v = jnp.sum(grad_gate_scaled * up_gate[:, ff_width:], axis=0) * math.sqrt(D)
    grad_up_gate = jnp.concatenate(
        [grad_up_scaled * unit_gains[:, 0], grad_gate_scaled * gate_factor], axis=1
    ).astype(jnp.bfloat16)
    grad_mixed_one = grad_mix_two * (1.0 - alpha_mlp) + contract_cols(
        grad_up_gate, w_mlp[:, : 2 * ff_width]
    )
    grad_mix_one = unit_back(mixed_one, mix_factor, grad_mixed_one)
    grad_alpha_a = jnp.sum(grad_mix_one * (attn_unit - states_full), axis=0)
    grad_branch_attn = unit_back(attn_unit, attn_factor, grad_mix_one * alpha_attn).astype(
        jnp.bfloat16
    )
    grad_attended = (
        contract_cols(grad_branch_attn, w_attn[:, 3 * model_width :])
        .astype(jnp.bfloat16)
        .reshape(head_shape)
    )
    row_dots = jnp.einsum("qhd,qhd->hq", grad_attended.astype(jnp.float32), attended)

    def grad_step(grad_query, inputs):
        key_rows, value_rows, key_places = inputs
        raw_scores, allowed = block_scores(key_rows, key_places)
        probabilities = jnp.where(allowed, jnp.exp(raw_scores - log_total[..., None]), 0.0)
        grad_prob = jnp.einsum(
            "qhd,khd->hqk", grad_attended, value_rows, preferred_element_type=jnp.float32
        )
        grad_scores = (probabilities * (grad_prob - row_dots[..., None])).astype(jnp.bfloat16)
        grad_query = grad_query + score_scale * jnp.einsum(
            "hqk,khd->qhd", grad_scores, key_rows, preferred_element_type=jnp.float32
        )
        key_terms = score_scale * jnp.einsum(
            "hqk,qhd->khd", grad_scores, query_low, preferred_element_type=jnp.float32
        )
        value_terms = jnp.einsum(
            "hqk,qhd->khd",
            probabilities.astype(jnp.bfloat16),
            grad_attended,
            preferred_element_type=jnp.float32,
        )
        return (grad_query, (key_terms, value_terms))

    grad_query_low, (key_terms, value_terms) = lax.scan(
        grad_step, jnp.zeros(head_shape, jnp.float32), (key_blocks, value_blocks, pos_blocks)
    )
    key_terms = key_terms.reshape(seq_len, model_width)
    value_terms = value_terms.reshape(seq_len, model_width)
    own_key_grad, own_value_grad = (
        lax.psum_scatter(
            key_terms.astype(jnp.bfloat16), "ctx", scatter_dimension=0, tiled=True
        ).astype(jnp.float32),
        lax.psum_scatter(
            value_terms.astype(jnp.bfloat16), "ctx", scatter_dimension=0, tiled=True
        ).astype(jnp.float32),
    )
    grad_key_low = own_key_grad.reshape(head_shape)
    grad_s_qk = jnp.sum(grad_query_low * query_unit + grad_key_low * key_unit, axis=0).reshape(
        model_width
    )
    grad_query_raw = unit_back(query_unit, query_factor, grad_query_low * qk_gain).reshape(
        tok_rows, model_width
    )
    grad_key_raw = unit_back(key_unit, key_factor, grad_key_low * qk_gain).reshape(
        tok_rows, model_width
    )
    grad_projected = jnp.concatenate([grad_query_raw, grad_key_raw, own_value_grad], axis=1).astype(
        jnp.bfloat16
    )
    grad_states = grad_mix_one * (1.0 - alpha_attn) + contract_cols(
        grad_projected, w_attn[:, : 3 * model_width]
    )
    feature_total = jnp.stack([grad_s_qk, grad_alpha_a, grad_alpha_m], axis=1)
    unit_fold = jnp.stack([grad_s_u, grad_s_v], axis=1).reshape(
        model_width, 2 * ff_width // model_width
    )
    attn_cols = 4 * model_width
    mlp_cols = 3 * ff_width
    attn_share = lax.psum_scatter(
        jnp.concatenate(
            [
                contract_rows(states, grad_projected),
                contract_rows(attended_low, grad_branch_attn),
                feature_total,
            ],
            axis=1,
        ),
        ("seq", "ctx"),
        scatter_dimension=0,
        tiled=True,
    )
    mlp_share = lax.psum_scatter(
        jnp.concatenate(
            [
                contract_rows(mixed_low, grad_up_gate),
                contract_rows(grad_branch_mlp, hidden),
                unit_fold,
            ],
            axis=1,
        ),
        ("seq", "ctx"),
        scatter_dimension=0,
        tiled=True,
    )
    grad_attn = attn_share[:, :attn_cols]
    grad_feature = attn_share[:, attn_cols:]
    grad_mlp = mlp_share[:, :mlp_cols]
    grad_unit = mlp_share[:, mlp_cols:].reshape(
        unit_gains.shape[0] // lax.axis_size(("seq", "ctx")), 2
    )
    return (
        out_full.astype(jnp.bfloat16),
        grad_states.astype(jnp.bfloat16),
        grad_attn,
        grad_mlp,
        grad_feature,
        grad_unit,
    )


def solution(mesh):
    in_specs = (
        P(("seq", "ctx"), None),
        P(("seq", "ctx"), None),
        P(("seq", "ctx"), None),
        P(("seq", "ctx"), None),
        P(),
        P(),
        P("seq", None),
    )
    out_specs = (
        P(("seq", "ctx"), None),
        P(("seq", "ctx"), None),
        P(("seq", "ctx"), None),
        P(("seq", "ctx"), None),
        P(("seq", "ctx"), None),
        P(("seq", "ctx"), None),
    )
    return jax.shard_map(shards, mesh=mesh, in_specs=in_specs, out_specs=out_specs, check_vma=False)
```

profile of v0, /device:TPU:0, one launch (start us, length us, event | category | flops | bytes accessed | tf_op | source)
XLA Modules:
  0.0 2192.5 jit_solution(11165288394254522064)
XLA Ops:
  9.2 103.5 %all-gather.5.cloned.1.call-done = bf16[1280,5120]{1,0:T(8,128)(2,1)} async-done(((bf16[40,5120]{1,0:T(8,128)(2,1)}), bf16[1280,5120]{1,0:T(8,128)(2,1)}) %all-gather.5.cloned.1.call-update) | async-done | bytes 13107216 | tf_op jit(solution)/shard_map/all_gather | solution.py:44
  112.7 5.4 fusion.89
  123.0 3.0 convert_element_type.82
  128.8 22.4 %all-gather.7.cloned.1.call-done = bf16[1024,1280]{1,0:T(8,128)(2,1)} async-done(((bf16[128,1280]{1,0:T(8,128)(2,1)}), bf16[1024,1280]{1,0:T(8,128)(2,1)}) %all-gather.7.cloned.1.call-update) | async-done | bytes 2621456 | tf_op jit(solution)/shard_map/all_gather | solution.py:59
  151.3 3.2 copy.88
  154.5 3.5 reshape.255
  158.0 4.0 copy.94
  162.0 24.3 %all-gather.9.cloned.1.call-done = bf16[1024,1280]{1,0:T(8,128)(2,1)} async-done(((bf16[128,1280]{1,0:T(8,128)(2,1)}), bf16[1024,1280]{1,0:T(8,128)(2,1)}) %all-gather.9.cloned.1.call-update) | async-done | bytes 2621456 | tf_op jit(solution)/shard_map/all_gather | solution.py:58
  186.3 3.0 copy.91
  189.3 3.5 reshape.257
  192.9 2.3 copy.95
  195.2 15.0 while.39
  195.4 3.6 fusion.179
  198.9 3.8 select_reduce_fusion.3
  202.9 3.5 fusion.179
  206.4 3.7 select_reduce_fusion.3
  210.2 8.3 while.40
  210.4 3.9 fusion.185
  214.4 4.1 fusion.185
  219.7 2.8 multiply_reduce_fusion.11
  224.4 186.3 %all-gather.11.cloned.1.call-done = bf16[1280,15360]{1,0:T(8,128)(2,1)} async-done(((bf16[40,15360]{1,0:T(8,128)(2,1)}), bf16[1280,15360]{1,0:T(8,128)(2,1)}) %all-gather.11.cloned.1.call-update) | async-done | bytes 39321616 | tf_op jit(solution)/shard_map/all_gather | solution.py:45
  410.8 10.6 fusion.81
  422.2 8.1 multiply_reduce_fusion.9
  432.2 7.3 multiply_reduce_fusion.1
  440.9 15.1 multiply_reduce_fusion.6
  459.7 3.9 fusion.105
  466.0 29.8 %while.41 = (s32[]{:T(128)}, f32[128,20,64]{0,2,1:T(8,128)}, bf16[2,512,20,64]{1,3,2,0:T(8,128)(2,1)}, bf16[2,512,20,64]{1,3,2,0:T(8,128)(2,1)}, bf16[2,512,20,6...) while((s32[]{:T(128)}, f32[128,20,64]{0,2,1:T(8,128)}, ...), condition=%wide.region_19.20_spmd.clone, body=%wide.region_18.19_spmd.clone.sunk | while | flops 853180544 | bytes 150973888 | solution.py:185
  469.8 2.1 fusion.197
  471.9 3.0 fusion.198
  475.9 2.4 copy-done.3
  484.3 2.1 fusion.197
  486.4 3.1 fusion.198
  490.6 2.4 copy-done.3
  495.8 4.4 copy.104
  500.9 2.9 copy.105
  503.8 4.4 copy.99
  509.0 2.7 copy.100
  516.7 4.9 fusion.137
  521.6 10.7 fusion.138
  532.3 21.9 fusion.108
  555.3 53.1 %pad_maximum_fusion = f32[1280,15368]{1,0:T(8,128)} fusion(f32[1280,8]{1,0:T(8,128)S(1)} %copy-done.24, f32[1280,5120]{1,0:T(8,128)} %fusion.138, f32[1280,10240]{1,0:T(8,128)} %fusion.108), kind=kLoop, calls=%fused_computation.68 | loop fusion | flops 39342080 | bytes 157368320 | tf_op jit(solution)/shard_map/concatenate | solution.py:234
  610.7 2.2 copy.102
  614.9 10.4 convolution_bitcast_fusion
  625.3 60.2 %concatenate.16 = f32[1280,5123]{0,1:T(8,128)} concatenate(f32[1280,3840]{0,1:T(8,128)} %convolution_bitcast_fusion, f32[1280,1280]{0,1:T(8,128)} %fusion.137, f32[1280,1]{0,1:T(1,128)S(1)} %stack_reshape.3, f32[1280,1]{0,1:T(1,128)S(1)} %stack.13, f32[1280,1]{0,1:T(1,128)S(1)} %stack.14), dimensions={1} | concatenate | bytes 52459520 | tf_op jit(solution)/shard_map/concatenate | solution.py:221
  686.7 8.6 fusion.102
  695.3 1479.0 %all-reduce.5.cloned.1.call-done = (f32[1280,5123]{0,1:T(8,128)}, f32[1280,15368]{1,0:T(8,128)}) async-done(((f32[1280,5123]{0,1:T(8,128)}, f32[1280,15368]{1,0:T(8,128)}), (f32[1280,5123]{0,1:T(8,128)}, f32[1280,15368]{1,0:T(8,128)})) %all-reduce.5.cloned.1.call-update) | async-done | bytes 104913936
  2174.3 3.2 constant_dynamic-slice_fusion.4
  2179.2 3.3 constant_dynamic-slice_fusion.3
  (233 shorter events, 54.3 us)
Async XLA Ops:
  7.2 105.5 %all-gather.5.cloned.1.call-start = ((), (), s32[]{:S(2)}) async-start(), calls=%async_computation.2 | async-start | bytes 13516800 | tf_op jit(solution)/shard_map/all_gather | solution.py:44
  9.2 109.9 %copy-start.50 = (f32[1280,3]{0,1:T(4,128)S(1)}, f32[1280,3]{0,1:T(4,128)}, u32[]{:S(2)}) copy-start(f32[1280,3]{0,1:T(4,128)} %param.17) | copy-start | bytes 46084
  9.2 142.1 %all-gather.7.cloned.1.call-start = ((), (), s32[]{:S(2)}) async-start(), calls=%async_computation.3 | async-start | bytes 2949120 | tf_op jit(solution)/shard_map/all_gather | solution.py:59
  118.1 3.7 copy-start.20
  119.0 67.4 %all-gather.9.cloned.1.call-start = ((), (), s32[]{:S(2)}) async-start(), calls=%async_computation.4 | async-start | bytes 2949120 | tf_op jit(solution)/shard_map/all_gather | solution.py:58
  119.1 7.0 copy-start.43
  119.1 338.9 %copy-start.39 = (f32[1280]{0:T(1024)}, f32[1280]{0:T(1024)S(1)}, u32[]{:S(2)}) copy-start(f32[1280]{0:T(1024)S(1)} %get-tuple-element.394) | copy-start | bytes 15364
  119.4 3.5 copy-start.7
  121.8 4.3 copy-start.15
  122.9 3.3 copy-start.51
  122.9 4.7 copy-start.49
  123.0 4.8 copy-start.32
  123.0 287.8 %all-gather.11.cloned.1.call-start = ((), (), s32[]{:S(2)}) async-start(), calls=%async_computation.5 | async-start | bytes 40550400 | tf_op jit(solution)/shard_map/all_gather | solution.py:45
  126.1 482.3 %reduce-scatter.4.cloned.1.call-start = ((), (), s32[]{:S(2)}) async-start(), calls=%async_computation.6 | async-start | bytes 2949120 | tf_op jit(solution)/shard_map/reduce_scatter | solution.py:191
  126.2 28.3 %copy-start.45 = (f32[20,64]{1,0:T(8,128)}, f32[20,64]{1,0:T(8,128)S(1)}, u32[]{:S(2)}) copy-start(f32[20,64]{1,0:T(8,128)S(1)} %mul.412) | copy-start | bytes 15364
  128.1 26.4 %copy-start.47 = (f32[128,20]{0,1:T(8,128)}, f32[128,20]{0,1:T(8,128)S(1)}, u32[]{:S(2)}) copy-start(f32[128,20]{0,1:T(8,128)S(1)} %add_rsqrt_fusion) | copy-start | bytes 30724
  218.5 4.8 copy-start.22
  219.7 4.8 copy-start.33
  422.2 8.1 copy-start.17
  422.2 8.1 copy-start.5
  422.2 8.4 copy-start.21
  432.2 7.4 copy-start.34
  455.9 2.9 copy-start.14
  466.5 3.3 copy-start.27
  467.9 3.9 copy-start.2
  471.8 3.0 copy-start.28
  471.9 4.0 copy-start.30
  474.8 3.4 copy-start.3
  475.9 3.7 copy-start.29
  478.3 2.8 copy-start.1
  481.1 3.3 copy-start.27
  482.5 3.9 copy-start.2
  486.4 3.2 copy-start.28
  486.4 4.2 copy-start.30
  489.6 3.4 copy-start.3
  490.6 3.7 copy-start.29
  493.0 2.8 copy-start.1
  511.8 103.1 %reduce-scatter.6.cloned.1.call-start = ((), (), s32[]{:S(2)}) async-start(), calls=%async_computation.7 | async-start | bytes 2949120 | tf_op jit(solution)/shard_map/reduce_scatter | solution.py:194
  516.6 4.9 copy-start.18
  516.6 5.0 copy-start.35
  521.6 10.7 copy-start.6
  521.6 10.7 copy-start.19
  554.2 55.3 %copy-start.8 = (f32[128,1280]{0,1:T(8,128)S(1)}, f32[128,1280]{0,1:T(8,128)}, u32[]{:S(2)}) copy-start(f32[128,1280]{0,1:T(8,128)} %copy-done.7) | copy-start | bytes 1966084
  554.2 55.3 %copy-start.42 = (f32[128,20]{0,1:T(8,128)S(1)}, f32[128,20]{0,1:T(8,128)}, u32[]{:S(2)}) copy-start(f32[128,20]{0,1:T(8,128)} %copy-done.41) | copy-start | bytes 30724
  554.2 1620.1 %all-reduce.5.cloned.1.call-start = ((), (), s32[]{:S(2)}) async-start(), calls=%async_computation.8 | async-start | bytes 211107840
  608.3 4.5 copy-start.11
  609.6 3.7 copy-start.16
  609.6 3.6 copy-start.44
  (20 other events, 24.3 us)
Sparse Core Ops, SparseCore 0:
  11.4 101.2 all-gather.4
  119.1 32.1 all-gather.6
  153.5 32.7 all-gather.8
  189.2 221.5 all-gather.10
  511.9 35.5 reduce-scatter.3
  554.3 35.5 reduce-scatter.5
  685.7 1488.5 all-reduce.4
where the time goes:
time: 2200 us; the launch traced here: 2190 us
  waiting for transfers between devices  1820 us (83%)
  matrix products  141 us (6%)
  local copies, waits for them, and re-layouts  137 us (6%)
  other arithmetic  81.8 us (4%)
    unnamed x8, waiting for transfers between devices  1480 us
    all_gather x1, waiting for transfers between devices, shards(): lax.all_gather(mlp_weights.astype(jnp.bfloat16), ('seq', 'ctx'), axis=0,...  186 us
    all_gather x1, waiting for transfers between devices, shards(): lax.all_gather(attn_weights.astype(jnp.bfloat16), ('seq', 'ctx'), axis=0,...  103 us
    concatenate x1, local copies, waits for them, and re-layouts, shards(): jnp.concatenate([contract_rows(states, grad_projected), contract_rows(att...  60.2 us
    concatenate x1, other arithmetic, shards(): jnp.concatenate([contract_rows(mixed_low, grad_up_gate), contract_rows(gr...  53.1 us
    dot_general x4, matrix products, contract_rows(): lax.dot_general(left_mat, right_mat, (((0,), (0,)), ((), ())), preferred_...  48 us
  transfers between devices with their start and end apart: 7, of which 5 were waited for; matrix products, arithmetic and copies ran while one was open for 8% of the time, Pallas kernels for 0%

commit v1 on v0

--- a/solution.py
+++ b/solution.py
@@ -35,7 +35,7 @@
     )
 
 
-def shards(states, cotangent, attn_weights, mlp_weights, feature_gains, unit_gains, block_place):
+def shards_general(states, cotangent, attn_weights, mlp_weights, feature_gains, unit_gains, block_place):
     tok_rows = states.shape[0]
     model_width = states.shape[1]
     ff_width = unit_gains.shape[0]
@@ -259,6 +259,245 @@
     )
 
 
+CORES = 2
+ALL = ("seq", "ctx")
+
+
+def fits(n_seq, chips):
+    return n_seq == 4 and chips == 4 and HEADS % chips == 0
+
+
+def chip_groups(chips):
+    return [[CORES * chip + core for chip in range(chips)] for core in range(CORES)]
+
+
+def core_groups(chips):
+    return [[CORES * chip + core for core in range(CORES)] for chip in range(chips)]
+
+
+def copy_groups(n_seq, chips):
+    return [
+        [(seq * chips + chip) * CORES + core for seq in range(n_seq) for core in range(CORES)]
+        for chip in range(chips)
+    ]
+
+
+def spread_weights(weights_low, parts, n_seq, chips):
+    rows, columns = weights_low.shape
+    share = columns // parts // chips
+    by_chip = weights_low.reshape(rows, parts, chips, share).transpose(2, 0, 1, 3)
+    by_chip = by_chip.reshape(chips, rows, parts * share)
+    mine = lax.all_to_all(
+        by_chip, "ctx", split_axis=0, concat_axis=0, tiled=True,
+        axis_index_groups=chip_groups(chips),
+    )
+    full = lax.all_gather(mine, ALL, axis=0, axis_index_groups=copy_groups(n_seq, chips))
+    full = full.reshape(n_seq, CORES, chips, rows, parts * share).transpose(0, 2, 1, 3, 4)
+    return full.reshape(n_seq * CORES * chips * rows, parts * share)
+
+
+def collect_grads(partial, parts, n_seq, chips):
+    rows = partial.shape[0] // (n_seq * CORES * chips)
+    share = partial.shape[1] // parts
+    by_owner = partial.astype(jnp.bfloat16).reshape(n_seq, chips, CORES, rows, parts * share)
+    by_owner = by_owner.transpose(0, 2, 1, 3, 4).reshape(n_seq * CORES * chips * rows, parts * share)
+    mine = lax.psum_scatter(
+        by_owner, ALL, scatter_dimension=0, tiled=True,
+        axis_index_groups=copy_groups(n_seq, chips),
+    ).reshape(chips, rows, parts * share)
+    back = lax.all_to_all(
+        mine, "ctx", split_axis=0, concat_axis=0, tiled=True,
+        axis_index_groups=chip_groups(chips),
+    )
+    back = back.reshape(chips, rows, parts, share).transpose(1, 2, 0, 3)
+    return back.reshape(rows, parts * chips * share).astype(jnp.float32)
+
+
+def shards_split(states, cotangent, attn_weights, mlp_weights, feature_gains, unit_gains, block_place):
+    tok_rows, model_width = states.shape
+    ff_width = unit_gains.shape[0]
+    n_seq, n_ctx = lax.axis_size("seq"), lax.axis_size("ctx")
+    chips = n_ctx // CORES
+    score_scale = math.sqrt(HEAD_DIM)
+    chip = lax.axis_index("ctx") // CORES
+    core = lax.axis_index("ctx") % CORES
+    heads = HEADS // chips
+    head_cols = heads * HEAD_DIM
+    units = ff_width // chips
+    group_rows = chips * tok_rows
+    chip_grp, core_grp = chip_groups(chips), core_groups(chips)
+
+    def gather_chips(own):
+        return lax.all_gather(own, "ctx", axis=0, tiled=True, axis_index_groups=chip_grp)
+
+    def sum_chips(partial):
+        return lax.psum_scatter(
+            partial.astype(jnp.bfloat16), "ctx", scatter_dimension=0, tiled=True,
+            axis_index_groups=chip_grp,
+        ).astype(jnp.float32)
+
+    def to_tokens(by_heads):
+        moved = lax.all_to_all(
+            by_heads.reshape(chips, tok_rows, head_cols), "ctx", split_axis=0, concat_axis=0,
+            tiled=True, axis_index_groups=chip_grp,
+        )
+        return moved.transpose(1, 0, 2).reshape(tok_rows, model_width)
+
+    def to_heads(by_tokens):
+        moved = lax.all_to_all(
+            by_tokens.reshape(tok_rows, chips, head_cols).transpose(1, 0, 2), "ctx",
+            split_axis=0, concat_axis=0, tiled=True, axis_index_groups=chip_grp,
+        )
+        return moved.reshape(group_rows, head_cols)
+
+    attn_low = attn_weights.astype(jnp.bfloat16)
+    w_qkv = spread_weights(attn_low[:, : 3 * model_width], 3, n_seq, chips)
+    w_mlp = spread_weights(mlp_weights.astype(jnp.bfloat16), 3, n_seq, chips)
+    w_out = lax.all_gather(attn_low[:, 3 * model_width :], ALL, axis=0, tiled=True)
+    states_all = gather_chips(states)
+
+    qk_gain = lax.dynamic_slice_in_dim(feature_gains[:, 0], chip * head_cols, head_cols)
+    qk_gain = qk_gain.reshape(heads, HEAD_DIM)
+    projected = jnp.dot(states_all, w_qkv, preferred_element_type=jnp.float32)
+    head_shape = (group_rows, heads, HEAD_DIM)
+    query_unit, query_factor = unit_rows(projected[:, :head_cols].reshape(head_shape))
+    key_unit, key_factor = unit_rows(projected[:, head_cols : 2 * head_cols].reshape(head_shape))
+    query_low = (query_unit * qk_gain).astype(jnp.bfloat16)
+    key_low = (key_unit * qk_gain).astype(jnp.bfloat16)
+    value_low = projected[:, 2 * head_cols :].astype(jnp.bfloat16).reshape(head_shape)
+    both = lax.all_gather(
+        jnp.stack([key_low, value_low]), "ctx", axis=1, tiled=True, axis_index_groups=core_grp
+    )
+    key_all, value_all = both[0], both[1]
+    places = block_place[0].reshape(chips, CORES)
+    offsets = jnp.arange(tok_rows, dtype=jnp.int32)
+    own_places = jnp.sum(
+        jnp.where(jnp.arange(CORES, dtype=jnp.int32)[None, :] == core, places, 0), axis=1
+    )
+    query_pos = (own_places[:, None] * tok_rows + offsets).reshape(group_rows)
+    key_pos = (places.T[:, :, None] * tok_rows + offsets).reshape(CORES * group_rows)
+    allowed = (key_pos[None, :] <= query_pos[:, None])[None]
+    scores = score_scale * jnp.einsum(
+        "qhd,khd->hqk", query_low, key_all, preferred_element_type=jnp.float32
+    )
+    masked = jnp.where(allowed, scores, NEG_LARGE)
+    row_max = jnp.max(masked, axis=-1, keepdims=True)
+    powered = jnp.where(allowed, jnp.exp(masked - row_max), 0.0)
+    row_sum = jnp.sum(powered, axis=-1, keepdims=True)
+    probabilities = powered / row_sum
+    weights_low = probabilities.astype(jnp.bfloat16)
+    attended = jnp.einsum("hqk,khd->qhd", weights_low, value_all, preferred_element_type=jnp.float32)
+    attended_own = to_tokens(attended.reshape(group_rows, head_cols).astype(jnp.bfloat16))
+
+    states_full = states.astype(jnp.float32)
+    branch_attn = jnp.dot(attended_own, w_out, preferred_element_type=jnp.float32)
+    attn_unit, attn_factor = unit_rows(branch_attn)
+    alpha_attn = feature_gains[:, 1]
+    mixed_one, mix_factor = unit_rows(states_full + alpha_attn * (attn_unit - states_full))
+
+    gain_u = lax.dynamic_slice_in_dim(unit_gains[:, 0], chip * units, units)
+    gain_v = lax.dynamic_slice_in_dim(unit_gains[:, 1], chip * units, units) * math.sqrt(D)
+    mixed_all = gather_chips(mixed_one.astype(jnp.bfloat16))
+    up_gate = jnp.dot(mixed_all, w_mlp[:, : 2 * units], preferred_element_type=jnp.float32)
+    up_scaled = up_gate[:, :units] * gain_u
+    gate_scaled = up_gate[:, units:] * gain_v
+    sigmoid_gate = jax.nn.sigmoid(gate_scaled)
+    activated = gate_scaled * sigmoid_gate
+    hidden = (activated * up_scaled).astype(jnp.bfloat16)
+    branch_mlp = sum_chips(contract_cols(hidden, w_mlp[:, 2 * units :]))
+    mlp_unit, mlp_factor = unit_rows(branch_mlp)
+    alpha_mlp = feature_gains[:, 2]
+    out_full, out_factor = unit_rows(mixed_one + alpha_mlp * (mlp_unit - mixed_one))
+    grad_mix_two = unit_back(out_full, out_factor, cotangent.astype(jnp.float32))
+    grad_alpha_m = jnp.sum(grad_mix_two * (mlp_unit - mixed_one), axis=0)
+    grad_branch_mlp = unit_back(mlp_unit, mlp_factor, grad_mix_two * alpha_mlp).astype(jnp.bfloat16)
+    grad_branch_all = gather_chips(grad_branch_mlp)
+    grad_hidden = jnp.dot(
+        grad_branch_all, w_mlp[:, 2 * units :], preferred_element_type=jnp.float32
+    )
+    grad_up_scaled = grad_hidden * activated
+    grad_gate_scaled = (
+        grad_hidden * up_scaled * sigmoid_gate * (1.0 + gate_scaled * (1.0 - sigmoid_gate))
+    )
+    grad_s_u = jnp.sum(grad_up_scaled * up_gate[:, :units], axis=0)
+    grad_s_v = jnp.sum(grad_gate_scaled * up_gate[:, units:], axis=0) * math.sqrt(D)
+    grad_up_gate = jnp.concatenate(
+        [grad_up_scaled * gain_u, grad_gate_scaled * gain_v], axis=1
+    ).astype(jnp.bfloat16)
+    grad_mixed_one = grad_mix_two * (1.0 - alpha_mlp) + sum_chips(
+        contract_cols(grad_up_gate, w_mlp[:, : 2 * units])
+    )
+    grad_mlp = collect_grads(
+        jnp.concatenate(
+            [contract_rows(mixed_all, grad_up_gate), contract_rows(grad_branch_all, hidden)], axis=1
+        ),
+        3, n_seq, chips,
+    )
+    grad_mix_one = unit_back(mixed_one, mix_factor, grad_mixed_one)
+    grad_alpha_a = jnp.sum(grad_mix_one * (attn_unit - states_full), axis=0)
+    grad_branch_attn = unit_back(attn_unit, attn_factor, grad_mix_one * alpha_attn).astype(
+        jnp.bfloat16
+    )
+    grad_out_proj = lax.psum_scatter(
+        contract_rows(attended_own, grad_branch_attn).astype(jnp.bfloat16), ALL,
+        scatter_dimension=0, tiled=True,
+    ).astype(jnp.float32)
+    grad_attended = to_heads(
+        contract_cols(grad_branch_attn, w_out).astype(jnp.bfloat16)
+    ).reshape(head_shape)
+    row_dots = jnp.einsum("qhd,qhd->hq", grad_attended.astype(jnp.float32), attended)
+    grad_prob = jnp.einsum(
+        "qhd,khd->hqk", grad_attended, value_all, preferred_element_type=jnp.float32
+    )
+    grad_scores = (probabilities * (grad_prob - row_dots[..., None])).astype(jnp.bfloat16)
+    grad_query_low = score_scale * jnp.einsum(
+        "hqk,khd->qhd", grad_scores, key_all, preferred_element_type=jnp.float32
+    )
+    key_terms = score_scale * jnp.einsum(
+        "hqk,qhd->khd", grad_scores, query_low, preferred_element_type=jnp.float32
+    )
+    value_terms = jnp.einsum(
+        "hqk,qhd->khd", weights_low, grad_attended, preferred_element_type=jnp.float32
+    )
+    summed = lax.psum_scatter(
+        jnp.stack([key_terms, value_terms]).astype(jnp.bfloat16), "ctx", scatter_dimension=1,
+        tiled=True, axis_index_groups=core_grp,
+    ).astype(jnp.float32)
+    grad_key_low, grad_value = summed[0], summed[1]
+    grad_s_qk = jnp.sum(grad_query_low * query_unit + grad_key_low * key_unit, axis=0)
+    grad_query_raw = unit_back(query_unit, query_factor, grad_query_low * qk_gain)
+    grad_key_raw = unit_back(key_unit, key_factor, grad_key_low * qk_gain)
+    grad_projected = jnp.concatenate(
+        [part.reshape(group_rows, head_cols) for part in (grad_query_raw, grad_key_raw, grad_value)],
+        axis=1,
+    ).astype(jnp.bfloat16)
+    grad_states = grad_mix_one * (1.0 - alpha_attn) + sum_chips(
+        contract_cols(grad_projected, w_qkv)
+    )
+    grad_qkv = collect_grads(contract_rows(states_all, grad_projected), 3, n_seq, chips)
+    slot = lambda own, width: lax.dynamic_update_slice_in_dim(
+        jnp.zeros((chips * width,), jnp.float32), own.reshape(width), chip * width, 0
+    )
+    small = jnp.concatenate(
+        [slot(grad_s_qk, head_cols), grad_alpha_a, grad_alpha_m, slot(grad_s_u, units), slot(grad_s_v, units)]
+    )
+    small = lax.psum(small, ALL)
+    rank = lax.axis_index(ALL)
+    feature = small[: 3 * model_width].reshape(3, model_width).T
+    unit = small[3 * model_width :].reshape(2, ff_width).T
+    devices = n_seq * n_ctx
+    grad_feature = lax.dynamic_slice_in_dim(feature, rank * (model_width // devices), model_width // devices)
+    grad_unit = lax.dynamic_slice_in_dim(unit, rank * (ff_width // devices), ff_width // devices)
+    return (
+        out_full.astype(jnp.bfloat16),
+        grad_states.astype(jnp.bfloat16),
+        jnp.concatenate([grad_qkv, grad_out_proj], axis=1),
+        grad_mlp,
+        grad_feature,
+        grad_unit,
+    )
+
+
 def solution(mesh):
     in_specs = (
         P(("seq", "ctx"), None),
@@ -277,4 +516,6 @@
         P(("seq", "ctx"), None),
         P(("seq", "ctx"), None),
     )
+    chips = mesh.shape["ctx"] // CORES
+    shards = shards_split if fits(mesh.shape["seq"], chips) else shards_general
     return jax.shard_map(shards, mesh=mesh, in_specs=in_specs, out_specs=out_specs, check_vma=False)

time: 2200 us -> 802 us (0.36)
  waiting for transfers between devices: 1820 us -> 442 us
  blocking collectives: 0 us -> 137 us
  local copies, waits for them, and re-layouts: 137 us -> 62.5 us
  matrix products: 141 us -> 72.2 us
  other arithmetic: 81.8 us -> 52.7 us
    unnamed x8 -> x14, waiting for transfers between devices: 1480 us -> 0.91 us
    reduce_scatter x2 -> x7, waiting for transfers between devices: 0.04 us -> 268 us  [the longest x1 117 us: shards_split(): lax.psum_scatter(contract_rows(attended_own, grad_branch_attn).astype(jnp...]
    all_gather x4 -> x7, waiting for transfers between devices: 337 us -> 154 us  [the longest x3 88.9 us: gather_chips(): lax.all_gather(own, 'ctx', axis=0, tiled=True, axis_index_groups=chip_grp)]
    psum x0 -> x1, blocking collectives: none -> 70.2 us  [shards_split(): small = lax.psum(small, ALL)]
    all_to_all x0 -> x3, blocking collectives: none -> 67.2 us  [the longest x2 54.3 us: spread_weights(): lax.all_to_all(by_chip, 'ctx', split_axis=0, concat_axis=0, tiled=True, a...]
    concatenate x1 -> x2, local copies, waits for them, and re-layouts: 60.2 us -> 8.47 us  [the longest x1 8.46 us: shards_split(): jnp.concatenate([contract_rows(mixed_all, grad_up_gate), contract_rows(gr...]
    concatenate x1 -> x2, other arithmetic: 53.1 us -> 6.18 us  [the longest x1 4.34 us: shards_split(): jnp.concatenate([contract_rows(mixed_all, grad_up_gate), contract_rows(gr...]
    dot_general x4, matrix products: 48 us -> 12.9 us  [contract_rows(): lax.dot_general(left_mat, right_mat, (((0,), (0,)), ((), ())), preferred_...]
  transfers between devices with their start and end apart: 7 -> 17, of which waited for: 5 -> 13; matrix products, arithmetic and copies ran while one was open for 8% -> 12% of each run, Pallas kernels for 0% -> 0%
where the time goes in v1:
time: 802 us; the launch traced here: 796 us
  waiting for transfers between devices  442 us (55%)
  blocking collectives  137 us (17%)
  matrix products  72.2 us (9%)
  local copies, waits for them, and re-layouts  62.5 us (8%)
  other arithmetic  52.7 us (7%)
  between operations  15.1 us (2%)
  starting transfers between devices  13.8 us (2%)
    reduce_scatter x1, waiting for transfers between devices, shards_split(): lax.psum_scatter(contract_rows(attended_own, grad_branch_attn).astype(jnp...  117 us
    all_gather x3, waiting for transfers between devices, gather_chips(): lax.all_gather(own, 'ctx', axis=0, tiled=True, axis_index_groups=chip_grp)  88.9 us
    reduce_scatter x2, waiting for transfers between devices, collect_grads(): lax.psum_scatter(by_owner, ALL, scatter_dimension=0, tiled=True, axis_ind...  82.4 us
    psum x1, blocking collectives, shards_split(): small = lax.psum(small, ALL)  70.2 us
    all_gather x2, waiting for transfers between devices, spread_weights(): lax.all_gather(mine, ALL, axis=0, axis_index_groups=copy_groups(n_seq, ch...  65.3 us
    reduce_scatter x3, waiting for transfers between devices, sum_chips(): lax.psum_scatter(partial.astype(jnp.bfloat16), 'ctx', scatter_dimension=0...  60.6 us
    all_to_all x2, blocking collectives, spread_weights(): lax.all_to_all(by_chip, 'ctx', split_axis=0, concat_axis=0, tiled=True, a...  54.3 us
    dot_general x4, matrix products, contract_cols(): lax.dot_general(left_mat, right_mat, (((1,), (1,)), ((), ())), preferred_...  18 us
  transfers between devices with their start and end apart: 17, of which 13 were waited for; matrix products, arithmetic and copies ran while one was open for 12% of the time, Pallas kernels for 0%

profile of v1, /device:TPU:0, one launch (start us, length us, event | category | flops | bytes accessed | tf_op | source)
XLA Modules:
  0.0 795.8 jit_solution(717401786088077970)
XLA Ops:
  9.4 16.5 %all_to_all.30 = bf16[4,40,960]{2,1,0:T(8,128)(2,1)} all-to-all(bf16[4,40,960]{2,1,0:T(8,128)(2,1)S(1)} %reshape.270), channel_id=1, replica_groups={{0,2,4,6},{1,3,5,7},{8,10,12,14},{9,11,13,15},{16,18,20,22},{17,19,21,2..., dimensions={0} | all-to-all | bytes 614400 | tf_op jit(solution)/shard_map/all_to_all | solution.py:290
  27.0 28.3 %all-gather.20.cloned.1.call-done = bf16[32,40,960]{2,1,0:T(8,128)(2,1)} async-done(((bf16[4,40,960]{2,1,0:T(8,128)(2,1)}), bf16[32,40,960]{2,1,0:T(8,128)(2,1)}) %all-gather.20.cloned.1.call-update) | async-done | bytes 2457616 | tf_op jit(solution)/shard_map/all_gather | solution.py:294
  55.3 3.6 copy.55
  58.9 30.7 %all-gather.10.cloned.1.call-done = bf16[512,1280]{1,0:T(8,128)(2,1)} async-done(((bf16[128,1280]{1,0:T(8,128)(2,1)}), bf16[512,1280]{1,0:T(8,128)(2,1)}) %all-gather.10.cloned.1.call-update) | async-done | bytes 1310736 | tf_op jit(solution)/shard_map/all_gather | solution.py:331
  89.6 3.6 fusion.64
  102.4 2.5 reshape.278
  104.9 37.8 %all_to_all.31 = bf16[4,40,3840]{2,1,0:T(8,128)(2,1)} all-to-all(bf16[4,40,3840]{2,1,0:T(8,128)(2,1)} %reshape.278), channel_id=1, replica_groups={{0,2,4,6},{1,3,5,7},{8,10,12,14},{9,11,13,15},{16,18,20,22},{17,19,21,2..., dimensions={0} | all-to-all | bytes 2457600 | tf_op jit(solution)/shard_map/all_to_all | solution.py:290
  144.8 6.6 fusion.48
  151.4 16.6 %fusion.63 = (f32[5,512]{1,0:T(8,128)S(1)}, f32[5,512,1024]{2,1,0:T(8,128)}) fusion(f32[5,512,1024]{2,1,0:T(8,128)} %fusion.48, pred[512,1024]{1,0:T(8,128)(4,1)S(1)} %broadcast_compare_fusion), kind=kOutput, calls=%fused_computation.155 | output fusion | flops 18351104 | bytes 21506048 | tf_op jit(solution)/shard_map/sub | solution.py:385
  168.0 5.4 fusion.11
  173.4 2.6 bitcast_convert_fusion
  176.8 3.6 all-to-all-start.1
  180.5 9.2 %all-to-all-done.1 = bf16[4,128,320]{1,2,0:T(8,128)(2,1)S(1)} async-done(((bf16[4,128,320]{1,2,0:T(8,128)(2,1)}), bf16[4,128,320]{1,2,0:T(8,128)(2,1)S(1)}, u32[]{:S(2)}, u32[]{:S(2)}) %all-to-all-start.1) | async-done | bytes 327712 | tf_op jit(solution)/shard_map/all_to_all | solution.py:340
  189.7 2.8 multiply_reduce_fusion.8
  194.1 36.9 %all-gather.22.cloned.1.call-done = bf16[32,40,3840]{2,1,0:T(8,128)(2,1)} async-done(((bf16[4,40,3840]{2,1,0:T(8,128)(2,1)}), bf16[32,40,3840]{2,1,0:T(8,128)(2,1)}) %all-gather.22.cloned.1.call-update) | async-done | bytes 9830416 | tf_op jit(solution)/shard_map/all_gather | solution.py:294
  231.0 8.1 %copy.59 = bf16[4,4,2,40,3840]{4,3,2,1,0:T(8,128)(2,1)} copy(bf16[4,4,2,40,3840]{4,3,1,2,0:T(8,128)(2,1)} %bitcast.157) | data formatting | bytes 19660800 | tf_op jit(solution)/shard_map/transpose | solution.py:295
  239.1 26.6 %all-gather.16.cloned.1.call-done = bf16[512,1280]{1,0:T(8,128)(2,1)} async-done(((bf16[128,1280]{1,0:T(8,128)(2,1)}), bf16[512,1280]{1,0:T(8,128)(2,1)}) %all-gather.16.cloned.1.call-update) | async-done | bytes 1310736 | tf_op jit(solution)/shard_map/all_gather | solution.py:331
  265.7 6.1 fusion.6
  275.3 4.9 convolution_convert_fusion.5
  280.2 30.3 %reduce-scatter.8.cloned.1.call-done = bf16[128,1280]{1,0:T(8,128)(2,1)} async-done(((bf16[512,1280]{1,0:T(8,128)(2,1)}), bf16[128,1280]{1,0:T(8,128)(2,1)}) %reduce-scatter.8.cloned.1.call-update) | async-done | bytes 327696 | tf_op jit(solution)/shard_map/reduce_scatter | solution.py:334
  316.4 31.6 %all-gather.18.cloned.1.call-done = bf16[512,1280]{1,0:T(8,128)(2,1)} async-done(((bf16[128,1280]{1,0:T(8,128)(2,1)}), bf16[512,1280]{1,0:T(8,128)(2,1)}) %all-gather.18.cloned.1.call-update) | async-done | bytes 1310736 | tf_op jit(solution)/shard_map/all_gather | solution.py:331
  348.0 6.9 multiply_reduce_fusion
  356.4 7.5 fusion.13
  363.9 30.3 %reduce-scatter.10.cloned.1.call-done = bf16[128,1280]{1,0:T(8,128)(2,1)} async-done(((bf16[512,1280]{1,0:T(8,128)(2,1)}), bf16[128,1280]{1,0:T(8,128)(2,1)}) %reduce-scatter.10.cloned.1.call-update) | async-done | bytes 327696 | tf_op jit(solution)/shard_map/reduce_scatter | solution.py:334
  399.9 13.0 %all_to_all.32 = bf16[4,128,320]{1,2,0:T(8,128)(2,1)S(1)} all-to-all(bf16[4,128,320]{1,2,0:T(8,128)(2,1)S(1)} %bitcast.173), channel_id=1, replica_groups={{0,2,4,6},{1,3,5,7},{8,10,12,14},{9,11,13,15},{16,18,20,22},{17,19,21,2..., dimensions={0} | all-to-all | bytes 655360 | tf_op jit(solution)/shard_map/all_to_all | solution.py:347
  413.3 3.6 fusion.21
  417.1 5.1 multiply_convert_fusion
  425.8 7.9 reduce-scatter.12.cloned.1.call-done
  438.0 3.0 fusion.41
  441.4 2.9 fusion.12
  444.2 4.5 copy.62
  448.7 3.6 copy.63
  453.7 3.4 convolution_convert_fusion.1
  457.1 4.0 convolution_convert_fusion
  461.0 4.3 pad_maximum_fusion
  465.4 8.5 %copy.75 = bf16[4,4,2,40,3840]{4,3,1,2,0:T(8,128)(2,1)} copy(bf16[4,4,2,40,3840]{4,3,2,1,0:T(8,128)(2,1)} %pad_maximum_fusion) | data formatting | bytes 19660800 | tf_op jit(solution)/shard_map/concatenate | solution.py:431
  474.9 4.4 convolution_convert_fusion.4
  479.4 2.7 convolution_convert_fusion.2
  482.2 15.2 %reduce-scatter.16.cloned.1.call-done = bf16[160,960]{1,0:T(8,128)(2,1)} async-done(((bf16[1280,960]{1,0:T(8,128)(2,1)}), bf16[160,960]{1,0:T(8,128)(2,1)}) %reduce-scatter.16.cloned.1.call-update) | async-done | bytes 307216 | tf_op jit(solution)/shard_map/reduce_scatter | solution.py:304
  497.4 4.6 all-to-all-start.4
  502.7 9.6 %all-to-all-done.4 = bf16[4,40,960]{2,1,0:T(8,128)(2,1)S(1)} async-done(((bf16[4,40,960]{2,1,0:T(8,128)(2,1)}), bf16[4,40,960]{2,1,0:T(8,128)(2,1)S(1)}, u32[]{:S(2)}, u32[]{:S(2)}) %all-to-all-start.4) | async-done | bytes 307232 | tf_op jit(solution)/shard_map/all_to_all | solution.py:308
  512.3 67.2 %reduce-scatter.20.cloned.1.call-done = bf16[160,3840]{1,0:T(8,128)(2,1)} async-done(((bf16[1280,3840]{1,0:T(8,128)(2,1)}), bf16[160,3840]{1,0:T(8,128)(2,1)}) %reduce-scatter.20.cloned.1.call-update) | async-done | bytes 1228816 | tf_op jit(solution)/shard_map/reduce_scatter | solution.py:304
  579.5 4.6 all-to-all-start.5
  584.2 70.2 %psum.7 = f32[14080]{0:T(1024)S(1)} all-reduce(f32[14080]{0:T(1024)S(1)} %constant_dynamic-update-slice_fusion), channel_id=1, replica_groups=mesh['seq'=4,'ctx'=8] {'seq','ctx'}, use_global_device_ids=true, to_apply=%region_27.28 | all-reduce | flops 14080 | bytes 112640 | tf_op jit(solution)/shard_map/psum | solution.py:484
  658.3 117.3 %reduce-scatter.18.cloned.1.call-done = bf16[40,1280]{1,0:T(8,128)(2,1)} async-done(((bf16[1280,1280]{1,0:T(8,128)(2,1)}), bf16[40,1280]{1,0:T(8,128)(2,1)}) %reduce-scatter.18.cloned.1.call-update) | async-done | bytes 102416 | tf_op jit(solution)/shard_map/reduce_scatter | solution.py:441
  777.4 2.8 reshape.291
  780.2 5.0 copy.67
  785.2 3.6 reshape.290
  (183 shorter events, 50.8 us)
Async XLA Ops:
  7.2 19.6 %copy-start.25 = (f32[1280,3]{0,1:T(4,128)S(1)}, f32[1280,3]{0,1:T(4,128)}, u32[]{:S(2)}) copy-start(f32[1280,3]{0,1:T(4,128)} %param.11) | copy-start | bytes 46084
  7.2 48.1 %all-gather.20.cloned.1.call-start = ((), (), s32[]{:S(2)}) async-start(), calls=%async_computation.25 | async-start | bytes 2949120 | tf_op jit(solution)/shard_map/all_gather | solution.py:294
  25.9 63.7 %all-gather.10.cloned.1.call-start = ((), (), s32[]{:S(2)}) async-start(), calls=%async_computation.13 | async-start | bytes 1638400 | tf_op jit(solution)/shard_map/all_gather | solution.py:331
  26.7 118.1 %all-gather.12.cloned.1.call-start = ((), (), s32[]{:S(2)}) async-start(), calls=%async_computation.14 | async-start | bytes 1966080 | tf_op jit(solution)/shard_map/all_gather | solution.py:368
  93.2 1.3 copy-start.13
  95.7 84.8 %all-gather.14.cloned.1.call-start = ((), (), s32[]{:S(2)}) async-start(), calls=%async_computation.15 | async-start | bytes 3379200 | tf_op jit(solution)/shard_map/all_gather | solution.py:356
  96.5 134.5 %all-gather.22.cloned.1.call-start = ((), (), s32[]{:S(2)}) async-start(), calls=%async_computation.26 | async-start | bytes 11059200 | tf_op jit(solution)/shard_map/all_gather | solution.py:294
  102.4 40.8 %copy-start.28 = (s32[1,8]{1,0:T(1,128)S(1)}, s32[1,8]{1,0:T(1,128)}, u32[]{:S(2)}) copy-start(s32[1,8]{1,0:T(1,128)} %param.13) | copy-start | bytes 100
  168.0 5.4 copy-start.10
  173.4 2.6 copy-start
  176.8 15.7 %copy-start.12 = (bf16[128,1280]{1,0:T(8,128)(2,1)S(1)}, bf16[128,1280]{1,0:T(8,128)(2,1)}, u32[]{:S(2)}) copy-start(bf16[128,1280]{1,0:T(8,128)(2,1)} %param.7) | copy-start | bytes 983044
  176.8 12.9 %all-to-all-start.1 = ((bf16[4,128,320]{1,2,0:T(8,128)(2,1)}), bf16[4,128,320]{1,2,0:T(8,128)(2,1)S(1)}, u32[]{:S(2)}, u32[]{:S(2)}) async-start(bf16[4,128,320]{1,2,0:T(8,128)(2,1)} %copy.57), calls=%async_computation.1 | async-start | bytes 655360 | tf_op jit(solution)/shard_map/all_to_all | solution.py:340
  180.5 85.3 %all-gather.16.cloned.1.call-start = ((), (), s32[]{:S(2)}) async-start(), calls=%async_computation.16 | async-start | bytes 1638400 | tf_op jit(solution)/shard_map/all_gather | solution.py:331
  189.7 2.8 copy-start.8
  189.7 4.2 copy-start.24
  193.7 116.9 %reduce-scatter.8.cloned.1.call-start = ((), (), s32[]{:S(2)}) async-start(), calls=%async_computation.17 | async-start | bytes 1638400 | tf_op jit(solution)/shard_map/reduce_scatter | solution.py:334
  271.9 2.3 copy-start.7
  274.2 1.1 copy-start.15
  280.2 32.9 %copy-start.19 = (bf16[128,1280]{1,0:T(8,128)(2,1)S(1)}, bf16[128,1280]{1,0:T(8,128)(2,1)}, u32[]{:S(2)}) copy-start(bf16[128,1280]{1,0:T(8,128)(2,1)} %param.8) | copy-start | bytes 983044
  280.2 67.8 %all-gather.18.cloned.1.call-start = ((), (), s32[]{:S(2)}) async-start(), calls=%async_computation.18 | async-start | bytes 1638400 | tf_op jit(solution)/shard_map/all_gather | solution.py:331
  310.6 2.8 copy-start.4
  316.3 77.9 %reduce-scatter.10.cloned.1.call-start = ((), (), s32[]{:S(2)}) async-start(), calls=%async_computation.19 | async-start | bytes 1638400 | tf_op jit(solution)/shard_map/reduce_scatter | solution.py:334
  354.8 1.1 copy-start.29
  355.0 1.3 copy-start.17
  363.9 69.8 %reduce-scatter.12.cloned.1.call-start = ((), (), s32[]{:S(2)}) async-start(), calls=%async_computation.20 | async-start | bytes 1966080 | tf_op jit(solution)/shard_map/reduce_scatter | solution.py:462
  395.7 2.8 copy-start.3
  397.4 0.9 copy-start.5
  413.3 3.7 copy-start.14
  413.3 3.8 copy-start.11
  422.2 2.3 copy-start.1
  425.7 71.7 %reduce-scatter.16.cloned.1.call-start = ((), (), s32[]{:S(2)}) async-start(), calls=%async_computation.22 | async-start | bytes 2949120 | tf_op jit(solution)/shard_map/reduce_scatter | solution.py:304
  433.6 4.3 copy-start.2
  435.0 6.4 copy-start.20
  438.0 3.3 copy-start.22
  438.0 3.3 copy-start.26
  452.3 1.3 copy-start.16
  452.4 4.7 copy-start.18
  452.4 127.2 %reduce-scatter.20.cloned.1.call-start = ((), (), s32[]{:S(2)}) async-start(), calls=%async_computation.24 | async-start | bytes 11059200 | tf_op jit(solution)/shard_map/reduce_scatter | solution.py:304
  453.7 3.4 copy-start.27
  453.7 3.4 copy-start.30
  473.8 1.0 copy-start.21
  473.9 1.1 copy-start.23
  473.9 5.5 copy-start.9
  473.9 181.9 %reduce-scatter.14.cloned.1.call-start = ((), (), s32[]{:S(2)}) async-start(), calls=%async_computation.21 | async-start | bytes 1638400 | tf_op jit(solution)/shard_map/reduce_scatter | solution.py:334
  479.4 296.2 %reduce-scatter.18.cloned.1.call-start = ((), (), s32[]{:S(2)}) async-start(), calls=%async_computation.23 | async-start | bytes 3379200 | tf_op jit(solution)/shard_map/reduce_scatter | solution.py:441
  482.2 173.6 %copy-start.6 = (f32[128,1280]{1,0:T(8,128)S(1)}, f32[128,1280]{1,0:T(8,128)}, u32[]{:S(2)}) copy-start(f32[128,1280]{1,0:T(8,128)} %copy-done.5) | copy-start | bytes 1966084
  497.4 14.9 %all-to-all-start.4 = ((bf16[4,40,960]{2,1,0:T(8,128)(2,1)}), bf16[4,40,960]{2,1,0:T(8,128)(2,1)S(1)}, u32[]{:S(2)}, u32[]{:S(2)}) async-start(bf16[4,40,960]{2,1,0:T(8,128)(2,1)} %bitcast.175), calls=%async_computation.9 | async-start | bytes 655360 | tf_op jit(solution)/shard_map/all_to_all | solution.py:308
  579.5 197.9 %all-to-all-start.5 = ((bf16[4,40,3840]{2,1,0:T(8,128)(2,1)}), bf16[4,40,3840]{2,1,0:T(8,128)(2,1)S(1)}, u32[]{:S(2)}, u32[]{:S(2)}) async-start(bf16[4,40,3840]{2,1,0:T(8,128)(2,1)} %bitcast.174), calls=%async_computation.12 | async-start | bytes 2457600 | tf_op jit(solution)/shard_map/all_to_all | solution.py:308
Sparse Core Ops, SparseCore 0:
  26.0 29.2 all-gather.19
  56.9 32.6 all-gather.9
  95.9 8.4 all-gather.11
  107.6 62.2 all-gather.13
  171.6 59.3 all-gather.21
  233.0 32.6 all-gather.15
  280.3 30.1 reduce-scatter.7
  316.4 31.4 all-gather.17
  364.0 30.1 reduce-scatter.9
  425.8 7.7 reduce-scatter.11
  452.5 44.8 reduce-scatter.15
  501.2 78.2 reduce-scatter.19
  582.5 49.6 reduce-scatter.13
  634.4 141.0 reduce-scatter.17

commit v2 on v1

--- a/solution.py
+++ b/solution.py
@@ -1,8 +1,11 @@
+import functools
 import math
 
 import jax
 import jax.numpy as jnp
 from jax import lax
+from jax.experimental import pallas as pl
+from jax.experimental.pallas import tpu as pltpu
 from jax.sharding import PartitionSpec as P
 
 D = 1280
@@ -313,6 +316,511 @@
     return back.reshape(rows, parts * chips * share).astype(jnp.float32)
 
 
+MESH = pl.DeviceIdType.MESH
+VMEM = pltpu.VMEM
+CHIPS = 4
+STEPS = (1, 2, 3)
+LIMIT = 60 * 1024 * 1024
+
+
+def place_of():
+    seq = lax.axis_index("seq")
+    ctx = lax.axis_index("ctx")
+    return seq, ctx // CORES, ctx % CORES
+
+
+def chip_peer(step):
+    seq, chip, core = place_of()
+    other = lax.rem(chip + step, CHIPS)
+    return (seq, other * CORES + core), other
+
+
+def seq_peer(step):
+    seq, chip, core = place_of()
+    other = seq ^ step
+    return (other, chip * CORES + core), other
+
+
+def twin():
+    seq, chip, core = place_of()
+    return (seq, chip * CORES + 1 - core)
+
+
+def meet():
+    devices = [chip_peer(step)[0] for step in STEPS] + [seq_peer(step)[0] for step in STEPS] + [twin()]
+    gate = pltpu.get_barrier_semaphore()
+    for device in devices:
+        pl.semaphore_signal(gate, inc=1, device_id=device, device_id_type=MESH)
+    pl.semaphore_wait(gate, len(devices))
+
+
+def remote(src, dst, send, recv, device):
+    return pltpu.make_async_remote_copy(
+        src_ref=src, dst_ref=dst, send_sem=send, recv_sem=recv, device_id=device,
+        device_id_type=MESH,
+    )
+
+
+def begin(copy):
+    copy.start()
+    return copy
+
+
+def rows_at(index, count):
+    return pl.ds(pl.multiple_of(index * count, count), count)
+
+
+def gather_line(src, dst_of, send, recv):
+    return [
+        begin(remote(src, dst_of, send.at[step], recv.at[step], chip_peer(step)[0])) for step in STEPS
+    ]
+
+
+def dot(left, right):
+    return jnp.dot(left, right, preferred_element_type=jnp.float32)
+
+
+def dot_nt(left, right):
+    return lax.dot_general(
+        left, right, (((1,), (1,)), ((), ())), preferred_element_type=jnp.float32
+    )
+
+
+def dot_tn(left, right):
+    return lax.dot_general(
+        left, right, (((0,), (0,)), ((), ())), preferred_element_type=jnp.float32
+    )
+
+
+def dma(*shape):
+    return pltpu.SemaphoreType.DMA(shape)
+
+
+def in_vmem():
+    return pl.BlockSpec(memory_space=pltpu.VMEM)
+
+
+def in_hbm():
+    return pl.BlockSpec(memory_space=pl.ANY)
+
+
+def attend_kernel(
+    states, qkv_src, mlp_src, qk_gain, query_pos, key_pos,
+    states_all, w_qkv, w_part, raw_out, query_out, both, att_out, inv_out, attx,
+    stage_q, low_q, stage_m, low_m, raw, att_low,
+    local_sem, x_send, x_recv, q_send, q_recv, mt_send, mt_recv, wz_send, wz_recv,
+    ws_send, ws_recv, wt_send, wt_recv, m_send, m_recv, kv_send, kv_recv, a_send, a_recv,
+):
+    seq, chip, core = place_of()
+    rows = qkv_src.shape[2]
+    half_cols = qkv_src.shape[3]
+    part_cols = half_cols // 3
+    tok_rows = states.shape[0]
+    heads = qk_gain.shape[0]
+    head_cols = heads * HEAD_DIM
+    group_rows = tok_rows * CHIPS
+    chip_rows = CORES * rows
+    seq_rows = CHIPS * chip_rows
+    half_units = w_part.shape[2]
+    ff_width = mlp_src.shape[1] // 3
+    meet()
+    block = rows_at(chip, tok_rows)
+    mine = rows_at(core, rows)
+    swaps = [
+        begin(remote(qkv_src.at[at, 1 - core], stage_q.at[at, mine], q_send.at[at], q_recv.at[at], twin()))
+        for at in range(CHIPS)
+    ]
+    keeps = [
+        begin(pltpu.make_async_copy(qkv_src.at[at, core], stage_q.at[at, mine], local_sem.at[at]))
+        for at in range(CHIPS)
+    ]
+    states_all[block, :] = states[...]
+    m_swaps, m_keeps = [], []
+    for part in range(3):
+        for at in range(CHIPS):
+            start = part * ff_width + at * CORES * half_units
+            theirs = pl.ds(pl.multiple_of(start + (1 - core) * half_units, 128), half_units)
+            ours = pl.ds(pl.multiple_of(start + core * half_units, 128), half_units)
+            there = stage_m.at[part, at, mine]
+            m_swaps.append(begin(remote(mlp_src.at[:, theirs], there, mt_send.at[part, at], mt_recv.at[part, at], twin())))
+            m_keeps.append(begin(pltpu.make_async_copy(mlp_src.at[:, ours], there, local_sem.at[CHIPS + part * CHIPS + at])))
+    for copy in keeps:
+        copy.wait()
+    for copy in swaps:
+        copy.wait()
+    low_q[...] = stage_q[...].astype(jnp.bfloat16)
+    my_rows = rows_at(seq * CHIPS + chip, chip_rows)
+    line = []
+    for step in STEPS:
+        device, other = chip_peer(step)
+        line.append(begin(remote(low_q.at[other], w_qkv.at[core, my_rows], wz_send.at[step], wz_recv.at[step], device)))
+    w_qkv[core, my_rows, :] = low_q[chip]
+    for copy in m_keeps:
+        copy.wait()
+    for copy in m_swaps:
+        copy.wait()
+    low_m[...] = stage_m[...].astype(jnp.bfloat16)
+    for copy in line:
+        copy.wait_recv()
+    sends = gather_line(states, states_all.at[block], x_send, x_recv)
+    seq_part = w_qkv.at[core, rows_at(seq, seq_rows)]
+    across = [
+        begin(remote(seq_part, seq_part, ws_send.at[step], ws_recv.at[step], seq_peer(step)[0]))
+        for step in STEPS
+    ]
+    for copy in across:
+        copy.wait_recv()
+    swap = begin(remote(w_qkv.at[core], w_qkv.at[core], wt_send.at[0], wt_recv.at[0], twin()))
+    swap.wait()
+    for copy in sends:
+        copy.wait_recv()
+    m_line = []
+    for part in range(3):
+        for step in STEPS:
+            device, other = chip_peer(step)
+            there = w_part.at[part, rows_at(chip, chip_rows)]
+            m_line.append(begin(remote(low_m.at[part, other], there, m_send.at[part, step], m_recv.at[part, step], device)))
+        w_part[part, rows_at(chip, chip_rows), :] = low_m[part, chip]
+
+    for half in range(CORES):
+        value = dot(states_all[...], w_qkv[half])
+        for which in range(3):
+            start = which * head_cols + half * part_cols
+            raw[:, start : start + part_cols] = value[:, which * part_cols : (which + 1) * part_cols]
+    for head in range(heads):
+        gain = qk_gain[head]
+        for which in range(2):
+            start = which * head_cols + head * HEAD_DIM
+            value = raw[:, start : start + HEAD_DIM]
+            factor = lax.rsqrt(jnp.sum(value * value, axis=-1, keepdims=True) + EPSILON)
+            low = (value * factor * gain).astype(jnp.bfloat16)
+            raw_out[which, head] = value
+            if which == 0:
+                query_out[head] = low * math.sqrt(HEAD_DIM)
+            else:
+                both[core, 0, head] = low
+        start = 2 * head_cols + head * HEAD_DIM
+        both[core, 1, head] = raw[:, start : start + HEAD_DIM].astype(jnp.bfloat16)
+    swap = begin(remote(both.at[core], both.at[core], kv_send.at[0], kv_recv.at[0], twin()))
+    swap.wait()
+
+    tile = min(128, group_rows)
+    tiles = group_rows // tile
+
+    def one_tile(index, carry):
+        head = index // tiles
+        at = rows_at(lax.rem(index, tiles), tile)
+        query = query_out[head, at, :]
+        allowed = key_pos[...] <= query_pos[at, :]
+        scores = jnp.concatenate([dot_nt(query, both[half, 0, head]) for half in range(CORES)], axis=1)
+        powered = jnp.exp(jnp.where(allowed, scores, NEG_LARGE))
+        inverse = 1.0 / jnp.sum(powered, axis=-1, keepdims=True)
+        weights = (powered * inverse).astype(jnp.bfloat16)
+        att_out[head, at, :] = sum(
+            dot(weights[:, half * group_rows : (half + 1) * group_rows], both[half, 1, head])
+            for half in range(CORES)
+        )
+        inv_out[head, at, :] = inverse
+        return carry
+
+    lax.fori_loop(0, heads * tiles, one_tile, 0)
+    for head in range(heads):
+        att_low[:, head * HEAD_DIM : (head + 1) * HEAD_DIM] = att_out[head].astype(jnp.bfloat16)
+    out = []
+    for step in STEPS:
+        device, other = chip_peer(step)
+        out.append(begin(remote(att_low.at[rows_at(other, tok_rows)], attx.at[chip], a_send.at[step], a_recv.at[step], device)))
+    attx[chip] = att_low[block, :]
+    for copy in out + m_line:
+        copy.wait()
+    for copy in sends + line + across:
+        copy.wait_send()
+
+
+def attend_call(states, qkv_src, mlp_src, qk_gain, query_pos, key_pos):
+    tok_rows, model_width = states.shape
+    chips, _, rows, half_cols = qkv_src.shape
+    heads = qk_gain.shape[0]
+    group_rows = chips * tok_rows
+    half_units = mlp_src.shape[1] // 3 // chips // CORES
+    f32, low = jnp.float32, jnp.bfloat16
+    shape = jax.ShapeDtypeStruct
+    return pl.pallas_call(
+        attend_kernel,
+        out_shape=[
+            shape((group_rows, model_width), low),
+            shape((CORES, model_width, half_cols), low),
+            shape((3, chips * CORES * rows, half_units), low),
+            shape((2, heads, group_rows, HEAD_DIM), f32),
+            shape((heads, group_rows, HEAD_DIM), low),
+            shape((CORES, 2, heads, group_rows, HEAD_DIM), low),
+            shape((heads, group_rows, HEAD_DIM), f32),
+            shape((heads, group_rows, 1), f32),
+            shape((chips, tok_rows, heads * HEAD_DIM), low),
+        ],
+        in_specs=[in_vmem(), in_hbm(), in_hbm(), in_vmem(), in_vmem(), in_vmem()],
+        out_specs=[in_vmem()] * 9,
+        scratch_shapes=[
+            VMEM((chips, CORES * rows, half_cols), f32),
+            VMEM((chips, CORES * rows, half_cols), low),
+            VMEM((3, chips, CORES * rows, half_units), f32),
+            VMEM((3, chips, CORES * rows, half_units), low),
+            VMEM((group_rows, 3 * heads * HEAD_DIM), f32),
+            VMEM((group_rows, heads * HEAD_DIM), low),
+            dma(16), dma(4), dma(4), dma(4), dma(4), dma(3, 4), dma(3, 4), dma(4), dma(4),
+            dma(4), dma(4), dma(1), dma(1), dma(3, 4), dma(3, 4), dma(1), dma(1), dma(4), dma(4),
+        ],
+        compiler_params=pltpu.CompilerParams(
+            collective_id=1, has_side_effects=True, vmem_limit_bytes=LIMIT
+        ),
+        name="attend",
+    )(states, qkv_src, mlp_src, qk_gain, query_pos, key_pos)
+
+
+def unit_of(value):
+    factor = lax.rsqrt(jnp.sum(value * value, axis=-1, keepdims=True) + EPSILON)
+    return value * factor, factor
+
+
+def mlp_kernel(
+    attx, states, cotangent, w_out, alpha_attn, alpha_mlp, gain_u, gain_v, w_part,
+    out, grad_attx, grad_w_out, grad_direct, dot_a, dot_m, dot_u, dot_v, grad_half,
+    weights, mixed_one, attn_unit, factors, mixed_low, mixed_all, up, gate, hidden, part,
+    sums, grad_two, branch_low, branch_all, grad_u, grad_v, wide, turned, arrived,
+    local_sem, ws_send, ws_recv, wt_send, wt_recv, x_send, x_recv, r_send, r_recv,
+    g_send, g_recv, b_send, b_recv, d_send, d_recv,
+):
+    seq, chip, core = place_of()
+    tok_rows, model_width = states.shape
+    chip_heads = attx.shape[2]
+    seq_rows = w_part.shape[1]
+    half_units = w_part.shape[2]
+    group_rows = CHIPS * tok_rows
+    block = rows_at(chip, tok_rows)
+    meet()
+    seq_at = rows_at(seq, seq_rows)
+
+    def spread(which):
+        return [
+            begin(remote(w_part.at[which], weights.at[which, core, seq_at], ws_send.at[which, step], ws_recv.at[which, step], seq_peer(step)[0]))
+            for step in STEPS
+        ]
+
+    across = spread(0) + spread(1)
+    keeps = [
+        begin(pltpu.make_async_copy(w_part.at[which], weights.at[which, core, seq_at], local_sem.at[which]))
+        for which in range(3)
+    ]
+    branch = sum(dot(attx[at], w_out[at]) for at in range(CHIPS))
+    unit, factor = unit_of(branch)
+    attn_unit[...] = unit
+    factors[0] = factor
+    base = states[...].astype(jnp.float32)
+    value, factor = unit_of(base + alpha_attn[...] * (unit - base))
+    mixed_one[...] = value
+    factors[1] = factor
+    mixed_low[...] = value.astype(jnp.bfloat16)
+    line = gather_line(mixed_low, mixed_all.at[block], x_send, x_recv)
+    mixed_all[block, :] = mixed_low[...]
+    for copy in keeps:
+        copy.wait()
+    for copy in across:
+        copy.wait_recv()
+    swaps = [
+        begin(remote(weights.at[which, core], weights.at[which, core], wt_send.at[which], wt_recv.at[which], twin()))
+        for which in range(2)
+    ]
+    across += spread(2)
+    for copy in line:
+        copy.wait_recv()
+    for copy in swaps:
+        copy.wait_recv()
+    for half in range(CORES):
+        up[half] = dot(mixed_all[...], weights[0, half])
+        gate[half] = dot(mixed_all[...], weights[1, half])
+    slab = min(64, group_rows)
+    slabs = group_rows // slab
+
+    def activate(index, carry):
+        half = index // slabs
+        at = rows_at(lax.rem(index, slabs), slab)
+        gated = gate[half, at, :] * gain_v[half]
+        scaled = up[half, at, :] * gain_u[half]
+        hidden[half, at, :] = (gated * jax.nn.sigmoid(gated) * scaled).astype(jnp.bfloat16)
+        return carry
+
+    lax.fori_loop(0, CORES * slabs, activate, 0)
+    for copy in across[-3:]:
+        copy.wait_recv()
+    swap = begin(remote(weights.at[2, core], weights.at[2, core], wt_send.at[2], wt_recv.at[2], twin()))
+    swaps.append(swap)
+    swap.wait_recv()
+    tile = model_width // 5
+
+    def down(index, carry):
+        at = rows_at(index, tile)
+        part[0, :, at] = sum(dot_nt(hidden[half], weights[2, half, at, :]) for half in range(CORES)).astype(jnp.bfloat16)
+        return carry
+
+    lax.fori_loop(0, model_width // tile, down, 0)
+
+    def reduce_line(which, send, recv):
+        sent = []
+        for step in STEPS:
+            device, other = chip_peer(step)
+            sent.append(begin(remote(part.at[which, rows_at(other, tok_rows)], sums.at[which, step], send.at[step], recv.at[step], device)))
+        return sent
+
+    def reduced(which):
+        total = part[which, block, :].astype(jnp.float32)
+        for step in STEPS:
+            total = total + sums[which, step].astype(jnp.float32)
+        return total
+
+    sent = reduce_line(0, r_send, r_recv)
+    for copy in sent:
+        copy.wait_recv()
+    mlp_unit, mlp_factor = unit_of(reduced(0))
+    value, factor = unit_of(mixed_one[...] + alpha_mlp[...] * (mlp_unit - mixed_one[...]))
+    out[...] = value.astype(jnp.bfloat16)
+    above = cotangent[...].astype(jnp.float32)
+    grad = factor * (above - value * jnp.sum(above * value, axis=-1, keepdims=True))
+    grad_two[...] = grad
+    dot_m[...] = jnp.sum(grad * (mlp_unit - mixed_one[...]), axis=0, keepdims=True)
+    grad = grad * alpha_mlp[...]
+    grad = mlp_factor * (grad - mlp_unit * jnp.sum(grad * mlp_unit, axis=-1, keepdims=True))
+    branch_low[...] = grad.astype(jnp.bfloat16)
+    back = gather_line(branch_low, branch_all.at[block], g_send, g_recv)
+    branch_all[block, :] = branch_low[...]
+    turned[0] = mixed_all[...].T
+    for copy in back:
+        copy.wait_recv()
+    for half in range(CORES):
+        wide[half] = dot(branch_all[...], weights[2, half])
+    dot_u[...] = jnp.zeros_like(dot_u)
+    dot_v[...] = jnp.zeros_like(dot_v)
+
+    def deactivate(index, carry):
+        half = index // slabs
+        at = rows_at(lax.rem(index, slabs), slab)
+        gated = gate[half, at, :] * gain_v[half]
+        scaled = up[half, at, :] * gain_u[half]
+        upstream = wide[half, at, :]
+        sig = jax.nn.sigmoid(gated)
+        to_up = upstream * (gated * sig)
+        to_gate = upstream * scaled * sig * (1.0 + gated * (1.0 - sig))
+        dot_u[half] += jnp.sum(to_up * up[half, at, :], axis=0, keepdims=True)
+        dot_v[half] += jnp.sum(to_gate * gate[half, at, :], axis=0, keepdims=True)
+        grad_u[half, at, :] = (to_up * gain_u[half]).astype(jnp.bfloat16)
+        grad_v[half, at, :] = (to_gate * gain_v[half]).astype(jnp.bfloat16)
+        return carry
+
+    lax.fori_loop(0, CORES * slabs, deactivate, 0)
+
+    def back_down(index, carry):
+        at = rows_at(index, tile)
+        part[1, :, at] = sum(
+            dot_nt(grad_u[half], weights[0, half, at, :]) + dot_nt(grad_v[half], weights[1, half, at, :])
+            for half in range(CORES)
+        ).astype(jnp.bfloat16)
+        return carry
+
+    lax.fori_loop(0, model_width // tile, back_down, 0)
+    for copy in swaps:
+        copy.wait_send()
+    sent += reduce_line(1, b_send, b_recv)
+    turned[1] = branch_all[...].T
+    pairs = ((0, grad_u), (1, grad_v), (2, hidden))
+    swaps = []
+    for which, right in pairs:
+        left = 1 if which == 2 else 0
+
+        def weight_grad(index, carry, which=which, right=right, left=left):
+            half = index // 5
+            at = rows_at(lax.rem(index, 5), tile)
+            weights[which, half, at, :] = dot(turned[left, at, :], right[half]).astype(jnp.bfloat16)
+            return carry
+
+        lax.fori_loop(0, CORES * 5, weight_grad, 0)
+        swaps.append(begin(remote(weights.at[which, 1 - core], arrived.at[which], d_send.at[which], d_recv.at[which], twin())))
+    for copy in sent[3:]:
+        copy.wait_recv()
+    grad = grad_two[...] * (1.0 - alpha_mlp[...]) + reduced(1)
+    value = mixed_one[...]
+    grad = factors[1] * (grad - value * jnp.sum(grad * value, axis=-1, keepdims=True))
+    unit = attn_unit[...]
+    dot_a[...] = jnp.sum(grad * (unit - states[...].astype(jnp.float32)), axis=0, keepdims=True)
+    grad_direct[...] = grad * (1.0 - alpha_attn[...])
+    grad = grad * alpha_attn[...]
+    grad = factors[0] * (grad - unit * jnp.sum(grad * unit, axis=-1, keepdims=True))
+    low = grad.astype(jnp.bfloat16)
+    for at in range(CHIPS):
+        grad_attx[at] = dot_nt(low, w_out[at]).astype(jnp.bfloat16)
+        grad_w_out[at] = dot_tn(attx[at], low).astype(jnp.bfloat16)
+    for which in range(3):
+        swaps[which].wait_recv()
+        grad_half[which] = (
+            weights[which, core].astype(jnp.float32) + arrived[which].astype(jnp.float32)
+        ).astype(jnp.bfloat16)
+    for copy in across + line + sent + back + swaps:
+        copy.wait_send()
+
+
+def mlp_call(attx, states, cotangent, w_out, alpha_attn, alpha_mlp, gain_u, gain_v, w_part):
+    tok_rows, model_width = states.shape
+    chips, _, chip_heads = attx.shape
+    half_units = w_part.shape[2]
+    group_rows = chips * tok_rows
+    f32, low = jnp.float32, jnp.bfloat16
+    shape = jax.ShapeDtypeStruct
+    tokens, group = (tok_rows, model_width), (group_rows, model_width)
+    wide = (CORES, group_rows, half_units)
+    matrix = (model_width, half_units)
+    return pl.pallas_call(
+        mlp_kernel,
+        out_shape=[
+            shape(tokens, low),
+            shape(attx.shape, low),
+            shape((chips, chip_heads, model_width), low),
+            shape(tokens, f32),
+            shape((1, model_width), f32),
+            shape((1, model_width), f32),
+            shape((CORES, 1, half_units), f32),
+            shape((CORES, 1, half_units), f32),
+            shape((3,) + matrix, low),
+        ],
+        in_specs=[in_vmem()] * 8 + [in_hbm()],
+        out_specs=[in_vmem()] * 9,
+        scratch_shapes=[
+            VMEM((3, CORES) + matrix, low),
+            VMEM(tokens, f32),
+            VMEM(tokens, f32),
+            VMEM((2, tok_rows, 1), f32),
+            VMEM(tokens, low),
+            VMEM(group, low),
+            VMEM(wide, f32),
+            VMEM(wide, f32),
+            VMEM(wide, low),
+            VMEM((2,) + group, low),
+            VMEM((2, chips) + tokens, low),
+            VMEM(tokens, f32),
+            VMEM(tokens, low),
+            VMEM(group, low),
+            VMEM(wide, low),
+            VMEM(wide, low),
+            VMEM(wide, f32),
+            VMEM((2, model_width, group_rows), low),
+            VMEM((3,) + matrix, low),
+            dma(3), dma(3, 4), dma(3, 4), dma(3), dma(3), dma(4), dma(4), dma(4), dma(4),
+            dma(4), dma(4), dma(4), dma(4), dma(3), dma(3),
+        ],
+        compiler_params=pltpu.CompilerParams(
+            collective_id=2, has_side_effects=True, vmem_limit_bytes=LIMIT
+        ),
+        name="mlp",
+    )(attx, states, cotangent, w_out, alpha_attn, alpha_mlp, gain_u, gain_v, w_part)
+
+
 def shards_split(states, cotangent, attn_weights, mlp_weights, feature_gains, unit_gains, block_place):
     tok_rows, model_width = states.shape
     ff_width = unit_gains.shape[0]
@@ -350,25 +858,14 @@
         )
         return moved.reshape(group_rows, head_cols)
 
-    attn_low = attn_weights.astype(jnp.bfloat16)
-    w_qkv = spread_weights(attn_low[:, : 3 * model_width], 3, n_seq, chips)
-    w_mlp = spread_weights(mlp_weights.astype(jnp.bfloat16), 3, n_seq, chips)
-    w_out = lax.all_gather(attn_low[:, 3 * model_width :], ALL, axis=0, tiled=True)
-    states_all = gather_chips(states)
-
+    rows = attn_weights.shape[0]
+    qkv_src = attn_weights[:, : 3 * model_width].reshape(rows, 3, chips, CORES, head_cols // CORES)
+    qkv_src = qkv_src.transpose(2, 3, 0, 1, 4).reshape(chips, CORES, rows, -1)
+    w_out = lax.all_gather(
+        attn_weights[:, 3 * model_width :].astype(jnp.bfloat16), ALL, axis=0, tiled=True
+    )
     qk_gain = lax.dynamic_slice_in_dim(feature_gains[:, 0], chip * head_cols, head_cols)
     qk_gain = qk_gain.reshape(heads, HEAD_DIM)
-    projected = jnp.dot(states_all, w_qkv, preferred_element_type=jnp.float32)
-    head_shape = (group_rows, heads, HEAD_DIM)
-    query_unit, query_factor = unit_rows(projected[:, :head_cols].reshape(head_shape))
-    key_unit, key_factor = unit_rows(projected[:, head_cols : 2 * head_cols].reshape(head_shape))
-    query_low = (query_unit * qk_gain).astype(jnp.bfloat16)
-    key_low = (key_unit * qk_gain).astype(jnp.bfloat16)
-    value_low = projected[:, 2 * head_cols :].astype(jnp.bfloat16).reshape(head_shape)
-    both = lax.all_gather(
-        jnp.stack([key_low, value_low]), "ctx", axis=1, tiled=True, axis_index_groups=core_grp
-    )
-    key_all, value_all = both[0], both[1]
     places = block_place[0].reshape(chips, CORES)
     offsets = jnp.arange(tok_rows, dtype=jnp.int32)
     own_places = jnp.sum(
@@ -376,74 +873,53 @@
     )
     query_pos = (own_places[:, None] * tok_rows + offsets).reshape(group_rows)
     key_pos = (places.T[:, :, None] * tok_rows + offsets).reshape(CORES * group_rows)
+    head_shape = (group_rows, heads, HEAD_DIM)
+    states_all, w_halves, w_part, raw, query_h, both_h, att_h, inverse, attx = attend_call(
+        states, qkv_src, mlp_weights, qk_gain.reshape(heads, 1, HEAD_DIM),
+        query_pos.reshape(group_rows, 1), key_pos.reshape(1, CORES * group_rows),
+    )
+    w_qkv = w_halves.reshape(CORES, model_width, 3, head_cols // CORES).transpose(1, 2, 0, 3)
+    w_qkv = w_qkv.reshape(model_width, 3 * head_cols)
+    attended_own = attx.transpose(1, 0, 2).reshape(tok_rows, model_width)
+    attended = att_h.transpose(1, 0, 2)
+    query_low = query_h.transpose(1, 0, 2) / 8
+    key_all = both_h[:, 0].transpose(0, 2, 1, 3).reshape(CORES * group_rows, heads, HEAD_DIM)
+    value_all = both_h[:, 1].transpose(0, 2, 1, 3).reshape(CORES * group_rows, heads, HEAD_DIM)
+    query_unit, query_factor = unit_rows(raw[0].transpose(1, 0, 2))
+    key_unit, key_factor = unit_rows(raw[1].transpose(1, 0, 2))
     allowed = (key_pos[None, :] <= query_pos[:, None])[None]
     scores = score_scale * jnp.einsum(
         "qhd,khd->hqk", query_low, key_all, preferred_element_type=jnp.float32
     )
-    masked = jnp.where(allowed, scores, NEG_LARGE)
-    row_max = jnp.max(masked, axis=-1, keepdims=True)
-    powered = jnp.where(allowed, jnp.exp(masked - row_max), 0.0)
-    row_sum = jnp.sum(powered, axis=-1, keepdims=True)
-    probabilities = powered / row_sum
+    probabilities = jnp.where(allowed, jnp.exp(scores) * inverse, 0.0)
     weights_low = probabilities.astype(jnp.bfloat16)
-    attended = jnp.einsum("hqk,khd->qhd", weights_low, value_all, preferred_element_type=jnp.float32)
-    attended_own = to_tokens(attended.reshape(group_rows, head_cols).astype(jnp.bfloat16))
-
-    states_full = states.astype(jnp.float32)
-    branch_attn = jnp.dot(attended_own, w_out, preferred_element_type=jnp.float32)
-    attn_unit, attn_factor = unit_rows(branch_attn)
-    alpha_attn = feature_gains[:, 1]
-    mixed_one, mix_factor = unit_rows(states_full + alpha_attn * (attn_unit - states_full))
-
+    w_out_parts = w_out.reshape(chips, head_cols, model_width)
     gain_u = lax.dynamic_slice_in_dim(unit_gains[:, 0], chip * units, units)
     gain_v = lax.dynamic_slice_in_dim(unit_gains[:, 1], chip * units, units) * math.sqrt(D)
-    mixed_all = gather_chips(mixed_one.astype(jnp.bfloat16))
-    up_gate = jnp.dot(mixed_all, w_mlp[:, : 2 * units], preferred_element_type=jnp.float32)
-    up_scaled = up_gate[:, :units] * gain_u
-    gate_scaled = up_gate[:, units:] * gain_v
-    sigmoid_gate = jax.nn.sigmoid(gate_scaled)
-    activated = gate_scaled * sigmoid_gate
-    hidden = (activated * up_scaled).astype(jnp.bfloat16)
-    branch_mlp = sum_chips(contract_cols(hidden, w_mlp[:, 2 * units :]))
-    mlp_unit, mlp_factor = unit_rows(branch_mlp)
-    alpha_mlp = feature_gains[:, 2]
-    out_full, out_factor = unit_rows(mixed_one + alpha_mlp * (mlp_unit - mixed_one))
-    grad_mix_two = unit_back(out_full, out_factor, cotangent.astype(jnp.float32))
-    grad_alpha_m = jnp.sum(grad_mix_two * (mlp_unit - mixed_one), axis=0)
-    grad_branch_mlp = unit_back(mlp_unit, mlp_factor, grad_mix_two * alpha_mlp).astype(jnp.bfloat16)
-    grad_branch_all = gather_chips(grad_branch_mlp)
-    grad_hidden = jnp.dot(
-        grad_branch_all, w_mlp[:, 2 * units :], preferred_element_type=jnp.float32
-    )
-    grad_up_scaled = grad_hidden * activated
-    grad_gate_scaled = (
-        grad_hidden * up_scaled * sigmoid_gate * (1.0 + gate_scaled * (1.0 - sigmoid_gate))
-    )
-    grad_s_u = jnp.sum(grad_up_scaled * up_gate[:, :units], axis=0)
-    grad_s_v = jnp.sum(grad_gate_scaled * up_gate[:, units:], axis=0) * math.sqrt(D)
-    grad_up_gate = jnp.concatenate(
-        [grad_up_scaled * gain_u, grad_gate_scaled * gain_v], axis=1
-    ).astype(jnp.bfloat16)
-    grad_mixed_one = grad_mix_two * (1.0 - alpha_mlp) + sum_chips(
-        contract_cols(grad_up_gate, w_mlp[:, : 2 * units])
-    )
-    grad_mlp = collect_grads(
-        jnp.concatenate(
-            [contract_rows(mixed_all, grad_up_gate), contract_rows(grad_branch_all, hidden)], axis=1
-        ),
-        3, n_seq, chips,
-    )
-    grad_mix_one = unit_back(mixed_one, mix_factor, grad_mixed_one)
-    grad_alpha_a = jnp.sum(grad_mix_one * (attn_unit - states_full), axis=0)
-    grad_branch_attn = unit_back(attn_unit, attn_factor, grad_mix_one * alpha_attn).astype(
-        jnp.bfloat16
-    )
+    (
+        out_low, grad_attx, grad_w_out, grad_direct, grad_alpha_a, grad_alpha_m, grad_s_u, grad_s_v, grad_half
+    ) = mlp_call(
+        attx, states, cotangent, w_out_parts, feature_gains[:, 1].reshape(1, model_width),
+        feature_gains[:, 2].reshape(1, model_width), gain_u.reshape(CORES, 1, units // CORES),
+        gain_v.reshape(CORES, 1, units // CORES), w_part,
+    )
+    grad_s_v = grad_s_v * math.sqrt(D)
     grad_out_proj = lax.psum_scatter(
-        contract_rows(attended_own, grad_branch_attn).astype(jnp.bfloat16), ALL,
-        scatter_dimension=0, tiled=True,
+        grad_w_out.reshape(model_width, model_width), ALL, scatter_dimension=0, tiled=True
     ).astype(jnp.float32)
-    grad_attended = to_heads(
-        contract_cols(grad_branch_attn, w_out).astype(jnp.bfloat16)
+    halves = lax.psum_scatter(
+        grad_half.reshape(3, n_seq, -1, units // CORES), "seq", scatter_dimension=1, tiled=True
+    )
+    halves = halves.reshape(3, chips, -1, units // CORES).transpose(1, 0, 2, 3)
+    moved = lax.all_to_all(
+        halves, "ctx", split_axis=0, concat_axis=0, tiled=True, axis_index_groups=chip_grp
+    )
+    moved = lax.all_gather(moved, "ctx", axis=0, axis_index_groups=core_grp)
+    moved = moved.reshape(CORES, chips, 3, CORES, rows, units // CORES)
+    moved = lax.dynamic_index_in_dim(moved, core, 3, keepdims=False)
+    grad_mlp = moved.transpose(3, 2, 1, 0, 4).reshape(rows, 3 * ff_width).astype(jnp.float32)
+    grad_attended = lax.all_to_all(
+        grad_attx, "ctx", split_axis=0, concat_axis=0, tiled=True, axis_index_groups=chip_grp
     ).reshape(head_shape)
     row_dots = jnp.einsum("qhd,qhd->hq", grad_attended.astype(jnp.float32), attended)
     grad_prob = jnp.einsum(
@@ -471,7 +947,7 @@
         [part.reshape(group_rows, head_cols) for part in (grad_query_raw, grad_key_raw, grad_value)],
         axis=1,
     ).astype(jnp.bfloat16)
-    grad_states = grad_mix_one * (1.0 - alpha_attn) + sum_chips(
+    grad_states = grad_direct + sum_chips(
         contract_cols(grad_projected, w_qkv)
     )
     grad_qkv = collect_grads(contract_rows(states_all, grad_projected), 3, n_seq, chips)
@@ -479,7 +955,7 @@
         jnp.zeros((chips * width,), jnp.float32), own.reshape(width), chip * width, 0
     )
     small = jnp.concatenate(
-        [slot(grad_s_qk, head_cols), grad_alpha_a, grad_alpha_m, slot(grad_s_u, units), slot(grad_s_v, units)]
+        [slot(grad_s_qk, head_cols), grad_alpha_a.reshape(-1), grad_alpha_m.reshape(-1), slot(grad_s_u, units), slot(grad_s_v, units)]
     )
     small = lax.psum(small, ALL)
     rank = lax.axis_index(ALL)
@@ -489,7 +965,7 @@
     grad_feature = lax.dynamic_slice_in_dim(feature, rank * (model_width // devices), model_width // devices)
     grad_unit = lax.dynamic_slice_in_dim(unit, rank * (ff_width // devices), ff_width // devices)
     return (
-        out_full.astype(jnp.bfloat16),
+        out_low,
         grad_states.astype(jnp.bfloat16),
         jnp.concatenate([grad_qkv, grad_out_proj], axis=1),
         grad_mlp,

time: 802 us -> 670 us (0.84)
  waiting for transfers between devices: 442 us -> 160 us
  Pallas kernels: 0 us -> 266 us
  blocking collectives: 137 us -> 74.6 us
  matrix products: 72.2 us -> 29.4 us
    pallas_call x0 -> x2, Pallas kernels: none -> 266 us  [the longest x1 165 us: mlp_call(): pl.pallas_call(mlp_kernel, out_shape=[shape(tokens, low), shape(attx.shap...]
    all_gather x7 -> x2, waiting for transfers between devices: 154 us -> 6.93 us  [the longest x1 6.92 us: shards_split(): moved = lax.all_gather(moved, 'ctx', axis=0, axis_index_groups=core_grp)]
    reduce_scatter x2 -> x1, waiting for transfers between devices: 82.4 us -> 0.01 us  [collect_grads(): lax.psum_scatter(by_owner, ALL, scatter_dimension=0, tiled=True, axis_ind...]
    reduce_scatter x3 -> x1, waiting for transfers between devices: 60.6 us -> 0.02 us  [sum_chips(): lax.psum_scatter(partial.astype(jnp.bfloat16), 'ctx', scatter_dimension=0...]
    all_to_all x3 -> x1, blocking collectives: 67.2 us -> 34.4 us  [shards_split(): lax.all_to_all(halves, 'ctx', split_axis=0, concat_axis=0, tiled=True, ax...]
    psum x1, blocking collectives: 70.2 us -> 40.1 us  [shards_split(): small = lax.psum(small, ALL)]
    mul x2, other arithmetic: 1.93 us -> 29.5 us  [unit_back(): normed * jnp.sum(upstream * normed, axis=-1, keepdims=True)]
    dot_general x5 -> x0, matrix products: 21.9 us -> none  [the longest x1 6.85 us: shards_split(): jnp.dot(grad_branch_all, w_mlp[:, 2 * units:], preferred_element_type=jnp...]
  transfers between devices with their start and end apart: 17 -> 9, of which waited for: 13 -> 6; matrix products, arithmetic and copies ran while one was open for 12% -> 14% of each run, Pallas kernels for 0% -> 15%
where the time goes in v2:
time: 670 us; the launch traced here: 663 us
  Pallas kernels  266 us (40%)
  waiting for transfers between devices  160 us (24%)
  blocking collectives  74.6 us (11%)
  local copies, waits for them, and re-layouts  54.9 us (8%)
  other arithmetic  45.1 us (7%)
  matrix products  29.4 us (4%)
  starting transfers between devices  17.8 us (3%)
  between operations  14.9 us (2%)
    pallas_call x1, Pallas kernels, mlp_call(): pl.pallas_call(mlp_kernel, out_shape=[shape(tokens, low), shape(attx.shap...  165 us
    reduce_scatter x1, waiting for transfers between devices, shards_split(): lax.psum_scatter(grad_w_out.reshape(model_width, model_width), ALL, scatt...  130 us
    pallas_call x1, Pallas kernels, attend_call(): pl.pallas_call(attend_kernel, out_shape=[shape((group_rows, model_width),...  101 us
    psum x1, blocking collectives, shards_split(): small = lax.psum(small, ALL)  40.1 us
    all_to_all x1, blocking collectives, shards_split(): lax.all_to_all(halves, 'ctx', split_axis=0, concat_axis=0, tiled=True, ax...  34.4 us
    mul x2, other arithmetic, unit_back(): normed * jnp.sum(upstream * normed, axis=-1, keepdims=True)  29.5 us
    all_to_all x1, starting transfers between devices, shards_split(): lax.all_to_all(grad_attx, 'ctx', split_axis=0, concat_axis=0, tiled=True,...  14 us
  transfers between devices with their start and end apart: 9, of which 6 were waited for; matrix products, arithmetic and copies ran while one was open for 14% of the time, Pallas kernels for 15%

profile of v2, /device:TPU:0, one launch (start us, length us, event | category | flops | bytes accessed | tf_op | source)
XLA Modules:
  0.0 662.9 jit_solution(1513227302774309601)
XLA Ops:
  7.2 1.6 slice.118
  9.4 1.3 reduce.14
  11.0 1.4 slice_bitcast_fusion.4
  14.2 1.5 reshape.233
  16.2 1.6 reshape.234.qkv_src
  18.4 101.2 %attend.1 = (bf16[512,1280]{1,0:T(8,128)(2,1)}, bf16[2,1280,480]{2,1,0:T(8,128)(2,1)}, bf16[3,320,640]{2,1,0:T(8,128)(2,1)}, f32[2,5,512,64]{3,2,1,0:T(8,128)}, ...) custom-call(bf16[128,1280]{1,0:T(8,128)(2,1)} %states.3, ...), custom_call_target="tpu_custom_call" | custom-call | tf_op jit(solution)/shard_map/attend/pallas_call | solution.py:548
  119.7 1.9 slice_bitcast_fusion
  121.6 1.2 copy.120
  122.8 1.3 reshape.239
  124.1 1.2 copy.116
  125.7 1.7 reduce.3
  129.3 164.7 %mlp.1 = (bf16[128,1280]{1,0:T(8,128)(2,1)}, bf16[4,128,320]{2,1,0:T(8,128)(2,1)}, bf16[4,320,1280]{2,1,0:T(8,128)(2,1)}, f32[128,1280]{1,0:T(8,128)}, f32[1,128...) custom-call(bf16[4,128,320]{2,1,0:T(8,128)(2,1)} %get-tuple-element., ...), custom_call_target="tpu_custom_call" | custom-call | tf_op jit(solution)/shard_map/mlp/pallas_call | solution.py:779
  293.9 1.9 copy.118
  295.8 14.0 %all-to-all-start = ((bf16[4,128,320]{1,2,0:T(8,128)(2,1)}), bf16[4,128,320]{1,2,0:T(8,128)(2,1)S(1)}, u32[]{:S(2)}, u32[]{:S(2)}) async-start(bf16[4,128,320]{1,2,0:T(8,128)(2,1)} %copy.118), calls=%async_computation | async-start | bytes 655360 | tf_op jit(solution)/shard_map/all_to_all | solution.py:921
  309.8 5.5 fusion.28
  315.3 4.7 all-to-all-done
  321.6 1.8 multiply_reduce_fusion
  323.4 6.4 fusion.16
  330.8 4.1 multiply_convert_fusion
  334.9 2.3 copy-done.1
  337.2 2.0 fusion.8
  339.1 1.7 copy.126
  340.8 2.1 pad_maximum_fusion
  343.0 5.0 copy.134
  348.4 1.7 copy-done.3
  350.8 1.6 reduce-scatter.8.cloned.1.call-done
  354.5 16.3 %fusion.14 = bf16[512,5,64]{2,0,1:T(8,128)(2,1)} fusion(f32[2,5,512,64]{3,2,1,0:T(8,128)} %get-tuple-element.28, f32[5,64]{1,0:T(8,128)S(1)} %mul.196, f32[512,5]{0,1:T(8,128)S(1)} %get-tuple-element.59, bf16[2,512,5,64]{3,1,2,0:T(8,128)(2,1)} %reduce-scatter.8.cloned.1.call-done), kind=kOutput, calls=%fused_computation.22 | output fusion | flops 1804863 | bytes 2334720 | tf_op jit(solution)/shard_map/mul | solution.py:26
  370.8 2.1 copy.127
  372.9 4.5 fusion.20
  377.4 13.2 %fusion.15 = bf16[512,5,64]{2,0,1:T(8,128)(2,1)S(1)} fusion(f32[5,64,512]{1,2,0:T(8,128)S(1)} %get-tuple-element.56, f32[2,5,512,64]{3,2,1,0:T(8,128)S(1)} %copy-done.4, f32[5,64]{1,0:T(8,128)S(1)} %broadcast_multiply_fusion, f32[512,5]{0,1:T(8,128)S(1)} %get-tuple-element.60), kind=kOutput, calls=%fused_computation.23 | output fusion | flops 1477183 | bytes 5611520 | tf_op jit(solution)/shard_map/mul | solution.py:26
  391.6 4.4 convolution_convert_fusion
  396.0 3.0 copy.131
  399.0 1.8 copy.132
  400.9 3.2 copy.129
  405.3 2.6 convolution_convert_fusion.1
  408.6 7.2 %reduce-scatter.16.cloned.1.call-done = bf16[3,1,320,640]{3,2,0,1:T(8,128)(2,1)} async-done(((bf16[3,4,320,640]{3,2,0,1:T(8,128)(2,1)}), bf16[3,1,320,640]{3,2,0,1:T(8,128)(2,1)}) %reduce-scatter.16.cloned.1.call-update) | async-done | bytes 1228816
  415.8 1.4 copy.135
  417.3 34.4 %all_to_all.15 = bf16[4,3,80,640]{3,2,1,0:T(8,128)(2,1)} all-to-all(bf16[4,3,80,640]{3,2,1,0:T(8,128)(2,1)S(1)} %copy.135), channel_id=1, replica_groups={{0,2,4,6},{1,3,5,7},{8,10,12,14},{9,11,13,15},{16,18,20,22},{17,19,21,2..., dimensions={0} | all-to-all | bytes 2457600 | tf_op jit(solution)/shard_map/all_to_all | solution.py:914
  453.0 40.1 %psum.7 = f32[14080]{0:T(1024)S(1)} all-reduce(f32[14080]{0:T(1024)S(1)} %constant_dynamic-update-slice_fusion), channel_id=1, replica_groups=mesh['seq'=4,'ctx'=8] {'seq','ctx'}, use_global_device_ids=true, to_apply=%region_11.12 | all-reduce | flops 14080 | bytes 112640 | tf_op jit(solution)/shard_map/psum | solution.py:960
  494.5 3.5 all-to-all-start.1
  498.0 1.8 add_convert_fusion
  499.8 9.5 %all-to-all-done.1 = bf16[4,40,960]{2,1,0:T(8,128)(2,1)S(1)} async-done(((bf16[4,40,960]{2,1,0:T(8,128)(2,1)}), bf16[4,40,960]{2,1,0:T(8,128)(2,1)S(1)}, u32[]{:S(2)}, u32[]{:S(2)}) %all-to-all-start.1) | async-done | bytes 307232 | tf_op jit(solution)/shard_map/all_to_all | solution.py:311
  510.0 129.6 %reduce-scatter.14.cloned.1.call-done = bf16[40,1280]{1,0:T(8,128)(2,1)} async-done(((bf16[1280,1280]{1,0:T(8,128)(2,1)}), bf16[40,1280]{1,0:T(8,128)(2,1)}) %reduce-scatter.14.cloned.1.call-update) | async-done | bytes 102416 | tf_op jit(solution)/shard_map/reduce_scatter | solution.py:907
  639.6 1.8 maximum_convert_fusion
  641.4 6.9 %all-gather.6.cloned.1.call-done = bf16[8,3,80,640]{3,2,1,0:T(8,128)(2,1)} async-done(((bf16[4,3,80,640]{3,2,1,0:T(8,128)(2,1)}), bf16[8,3,80,640]{3,2,1,0:T(8,128)(2,1)}) %all-gather.6.cloned.1.call-update) | async-done | bytes 2457616 | tf_op jit(solution)/shard_map/all_gather | solution.py:917
  648.3 1.4 convert_bitcast_fusion
  649.8 1.9 copy.136
  651.7 3.4 reshape.258
  (116 shorter events, 18.6 us)
Async XLA Ops:
  7.2 7.0 %slice-start = ((f32[40,5120]{1,0:T(8,128)}), f32[40,3840]{1,0:T(8,128)S(1)}, s32[]{:S(2)}) async-start(f32[40,5120]{1,0:T(8,128)} %param.9), calls=%async_computation.15 | async-start | bytes 1228800 | tf_op jit(solution)/shard_map/slice | solution.py:862
  7.2 122.1 %all-gather.4.cloned.1.call-start = ((), (), s32[]{:S(2)}) async-start(), calls=%async_computation.8 | async-start | bytes 3379200 | tf_op jit(solution)/shard_map/all_gather | solution.py:864
  124.1 3.4 copy-start.15
  124.1 4.0 copy-start.16
  129.3 180.5 %copy-start.2 = (bf16[5,512,64]{2,1,0:T(8,128)(2,1)S(1)}, bf16[5,512,64]{2,1,0:T(8,128)(2,1)}, u32[]{:S(2)}) copy-start(bf16[5,512,64]{2,1,0:T(8,128)(2,1)} %get-tuple-element.30) | copy-start | bytes 983044
  295.8 24.1 %all-to-all-start = ((bf16[4,128,320]{1,2,0:T(8,128)(2,1)}), bf16[4,128,320]{1,2,0:T(8,128)(2,1)S(1)}, u32[]{:S(2)}, u32[]{:S(2)}) async-start(bf16[4,128,320]{1,2,0:T(8,128)(2,1)} %copy.118), calls=%async_computation | async-start | bytes 655360 | tf_op jit(solution)/shard_map/all_to_all | solution.py:921
  309.8 42.7 %reduce-scatter.8.cloned.1.call-start = ((), (), s32[]{:S(2)}) async-start(), calls=%async_computation.9 | async-start | bytes 3932160 | tf_op jit(solution)/shard_map/reduce_scatter | solution.py:938
  320.4 0.7 copy-start.5
  321.6 1.8 copy-start.6
  321.6 1.8 copy-start.9
  323.4 7.3 %copy-start = (f32[5,512,1024]{2,1,0:T(8,128)S(1)}, f32[5,512,1024]{2,1,0:T(8,128)}, u32[]{:S(2)}) copy-start(f32[5,512,1024]{2,1,0:T(8,128)} %fusion.28) | copy-start | bytes 31457284
  323.4 7.3 %copy-start.8 = (bf16[1024,5,64]{0,2,1:T(8,128)(2,1)S(1)}, bf16[1024,5,64]{0,2,1:T(8,128)(2,1)}, u32[]{:S(2)}) copy-start(bf16[1024,5,64]{0,2,1:T(8,128)(2,1)} %reshape.239) | copy-start | bytes 1966084
  334.8 2.3 copy-start.1
  343.0 72.9 %reduce-scatter.16.cloned.1.call-start = ((), (), s32[]{:S(2)}) async-start(), calls=%async_computation.14 | async-start | bytes 6144000
  348.0 2.0 copy-start.3
  348.1 146.4 %reduce-scatter.12.cloned.1.call-start = ((), (), s32[]{:S(2)}) async-start(), calls=%async_computation.11 | async-start | bytes 2949120 | tf_op jit(solution)/shard_map/reduce_scatter | solution.py:307
  354.5 18.4 %copy-start.4 = (f32[2,5,512,64]{3,2,1,0:T(8,128)S(1)}, f32[2,5,512,64]{3,2,1,0:T(8,128)}, u32[]{:S(2)}) copy-start(f32[2,5,512,64]{3,2,1,0:T(8,128)} %get-tuple-element.28) | copy-start | bytes 3932164
  390.9 0.7 copy-start.13
  400.9 97.1 %reduce-scatter.10.cloned.1.call-start = ((), (), s32[]{:S(2)}) async-start(), calls=%async_computation.10 | async-start | bytes 1638400 | tf_op jit(solution)/shard_map/reduce_scatter | solution.py:842
  404.1 1.0 copy-start.11
  404.1 1.1 copy-start.12
  404.2 1.2 copy-start.14
  408.0 231.6 %reduce-scatter.14.cloned.1.call-start = ((), (), s32[]{:S(2)}) async-start(), calls=%async_computation.12 | async-start | bytes 3379200 | tf_op jit(solution)/shard_map/reduce_scatter | solution.py:907
  408.6 239.8 %all-gather.6.cloned.1.call-start = ((), (), s32[]{:S(2)}) async-start(), calls=%async_computation.13 | async-start | bytes 3686400 | tf_op jit(solution)/shard_map/all_gather | solution.py:917
  417.2 34.5 %copy-start.20 = (f32[2,1,640]{2,1,0:T(1,128)S(1)}, f32[2,1,640]{2,1,0:T(1,128)}, u32[]{:S(2)}) copy-start(f32[2,1,640]{2,1,0:T(1,128)} %get-tuple-element.40) | copy-start | bytes 15364
  417.2 34.6 %copy-start.19 = (f32[2,1,640]{2,1,0:T(1,128)S(1)}, f32[2,1,640]{2,1,0:T(1,128)}, u32[]{:S(2)}) copy-start(f32[2,1,640]{2,1,0:T(1,128)} %get-tuple-element.41) | copy-start | bytes 15364
  417.2 34.6 %copy-start.18 = (f32[1,1280]{1,0:T(1,128)S(1)}, f32[1,1280]{1,0:T(1,128)}, u32[]{:S(2)}) copy-start(f32[1,1280]{1,0:T(1,128)} %get-tuple-element.38) | copy-start | bytes 15364
  417.3 34.7 %copy-start.17 = (f32[1,1280]{1,0:T(1,128)S(1)}, f32[1,1280]{1,0:T(1,128)}, u32[]{:S(2)}) copy-start(f32[1,1280]{1,0:T(1,128)} %get-tuple-element.39) | copy-start | bytes 15364
  417.3 80.7 %copy-start.7 = (f32[128,1280]{1,0:T(8,128)S(1)}, f32[128,1280]{1,0:T(8,128)}, u32[]{:S(2)}) copy-start(f32[128,1280]{1,0:T(8,128)} %get-tuple-element.27) | copy-start | bytes 1966084
  494.5 14.7 %all-to-all-start.1 = ((bf16[4,40,960]{2,1,0:T(8,128)(2,1)}), bf16[4,40,960]{2,1,0:T(8,128)(2,1)S(1)}, u32[]{:S(2)}, u32[]{:S(2)}) async-start(bf16[4,40,960]{2,1,0:T(8,128)(2,1)} %bitcast.154), calls=%async_computation.4 | async-start | bytes 655360 | tf_op jit(solution)/shard_map/all_to_all | solution.py:311
  651.7 3.4 copy-start.10
Sparse Core Ops, SparseCore 0:
  11.4 85.0 all-gather.3
  343.1 9.3 reduce-scatter.7
  355.8 60.0 reduce-scatter.15
  419.4 44.0 reduce-scatter.11
  466.3 31.4 reduce-scatter.9
  500.0 139.5 reduce-scatter.13
  641.1 7.1 all-gather.5

commit v3 on v2

--- a/solution.py
+++ b/solution.py
@@ -268,52 +268,6 @@
 
 def fits(n_seq, chips):
     return n_seq == 4 and chips == 4 and HEADS % chips == 0
-
-
-def chip_groups(chips):
-    return [[CORES * chip + core for chip in range(chips)] for core in range(CORES)]
-
-
-def core_groups(chips):
-    return [[CORES * chip + core for core in range(CORES)] for chip in range(chips)]
-
-
-def copy_groups(n_seq, chips):
-    return [
-        [(seq * chips + chip) * CORES + core for seq in range(n_seq) for core in range(CORES)]
-        for chip in range(chips)
-    ]
-
-
-def spread_weights(weights_low, parts, n_seq, chips):
-    rows, columns = weights_low.shape
-    share = columns // parts // chips
-    by_chip = weights_low.reshape(rows, parts, chips, share).transpose(2, 0, 1, 3)
-    by_chip = by_chip.reshape(chips, rows, parts * share)
-    mine = lax.all_to_all(
-        by_chip, "ctx", split_axis=0, concat_axis=0, tiled=True,
-        axis_index_groups=chip_groups(chips),
-    )
-    full = lax.all_gather(mine, ALL, axis=0, axis_index_groups=copy_groups(n_seq, chips))
-    full = full.reshape(n_seq, CORES, chips, rows, parts * share).transpose(0, 2, 1, 3, 4)
-    return full.reshape(n_seq * CORES * chips * rows, parts * share)
-
-
-def collect_grads(partial, parts, n_seq, chips):
-    rows = partial.shape[0] // (n_seq * CORES * chips)
-    share = partial.shape[1] // parts
-    by_owner = partial.astype(jnp.bfloat16).reshape(n_seq, chips, CORES, rows, parts * share)
-    by_owner = by_owner.transpose(0, 2, 1, 3, 4).reshape(n_seq * CORES * chips * rows, parts * share)
-    mine = lax.psum_scatter(
-        by_owner, ALL, scatter_dimension=0, tiled=True,
-        axis_index_groups=copy_groups(n_seq, chips),
-    ).reshape(chips, rows, parts * share)
-    back = lax.all_to_all(
-        mine, "ctx", split_axis=0, concat_axis=0, tiled=True,
-        axis_index_groups=chip_groups(chips),
-    )
-    back = back.reshape(chips, rows, parts, share).transpose(1, 2, 0, 3)
-    return back.reshape(rows, parts * chips * share).astype(jnp.float32)
 
 
 MESH = pl.DeviceIdType.MESH
@@ -821,43 +775,301 @@
     )(attx, states, cotangent, w_out, alpha_attn, alpha_mlp, gain_u, gain_v, w_part)
 
 
+def back_kernel(
+    grad_attx, grad_half, grad_w_out, small_in, raw, query, both, att, inverse, states_all,
+    w_qkv, qk_gain, query_pos, key_pos, grad_direct,
+    grad_states, out_mlp, out_qkv, out_proj, small_out,
+    att_low, heads_low, to_keys, swap_low, swap_kv, grad_heads, grad_sides, part, sums, turned,
+    grad_q, half_q, seq_q, line_q, wide_q, half_o, pair_o, seq_got, seq_low, line_got, wide,
+    wide_o, small, small_pair, small_seq, dots,
+    local_sem, a_send, a_recv, s_send, s_recv, o_send, o_recv, kv_send, kv_recv, r_send, r_recv,
+    qt_send, qt_recv, qs_send, qs_recv, qz_send, qz_recv, z_send, z_recv, f_send, f_recv,
+    p_send, p_recv, t_send, t_recv,
+):
+    seq, chip, core = place_of()
+    tok_rows, model_width = grad_direct.shape
+    heads = qk_gain.shape[0]
+    head_cols = heads * HEAD_DIM
+    group_rows = CHIPS * tok_rows
+    half_units = grad_half.shape[2]
+    seq_rows = seq_got.shape[2]
+    chip_rows = seq_rows // CHIPS
+    rows = chip_rows // CORES
+    part_cols = head_cols // CORES
+    ff_width = out_mlp.shape[1] // 3
+    scale = math.sqrt(HEAD_DIM)
+    block = rows_at(chip, tok_rows)
+    f32, low = jnp.float32, jnp.bfloat16
+    meet()
+    waits = []
+    line = []
+    for step in STEPS:
+        device, other = chip_peer(step)
+        line.append(begin(remote(grad_attx.at[other], att_low.at[block], a_send.at[step], a_recv.at[step], device)))
+    att_low[block, :] = grad_attx[chip]
+    half_at = pl.ds(pl.multiple_of(core * half_units, 128), half_units)
+    other_at = pl.ds(pl.multiple_of((1 - core) * half_units, 128), half_units)
+    pair = begin(remote(grad_w_out.at[:, :, other_at], pair_o, o_send.at[0], o_recv.at[0], twin()))
+    across = []
+    for which in range(3):
+        for step in STEPS:
+            device, other = seq_peer(step)
+            across.append(begin(remote(grad_half.at[which, rows_at(other, seq_rows)], seq_got.at[which, step - 1], s_send.at[which, step], s_recv.at[which, step], device)))
+    keeps = [
+        begin(pltpu.make_async_copy(grad_half.at[which, rows_at(seq, seq_rows)], seq_low.at[which], local_sem.at[which]))
+        for which in range(3)
+    ]
+    to_keys[...] = jnp.zeros_like(to_keys)
+    dots[...] = jnp.zeros_like(dots)
+    turned[...] = states_all[...].T
+    pair.wait_recv()
+    for at in range(4):
+        half_o[at] = (grad_w_out[at, :, half_at].astype(f32) + pair_o[at].astype(f32)).astype(low)
+    for step in STEPS:
+        device, other = seq_peer(step)
+        across.append(begin(remote(half_o.at[other], seq_got.at[3, step - 1], s_send.at[3, step], s_recv.at[3, step], device)))
+    for copy in line:
+        copy.wait_recv()
+    for head in range(heads):
+        heads_low[head] = att_low[:, head * HEAD_DIM : (head + 1) * HEAD_DIM]
+
+    tile = min(128, group_rows)
+    tiles = group_rows // tile
+
+    def raw_back(which, head, at, upstream):
+        value = raw[which, head, at, :]
+        unit, factor = unit_of(value)
+        dots[head] += jnp.sum(upstream * unit, axis=0, keepdims=True)
+        upstream = upstream * qk_gain[head]
+        upstream = factor * (upstream - unit * jnp.sum(upstream * unit, axis=-1, keepdims=True))
+        grad_heads[which, head, at, :] = upstream.astype(low)
+
+    def one_tile(index, carry):
+        head = index // tiles
+        at = rows_at(lax.rem(index, tiles), tile)
+        rows_q = query[head, at, :]
+        grad_att = heads_low[head, at, :]
+        allowed = key_pos[...] <= query_pos[at, :]
+        scores = jnp.concatenate([dot_nt(rows_q, both[half, 0, head]) for half in range(CORES)], axis=1)
+        probs = jnp.exp(jnp.where(allowed, scores, NEG_LARGE)) * inverse[head, at, :]
+        grad_prob = jnp.concatenate([dot_nt(grad_att, both[half, 1, head]) for half in range(CORES)], axis=1)
+        row_dot = jnp.sum(grad_att.astype(f32) * att[head, at, :], axis=-1, keepdims=True)
+        grad_scores = (probs * (grad_prob - row_dot)).astype(low)
+        weights = probs.astype(low)
+        total = jnp.zeros((tile, HEAD_DIM), f32)
+        for half in range(CORES):
+            cols = slice(half * group_rows, (half + 1) * group_rows)
+            total = total + dot(grad_scores[:, cols], both[half, 0, head])
+            to_keys[half, 0, head] += dot_tn(grad_scores[:, cols], rows_q)
+            to_keys[half, 1, head] += dot_tn(weights[:, cols], grad_att)
+        raw_back(0, head, at, total * scale)
+        return carry
+
+    lax.fori_loop(0, heads * tiles, one_tile, 0)
+    swap_low[...] = to_keys[1 - core].astype(low)
+    swap = begin(remote(swap_low, swap_kv, kv_send.at[0], kv_recv.at[0], twin()))
+    swap.wait()
+
+    def one_key(index, carry):
+        head = index // tiles
+        at = rows_at(lax.rem(index, tiles), tile)
+        mine = to_keys[core, 0, head, at, :] + swap_kv[0, head, at, :].astype(f32)
+        raw_back(1, head, at, mine)
+        value = to_keys[core, 1, head, at, :] + swap_kv[1, head, at, :].astype(f32)
+        grad_heads[2, head, at, :] = value.astype(low)
+        return carry
+
+    lax.fori_loop(0, heads * tiles, one_key, 0)
+    for which in range(3):
+        full = jnp.concatenate([grad_heads[which, head] for head in range(heads)], axis=1)
+        for half in range(CORES):
+            grad_sides[half, :, which * part_cols : (which + 1) * part_cols] = full[:, half * part_cols : (half + 1) * part_cols]
+    wide_tile = model_width // 5
+
+    def down(index, carry):
+        at = rows_at(index, wide_tile)
+        part[:, at] = sum(dot_nt(grad_sides[half], w_qkv[half, at, :]) for half in range(CORES)).astype(low)
+        return carry
+
+    lax.fori_loop(0, 5, down, 0)
+    reduce = []
+    for step in STEPS:
+        device, other = chip_peer(step)
+        reduce.append(begin(remote(part.at[rows_at(other, tok_rows)], sums.at[step - 1], r_send.at[step], r_recv.at[step], device)))
+
+    def weight_grad(index, carry):
+        half = index // 5
+        at = rows_at(lax.rem(index, 5), wide_tile)
+        grad_q[half, at, :] = dot(turned[at, :], grad_sides[half]).astype(low)
+        return carry
+
+    lax.fori_loop(0, CORES * 5, weight_grad, 0)
+    swap_q = begin(remote(grad_q.at[1 - core], half_q, qt_send.at[0], qt_recv.at[0], twin()))
+    small[...] = small_in[...]
+    small[4:5, :head_cols] = jnp.concatenate([dots[head] for head in range(heads)], axis=1)
+    swap_s = begin(remote(small, small_pair, t_send.at[0], t_recv.at[0], twin()))
+    swap_q.wait()
+    half_q[...] = (grad_q[core].astype(f32) + half_q[...].astype(f32)).astype(low)
+    across_q = []
+    for step in STEPS:
+        device, other = seq_peer(step)
+        across_q.append(begin(remote(half_q.at[rows_at(other, seq_rows)], seq_q.at[step - 1], qs_send.at[step], qs_recv.at[step], device)))
+    swap_s.wait()
+    small[...] = small[...] + small_pair[...]
+    spread_s = [
+        begin(remote(small, small_seq.at[step - 1], t_send.at[step], t_recv.at[step], seq_peer(step)[0]))
+        for step in STEPS
+    ]
+    for copy in keeps:
+        copy.wait()
+    seq_low[3] = half_o[seq]
+    onward = []
+    for which in range(4):
+        for copy in across[3 * which : 3 * which + 3]:
+            copy.wait_recv()
+        total = seq_low[which].astype(f32)
+        for step in STEPS:
+            total = total + seq_got[which, step - 1].astype(f32)
+        seq_low[which] = total.astype(low)
+        for step in STEPS:
+            device, other = chip_peer(step)
+            onward.append(begin(remote(seq_low.at[which, rows_at(other, chip_rows)], line_got.at[which, chip], z_send.at[which, step], z_recv.at[which, step], device)))
+        line_got[which, chip] = seq_low[which, rows_at(chip, chip_rows), :]
+    for copy in across_q:
+        copy.wait_recv()
+    total = half_q[rows_at(seq, seq_rows), :].astype(f32)
+    for step in STEPS:
+        total = total + seq_q[step - 1].astype(f32)
+    grad_q[0, :seq_rows, :] = total.astype(low)
+    onward_q = []
+    for step in STEPS:
+        device, other = chip_peer(step)
+        onward_q.append(begin(remote(grad_q.at[0, rows_at(other, chip_rows)], line_q.at[chip], qz_send.at[step], qz_recv.at[step], device)))
+    line_q[chip] = grad_q[0, rows_at(chip, chip_rows), :]
+    for copy in spread_s:
+        copy.wait()
+    small_pair[...] = small[...] + small_seq[0] + small_seq[1] + small_seq[2]
+    small_out[chip] = small_pair[...]
+    ends = gather_line(small_pair, small_out.at[chip], p_send, p_recv)
+    for copy in reduce:
+        copy.wait_recv()
+    total = part[block, :].astype(f32) + grad_direct[...]
+    for step in STEPS:
+        total = total + sums[step - 1].astype(f32)
+    grad_states[...] = total.astype(low)
+
+    mine = rows_at(core, rows)
+    theirs = rows_at(1 - core, rows)
+    last, lasts = [], []
+    for which in range(3):
+        for copy in onward[3 * which : 3 * which + 3]:
+            copy.wait_recv()
+        for at in range(CHIPS):
+            wide[which, at] = line_got[which, at].astype(f32)
+            start = which * ff_width + at * CORES * half_units + core * half_units
+            there = out_mlp.at[:, pl.ds(pl.multiple_of(start, 128), half_units)]
+            last.append(begin(remote(wide.at[which, at, theirs], there, f_send.at[which, at], f_recv.at[which, at], twin())))
+            lasts.append(begin(pltpu.make_async_copy(wide.at[which, at, mine], there, local_sem.at[3 + which * CHIPS + at])))
+    for copy in onward[9:]:
+        copy.wait_recv()
+    total = line_got[3, 0].astype(f32)
+    for at in range(1, CHIPS):
+        total = total + line_got[3, at].astype(f32)
+    wide_o[...] = total
+    there = out_proj.at[:, half_at]
+    last.append(begin(remote(wide_o.at[theirs], there, f_send.at[3, 0], f_recv.at[3, 0], twin())))
+    lasts.append(begin(pltpu.make_async_copy(wide_o.at[mine], there, local_sem.at[15])))
+    for copy in onward_q:
+        copy.wait_recv()
+    wide_q[...] = line_q[...].astype(f32)
+    there = out_qkv.at[core]
+    last.append(begin(remote(wide_q.at[:, theirs], there, f_send.at[3, 1], f_recv.at[3, 1], twin())))
+    lasts.append(begin(pltpu.make_async_copy(wide_q.at[:, mine], there, local_sem.at[16])))
+    for copy in ends + last + lasts:
+        copy.wait()
+    for copy in line + [pair] + across + reduce + across_q + onward + onward_q:
+        copy.wait_send()
+
+
+def back_call(
+    grad_attx, grad_half, grad_w_out, small_in, raw, query, both, att, inverse, states_all,
+    w_qkv, qk_gain, query_pos, key_pos, grad_direct, rows,
+):
+    tok_rows, model_width = grad_direct.shape
+    chips = grad_attx.shape[0]
+    heads = qk_gain.shape[0]
+    head_cols = heads * HEAD_DIM
+    group_rows = chips * tok_rows
+    half_units = grad_half.shape[2]
+    half_cols = w_qkv.shape[2]
+    chip_rows = CORES * rows
+    seq_rows = chips * chip_rows
+    f32, low = jnp.float32, jnp.bfloat16
+    shape = jax.ShapeDtypeStruct
+    per_head = (heads, group_rows, HEAD_DIM)
+    return pl.pallas_call(
+        back_kernel,
+        out_shape=[
+            shape((tok_rows, model_width), low),
+            shape((rows, 3 * chips * CORES * half_units), f32),
+            shape((CORES, chips, rows, half_cols), f32),
+            shape((rows, CORES * half_units), f32),
+            shape((chips,) + small_in.shape, f32),
+        ],
+        in_specs=[in_vmem(), in_hbm()] + [in_vmem()] * 13,
+        out_specs=[in_vmem(), in_hbm(), in_hbm(), in_hbm(), in_vmem()],
+        scratch_shapes=[
+            VMEM((group_rows, head_cols), low),
+            VMEM(per_head, low),
+            VMEM((CORES, 2) + per_head, f32),
+            VMEM((2,) + per_head, low),
+            VMEM((2,) + per_head, low),
+            VMEM((3,) + per_head, low),
+            VMEM((CORES, group_rows, half_cols), low),
+            VMEM((group_rows, model_width), low),
+            VMEM((3, tok_rows, model_width), low),
+            VMEM((model_width, group_rows), low),
+            VMEM((CORES, model_width, half_cols), low),
+            VMEM((model_width, half_cols), low),
+            VMEM((3, seq_rows, half_cols), low),
+            VMEM((chips, chip_rows, half_cols), low),
+            VMEM((chips, chip_rows, half_cols), f32),
+            VMEM((4, seq_rows, half_units), low),
+            VMEM((4, seq_rows, half_units), low),
+            VMEM((4, 3, seq_rows, half_units), low),
+            VMEM((4, seq_rows, half_units), low),
+            VMEM((4, chips, chip_rows, half_units), low),
+            VMEM((3, chips, chip_rows, half_units), f32),
+            VMEM((chip_rows, half_units), f32),
+            VMEM(small_in.shape, f32),
+            VMEM(small_in.shape, f32),
+            VMEM((3,) + small_in.shape, f32),
+            VMEM((heads, 1, HEAD_DIM), f32),
+            dma(17), dma(4), dma(4), dma(4, 4), dma(4, 4), dma(1), dma(1), dma(1), dma(1),
+            dma(4), dma(4), dma(1), dma(1), dma(4), dma(4), dma(4), dma(4), dma(4, 4), dma(4, 4),
+            dma(4, 4), dma(4, 4), dma(4), dma(4), dma(4), dma(4),
+        ],
+        compiler_params=pltpu.CompilerParams(
+            collective_id=3, has_side_effects=True, vmem_limit_bytes=LIMIT
+        ),
+        name="back",
+    )(
+        grad_attx, grad_half, grad_w_out, small_in, raw, query, both, att, inverse, states_all,
+        w_qkv, qk_gain, query_pos, key_pos, grad_direct,
+    )
+
+
 def shards_split(states, cotangent, attn_weights, mlp_weights, feature_gains, unit_gains, block_place):
     tok_rows, model_width = states.shape
     ff_width = unit_gains.shape[0]
     n_seq, n_ctx = lax.axis_size("seq"), lax.axis_size("ctx")
     chips = n_ctx // CORES
-    score_scale = math.sqrt(HEAD_DIM)
     chip = lax.axis_index("ctx") // CORES
     core = lax.axis_index("ctx") % CORES
     heads = HEADS // chips
     head_cols = heads * HEAD_DIM
     units = ff_width // chips
     group_rows = chips * tok_rows
-    chip_grp, core_grp = chip_groups(chips), core_groups(chips)
-
-    def gather_chips(own):
-        return lax.all_gather(own, "ctx", axis=0, tiled=True, axis_index_groups=chip_grp)
-
-    def sum_chips(partial):
-        return lax.psum_scatter(
-            partial.astype(jnp.bfloat16), "ctx", scatter_dimension=0, tiled=True,
-            axis_index_groups=chip_grp,
-        ).astype(jnp.float32)
-
-    def to_tokens(by_heads):
-        moved = lax.all_to_all(
-            by_heads.reshape(chips, tok_rows, head_cols), "ctx", split_axis=0, concat_axis=0,
-            tiled=True, axis_index_groups=chip_grp,
-        )
-        return moved.transpose(1, 0, 2).reshape(tok_rows, model_width)
-
-    def to_heads(by_tokens):
-        moved = lax.all_to_all(
-            by_tokens.reshape(tok_rows, chips, head_cols).transpose(1, 0, 2), "ctx",
-            split_axis=0, concat_axis=0, tiled=True, axis_index_groups=chip_grp,
-        )
-        return moved.reshape(group_rows, head_cols)
-
     rows = attn_weights.shape[0]
     qkv_src = attn_weights[:, : 3 * model_width].reshape(rows, 3, chips, CORES, head_cols // CORES)
     qkv_src = qkv_src.transpose(2, 3, 0, 1, 4).reshape(chips, CORES, rows, -1)
@@ -865,112 +1077,52 @@
         attn_weights[:, 3 * model_width :].astype(jnp.bfloat16), ALL, axis=0, tiled=True
     )
     qk_gain = lax.dynamic_slice_in_dim(feature_gains[:, 0], chip * head_cols, head_cols)
-    qk_gain = qk_gain.reshape(heads, HEAD_DIM)
+    qk_gain = qk_gain.reshape(heads, 1, HEAD_DIM)
     places = block_place[0].reshape(chips, CORES)
     offsets = jnp.arange(tok_rows, dtype=jnp.int32)
     own_places = jnp.sum(
         jnp.where(jnp.arange(CORES, dtype=jnp.int32)[None, :] == core, places, 0), axis=1
     )
-    query_pos = (own_places[:, None] * tok_rows + offsets).reshape(group_rows)
-    key_pos = (places.T[:, :, None] * tok_rows + offsets).reshape(CORES * group_rows)
-    head_shape = (group_rows, heads, HEAD_DIM)
-    states_all, w_halves, w_part, raw, query_h, both_h, att_h, inverse, attx = attend_call(
-        states, qkv_src, mlp_weights, qk_gain.reshape(heads, 1, HEAD_DIM),
-        query_pos.reshape(group_rows, 1), key_pos.reshape(1, CORES * group_rows),
-    )
-    w_qkv = w_halves.reshape(CORES, model_width, 3, head_cols // CORES).transpose(1, 2, 0, 3)
-    w_qkv = w_qkv.reshape(model_width, 3 * head_cols)
-    attended_own = attx.transpose(1, 0, 2).reshape(tok_rows, model_width)
-    attended = att_h.transpose(1, 0, 2)
-    query_low = query_h.transpose(1, 0, 2) / 8
-    key_all = both_h[:, 0].transpose(0, 2, 1, 3).reshape(CORES * group_rows, heads, HEAD_DIM)
-    value_all = both_h[:, 1].transpose(0, 2, 1, 3).reshape(CORES * group_rows, heads, HEAD_DIM)
-    query_unit, query_factor = unit_rows(raw[0].transpose(1, 0, 2))
-    key_unit, key_factor = unit_rows(raw[1].transpose(1, 0, 2))
-    allowed = (key_pos[None, :] <= query_pos[:, None])[None]
-    scores = score_scale * jnp.einsum(
-        "qhd,khd->hqk", query_low, key_all, preferred_element_type=jnp.float32
-    )
-    probabilities = jnp.where(allowed, jnp.exp(scores) * inverse, 0.0)
-    weights_low = probabilities.astype(jnp.bfloat16)
-    w_out_parts = w_out.reshape(chips, head_cols, model_width)
+    query_pos = (own_places[:, None] * tok_rows + offsets).reshape(group_rows, 1)
+    key_pos = (places.T[:, :, None] * tok_rows + offsets).reshape(1, CORES * group_rows)
+    states_all, w_qkv, w_part, raw, query, both, att, inverse, attx = attend_call(
+        states, qkv_src, mlp_weights, qk_gain, query_pos, key_pos
+    )
     gain_u = lax.dynamic_slice_in_dim(unit_gains[:, 0], chip * units, units)
     gain_v = lax.dynamic_slice_in_dim(unit_gains[:, 1], chip * units, units) * math.sqrt(D)
     (
         out_low, grad_attx, grad_w_out, grad_direct, grad_alpha_a, grad_alpha_m, grad_s_u, grad_s_v, grad_half
     ) = mlp_call(
-        attx, states, cotangent, w_out_parts, feature_gains[:, 1].reshape(1, model_width),
-        feature_gains[:, 2].reshape(1, model_width), gain_u.reshape(CORES, 1, units // CORES),
-        gain_v.reshape(CORES, 1, units // CORES), w_part,
-    )
-    grad_s_v = grad_s_v * math.sqrt(D)
-    grad_out_proj = lax.psum_scatter(
-        grad_w_out.reshape(model_width, model_width), ALL, scatter_dimension=0, tiled=True
-    ).astype(jnp.float32)
-    halves = lax.psum_scatter(
-        grad_half.reshape(3, n_seq, -1, units // CORES), "seq", scatter_dimension=1, tiled=True
-    )
-    halves = halves.reshape(3, chips, -1, units // CORES).transpose(1, 0, 2, 3)
-    moved = lax.all_to_all(
-        halves, "ctx", split_axis=0, concat_axis=0, tiled=True, axis_index_groups=chip_grp
-    )
-    moved = lax.all_gather(moved, "ctx", axis=0, axis_index_groups=core_grp)
-    moved = moved.reshape(CORES, chips, 3, CORES, rows, units // CORES)
-    moved = lax.dynamic_index_in_dim(moved, core, 3, keepdims=False)
-    grad_mlp = moved.transpose(3, 2, 1, 0, 4).reshape(rows, 3 * ff_width).astype(jnp.float32)
-    grad_attended = lax.all_to_all(
-        grad_attx, "ctx", split_axis=0, concat_axis=0, tiled=True, axis_index_groups=chip_grp
-    ).reshape(head_shape)
-    row_dots = jnp.einsum("qhd,qhd->hq", grad_attended.astype(jnp.float32), attended)
-    grad_prob = jnp.einsum(
-        "qhd,khd->hqk", grad_attended, value_all, preferred_element_type=jnp.float32
-    )
-    grad_scores = (probabilities * (grad_prob - row_dots[..., None])).astype(jnp.bfloat16)
-    grad_query_low = score_scale * jnp.einsum(
-        "hqk,khd->qhd", grad_scores, key_all, preferred_element_type=jnp.float32
-    )
-    key_terms = score_scale * jnp.einsum(
-        "hqk,qhd->khd", grad_scores, query_low, preferred_element_type=jnp.float32
-    )
-    value_terms = jnp.einsum(
-        "hqk,qhd->khd", weights_low, grad_attended, preferred_element_type=jnp.float32
-    )
-    summed = lax.psum_scatter(
-        jnp.stack([key_terms, value_terms]).astype(jnp.bfloat16), "ctx", scatter_dimension=1,
-        tiled=True, axis_index_groups=core_grp,
-    ).astype(jnp.float32)
-    grad_key_low, grad_value = summed[0], summed[1]
-    grad_s_qk = jnp.sum(grad_query_low * query_unit + grad_key_low * key_unit, axis=0)
-    grad_query_raw = unit_back(query_unit, query_factor, grad_query_low * qk_gain)
-    grad_key_raw = unit_back(key_unit, key_factor, grad_key_low * qk_gain)
-    grad_projected = jnp.concatenate(
-        [part.reshape(group_rows, head_cols) for part in (grad_query_raw, grad_key_raw, grad_value)],
+        attx, states, cotangent, w_out.reshape(chips, head_cols, model_width),
+        feature_gains[:, 1].reshape(1, model_width), feature_gains[:, 2].reshape(1, model_width),
+        gain_u.reshape(CORES, 1, units // CORES), gain_v.reshape(CORES, 1, units // CORES), w_part,
+    )
+    small = jnp.concatenate(
+        [
+            grad_alpha_a, grad_alpha_m, grad_s_u.reshape(1, units),
+            grad_s_v.reshape(1, units) * math.sqrt(D), jnp.zeros((4, units), jnp.float32),
+        ]
+    )
+    grad_states, grad_mlp, grad_qkv, grad_proj, small = back_call(
+        grad_attx, grad_half, grad_w_out, small, raw, query, both, att, inverse, states_all,
+        w_qkv, qk_gain, query_pos, key_pos, grad_direct, rows,
+    )
+    grad_qkv = grad_qkv.reshape(CORES, chips, rows, 3, head_cols // CORES)
+    grad_qkv = grad_qkv.transpose(2, 3, 1, 0, 4).reshape(rows, 3 * model_width)
+    feature = jnp.stack(
+        [small[:, 4, :head_cols].reshape(-1), jnp.sum(small[:, 0], axis=0), jnp.sum(small[:, 1], axis=0)],
         axis=1,
-    ).astype(jnp.bfloat16)
-    grad_states = grad_direct + sum_chips(
-        contract_cols(grad_projected, w_qkv)
-    )
-    grad_qkv = collect_grads(contract_rows(states_all, grad_projected), 3, n_seq, chips)
-    slot = lambda own, width: lax.dynamic_update_slice_in_dim(
-        jnp.zeros((chips * width,), jnp.float32), own.reshape(width), chip * width, 0
-    )
-    small = jnp.concatenate(
-        [slot(grad_s_qk, head_cols), grad_alpha_a.reshape(-1), grad_alpha_m.reshape(-1), slot(grad_s_u, units), slot(grad_s_v, units)]
-    )
-    small = lax.psum(small, ALL)
+    )
+    unit = jnp.stack([small[:, 2].reshape(-1), small[:, 3].reshape(-1)], axis=1)
     rank = lax.axis_index(ALL)
-    feature = small[: 3 * model_width].reshape(3, model_width).T
-    unit = small[3 * model_width :].reshape(2, ff_width).T
-    devices = n_seq * n_ctx
-    grad_feature = lax.dynamic_slice_in_dim(feature, rank * (model_width // devices), model_width // devices)
-    grad_unit = lax.dynamic_slice_in_dim(unit, rank * (ff_width // devices), ff_width // devices)
+    unit_rows_own = ff_width // (n_seq * n_ctx)
     return (
         out_low,
-        grad_states.astype(jnp.bfloat16),
-        jnp.concatenate([grad_qkv, grad_out_proj], axis=1),
+        grad_states,
+        jnp.concatenate([grad_qkv, grad_proj], axis=1),
         grad_mlp,
-        grad_feature,
-        grad_unit,
+        lax.dynamic_slice_in_dim(feature, rank * rows, rows),
+        lax.dynamic_slice_in_dim(unit, rank * unit_rows_own, unit_rows_own),
     )
 
 

time: 670 us -> 434 us (0.65)
  waiting for transfers between devices: 160 us -> 0.02 us
  Pallas kernels: 266 us -> 393 us
  blocking collectives: 74.6 us -> 0 us
  other arithmetic: 45.1 us -> 7.03 us
  local copies, waits for them, and re-layouts: 54.9 us -> 19.2 us
  matrix products: 29.4 us -> 0 us
  starting transfers between devices: 17.8 us -> 0.04 us
    reduce_scatter x4 -> x0, waiting for transfers between devices: 131 us -> none  [the longest x1 130 us: shards_split(): lax.psum_scatter(grad_w_out.reshape(model_width, model_width), ALL, scatt...]
    pallas_call x0 -> x1, Pallas kernels: none -> 129 us  [back_call(): pl.pallas_call(back_kernel, out_shape=[shape((tok_rows, model_width), low...]
    psum x1 -> x0, blocking collectives: 40.1 us -> none  [shards_split(): small = lax.psum(small, ALL)]
    all_to_all x1 -> x0, blocking collectives: 34.4 us -> none  [shards_split(): lax.all_to_all(halves, 'ctx', split_axis=0, concat_axis=0, tiled=True, ax...]
    dot_general x7 -> x0, matrix products: 29.4 us -> none  [the longest x1 6.37 us: shards_split(): jnp.einsum('hqk,qhd->khd', weights_low, grad_attended, preferred_element_...]
    mul x5 -> x2, other arithmetic: 29.6 us -> 0.7 us  [the longest x1 0.7 us: shards_split(): grad_s_v.reshape(1, units) * math.sqrt(D)]
    all_to_all x2 -> x0, starting transfers between devices: 17.4 us -> none  [the longest x1 14 us: shards_split(): lax.all_to_all(grad_attx, 'ctx', split_axis=0, concat_axis=0, tiled=True,...]
    all_to_all x2 -> x0, waiting for transfers between devices: 14.2 us -> none  [the longest x1 9.48 us: collect_grads(): lax.all_to_all(mine, 'ctx', split_axis=0, concat_axis=0, tiled=True, axis...]
  transfers between devices with their start and end apart: 9 -> 1, of which waited for: 6 -> 0; matrix products, arithmetic and copies ran while one was open for 14% -> 3% of each run, Pallas kernels for 15% -> 23%
where the time goes in v3:
time: 434 us
  Pallas kernels  393 us (91%)
  local copies, waits for them, and re-layouts  19.2 us (4%)
  between operations  14.2 us (3%)
  other arithmetic  7.03 us (2%)
    pallas_call x1, Pallas kernels, mlp_call(): pl.pallas_call(mlp_kernel, out_shape=[shape(tokens, low), shape(attx.shap...  163 us
    pallas_call x1, Pallas kernels, back_call(): pl.pallas_call(back_kernel, out_shape=[shape((tok_rows, model_width), low...  129 us
    pallas_call x1, Pallas kernels, attend_call(): pl.pallas_call(attend_kernel, out_shape=[shape((group_rows, model_width),...  101 us
  transfers between devices with their start and end apart: 1, of which 0 were waited for; matrix products, arithmetic and copies ran while one was open for 3% of the time, Pallas kernels for 23%

profile of v3, /device:TPU:0, one launch (start us, length us, event | category | flops | bytes accessed | tf_op | source)
XLA Modules:
  0.0 433.5 jit_solution(4772754859821046881)
XLA Ops:
  7.2 0.0 all-gather.2.cloned.1.call-start
  7.2 1.6 slice.56
  8.8 0.0 all-gather.2.cloned.1.call-update
  8.8 1.1 slice.37
  10.0 0.5 broadcast.70
  10.5 1.3 reduce.9
  11.8 0.1 reshape_squeeze.9
  11.9 0.1 multiply_bitcast_fusion
  12.0 0.1 iota_add_fusion.1
  12.1 0.9 copy.22.query_pos
  13.0 1.4 slice_bitcast_fusion
  14.4 0.1 fusion.3
  14.5 0.6 reshape.132.qk_gain
  15.1 0.1 copy.21
  15.2 1.5 reshape.130
  16.7 0.5 copy.26
  17.2 0.0 copy-start.4
  17.2 1.6 reshape.131.qkv_src
  18.8 0.7 iota_add_fusion
  19.5 101.0 %attend.1 = (bf16[512,1280]{1,0:T(8,128)(2,1)}, bf16[2,1280,480]{2,1,0:T(8,128)(2,1)}, bf16[3,320,640]{2,1,0:T(8,128)(2,1)}, f32[2,5,512,64]{3,2,1,0:T(8,128)}, ...) custom-call(bf16[128,1280]{1,0:T(8,128)(2,1)} %states.3, ...), custom_call_target="tpu_custom_call" | custom-call | tf_op jit(solution)/shard_map/attend/pallas_call | solution.py:502
  120.5 0.0 copy-done.4
  120.5 0.6 dynamic-slice_multiply_fusion
  121.1 0.0 all-gather.2.cloned.1.call-done
  121.2 163.2 %mlp.1 = (bf16[128,1280]{1,0:T(8,128)(2,1)}, bf16[4,128,320]{2,1,0:T(8,128)(2,1)}, bf16[4,320,1280]{2,1,0:T(8,128)(2,1)}, f32[128,1280]{1,0:T(8,128)}, f32[1,128...) custom-call(bf16[4,128,320]{2,1,0:T(8,128)(2,1)} %get-tuple-element., ...), custom_call_target="tpu_custom_call" | custom-call | tf_op jit(solution)/shard_map/mlp/pallas_call | solution.py:733
  284.3 0.7 broadcast_multiply_fusion
  285.0 1.4 concatenate.6.small_in
  286.4 128.9 %back.1 = (bf16[128,1280]{1,0:T(8,128)(2,1)}, f32[40,15360]{1,0:T(8,128)}, f32[2,4,40,480]{3,2,1,0:T(8,128)}, f32[40,1280]{1,0:T(8,128)}, f32[4,8,1280]{2,1,0:T(8,128)}) custom-call(bf16[4,128,320]{2,1,0:T(8,128)(2,1)} %get-tuple-element.32.grad_attx, bf16[3,1280,640]{2,1,0:T(8,128)(2,1)} %get-tuple-element.33.grad_half, ...), custom_call_target="tpu_custom_call" | custom-call | tf_op jit(solution)/shard_map/back/pallas_call | solution.py:1010
  415.3 1.3 fusion.4
  416.6 0.8 slice_reduce_fusion.2
  417.5 0.1 stack_reshape_squeeze.9
  417.5 0.0 copy-start.3
  417.5 1.9 reshape.136
  419.5 0.0 copy-start.1
  419.5 0.8 copy.24
  420.3 0.0 copy-start.2
  420.3 1.3 reshape.137
  421.5 0.0 copy-start
  421.5 0.0 copy-done.3
  421.5 0.9 pad_maximum_fusion
  422.5 0.7 fusion
  423.1 0.7 fusion.2
  423.8 0.0 copy-done.1
  423.8 0.7 copy.30
  424.5 0.0 copy-done.2
  424.5 0.7 copy.31
  425.2 0.0 copy-done
  425.2 1.4 copy.32
  (6 shorter events, 0.1 us)
Async XLA Ops:
  7.2 114.0 %all-gather.2.cloned.1.call-start = ((), (), s32[]{:S(2)}) async-start(), calls=%async_computation | async-start | bytes 3379200 | tf_op jit(solution)/shard_map/all_gather | solution.py:1076
  17.2 103.3 %copy-start.4 = (f32[5120,2]{0,1:T(2,128)S(1)}, f32[5120,2]{0,1:T(2,128)}, u32[]{:S(2)}) copy-start(f32[5120,2]{0,1:T(2,128)} %param.12) | copy-start | bytes 122884
  417.5 4.0 copy-start.3
  419.5 4.3 copy-start.1
  420.3 4.3 copy-start.2
  421.5 3.7 copy-start
Sparse Core Ops, SparseCore 0:
  11.4 82.3 all-gather.1

commit v4 on v3

--- a/solution.py
+++ b/solution.py
@@ -324,9 +324,133 @@
     return pl.ds(pl.multiple_of(index * count, count), count)
 
 
-def gather_line(src, dst_of, send, recv):
+def device_on(chip):
+    seq, _, core = place_of()
+    return (seq, chip * CORES + core)
+
+
+def when(condition, action):
+    pl.when(condition)(action)
+
+
+PIECES = 2
+
+
+def piece_at(block, piece, count):
+    step = count // PIECES
+    return pl.ds(pl.multiple_of(block * count + piece * step, step), step)
+
+
+def gather_copy(src, everything, count, block, side, hop, piece, send, recv):
+    chip = place_of()[1]
+    there = everything.at[piece_at(block, piece, count)]
+    near = chip + 1 if side == 0 else chip - 1
+    here = there if src is None else src.at[piece_at(0, piece, count)]
+    return remote(here, there, send.at[side, hop, piece], recv.at[side, hop, piece], device_on(near))
+
+
+def gather_start(src, everything, count, send, recv):
+    chip = place_of()[1]
+    for piece in range(PIECES):
+        for side in range(2):
+            copy = gather_copy(src, everything, count, chip, side, 0, piece, send, recv)
+            when(chip < CHIPS - 1 if side == 0 else chip > 0, copy.start)
+
+
+def gather_hop(everything, count, hop, send, recv):
+    chip = place_of()[1]
+    for piece in range(PIECES):
+        for side in range(2):
+            block = chip - hop if side == 0 else chip + hop
+
+            def pass_on(side=side, piece=piece, block=block):
+                gather_copy(None, everything, count, block, side, hop - 1, piece, send, recv).wait_recv()
+                if hop < CHIPS - 1:
+                    copy = gather_copy(None, everything, count, block, side, hop, piece, send, recv)
+                    when(chip < CHIPS - 1 if side == 0 else chip > 0, copy.start)
+
+            when(block >= 0 if side == 0 else block < CHIPS, pass_on)
+
+
+def gather_drain(everything, count, send, recv):
+    chip = place_of()[1]
+    for hop in range(CHIPS - 1):
+        for piece in range(PIECES):
+            for side in range(2):
+                copy = gather_copy(None, everything, count, chip, side, hop, piece, send, recv)
+                block = chip - hop if side == 0 else chip + hop
+                sent = (block >= 0) & (chip < CHIPS - 1) if side == 0 else (block < CHIPS) & (chip > 0)
+                when(sent, copy.wait_send)
+
+
+def inside_line():
+    chip = place_of()[1]
+    return (chip > 0) & (chip < CHIPS - 1)
+
+
+def spans_line(other):
+    return abs(place_of()[1] - other) == CHIPS - 1
+
+
+def reduce_start(part, count, sums, via, send, recv):
+    chip = place_of()[1]
+    near = jnp.where(chip == 0, 1, CHIPS - 2)
+    first = remote(part.at[rows_at(CHIPS - 1 - chip, count)], via, send.at[0], recv.at[0], device_on(near))
+
+    def ahead():
+        first.start()
+        first.wait_send()
+
+    when(jnp.logical_not(inside_line()), ahead)
+    for step in STEPS:
+        device, other = chip_peer(step)
+        copy = remote(part.at[rows_at(other, count)], sums.at[step - 1], send.at[step], recv.at[step], device)
+        if step == 2:
+            when(jnp.logical_not(inside_line()), copy.start)
+        else:
+            when(jnp.logical_not(spans_line(other)), copy.start)
+
+
+def reduce_relay(part, count, sums, via, mixed, send, recv):
+    chip = place_of()[1]
+    other = lax.rem(chip + 2, CHIPS)
+    copy = remote(mixed, sums.at[1], send.at[2], recv.at[2], device_on(other))
+
+    def pass_on():
+        remote(mixed, via, send.at[0], recv.at[0], device_on(other)).wait_recv()
+        mixed[...] = (
+            part[rows_at(other, count), :].astype(jnp.float32) + via[...].astype(jnp.float32)
+        ).astype(mixed.dtype)
+        copy.start()
+
+    when(inside_line(), pass_on)
+
+
+def reduce_wait(part, count, sums, total, send, recv):
+    chip = place_of()[1]
+    total[...] = part[rows_at(chip, count), :].astype(jnp.float32)
+    for step in (1, 3, 2):
+        source = lax.rem(chip + CHIPS - step, CHIPS)
+
+        def add(step=step, source=source):
+            here = sums.at[step - 1]
+            remote(here, here, send.at[step], recv.at[step], device_on(source)).wait_recv()
+            total[...] += sums[step - 1].astype(jnp.float32)
+
+        when(jnp.logical_not(spans_line(source)), add)
+
+
+def reduce_drain(part, count, sums, send, recv):
+    rows = part.at[rows_at(0, count)]
+    for step in STEPS:
+        device, other = chip_peer(step)
+        copy = remote(rows, sums.at[step - 1], send.at[step], recv.at[step], device)
+        when(jnp.logical_not(spans_line(other)), copy.wait_send)
+
+
+def to_line(src, there, send, recv):
     return [
-        begin(remote(src, dst_of, send.at[step], recv.at[step], chip_peer(step)[0])) for step in STEPS
+        begin(remote(src, there, send.at[step], recv.at[step], chip_peer(step)[0])) for step in STEPS
     ]
 
 
@@ -350,6 +474,10 @@
     return pltpu.SemaphoreType.DMA(shape)
 
 
+def line_dma():
+    return dma(2, CHIPS, PIECES)
+
+
 def in_vmem():
     return pl.BlockSpec(memory_space=pltpu.VMEM)
 
@@ -360,10 +488,10 @@
 
 def attend_kernel(
     states, qkv_src, mlp_src, qk_gain, query_pos, key_pos,
-    states_all, w_qkv, w_part, raw_out, query_out, both, att_out, inv_out, attx,
+    states_all, w_qkv, w_up, w_gate, low_down, raw_out, query_out, both, att_out, inv_out, attx,
     stage_q, low_q, stage_m, low_m, raw, att_low,
     local_sem, x_send, x_recv, q_send, q_recv, mt_send, mt_recv, wz_send, wz_recv,
-    ws_send, ws_recv, wt_send, wt_recv, m_send, m_recv, kv_send, kv_recv, a_send, a_recv,
+    ws_send, ws_recv, wt_send, wt_recv, m_send, m_recv, ms_send, ms_recv, kv_send, kv_recv, a_send, a_recv,
 ):
     seq, chip, core = place_of()
     rows = qkv_src.shape[2]
@@ -375,7 +503,7 @@
     group_rows = tok_rows * CHIPS
     chip_rows = CORES * rows
     seq_rows = CHIPS * chip_rows
-    half_units = w_part.shape[2]
+    half_units = w_up.shape[1]
     ff_width = mlp_src.shape[1] // 3
     meet()
     block = rows_at(chip, tok_rows)
@@ -413,28 +541,36 @@
         copy.wait()
     for copy in m_swaps:
         copy.wait()
-    low_m[...] = stage_m[...].astype(jnp.bfloat16)
+    low_m[...] = stage_m[:2].astype(jnp.bfloat16)
+    low_down[...] = stage_m[2].astype(jnp.bfloat16)
     for copy in line:
         copy.wait_recv()
-    sends = gather_line(states, states_all.at[block], x_send, x_recv)
-    seq_part = w_qkv.at[core, rows_at(seq, seq_rows)]
+    gather_start(states, states_all, tok_rows, x_send, x_recv)
+    seq_at = rows_at(seq, seq_rows)
+    seq_part = w_qkv.at[core, seq_at]
     across = [
         begin(remote(seq_part, seq_part, ws_send.at[step], ws_recv.at[step], seq_peer(step)[0]))
         for step in STEPS
     ]
+    gather_hop(states_all, tok_rows, 1, x_send, x_recv)
     for copy in across:
         copy.wait_recv()
     swap = begin(remote(w_qkv.at[core], w_qkv.at[core], wt_send.at[0], wt_recv.at[0], twin()))
+    gather_hop(states_all, tok_rows, 2, x_send, x_recv)
+    gather_hop(states_all, tok_rows, 3, x_send, x_recv)
+    here = rows_at(chip, chip_rows)
+
+    def to_chips(part, there):
+        return [
+            begin(remote(low_m.at[part, chip_peer(step)[1]], there, m_send.at[part, step], m_recv.at[part, step], chip_peer(step)[0]))
+            for step in STEPS
+        ]
+
+    mine_up = w_up.at[seq_at]
+    m_line = to_chips(0, w_up.at[my_rows])
+    w_up[my_rows, :] = low_m[0, chip]
+    w_gate[here, :] = low_m[1, chip]
     swap.wait()
-    for copy in sends:
-        copy.wait_recv()
-    m_line = []
-    for part in range(3):
-        for step in STEPS:
-            device, other = chip_peer(step)
-            there = w_part.at[part, rows_at(chip, chip_rows)]
-            m_line.append(begin(remote(low_m.at[part, other], there, m_send.at[part, step], m_recv.at[part, step], device)))
-        w_part[part, rows_at(chip, chip_rows), :] = low_m[part, chip]
 
     for half in range(CORES):
         value = dot(states_all[...], w_qkv[half])
@@ -456,6 +592,13 @@
         start = 2 * head_cols + head * HEAD_DIM
         both[core, 1, head] = raw[:, start : start + HEAD_DIM].astype(jnp.bfloat16)
     swap = begin(remote(both.at[core], both.at[core], kv_send.at[0], kv_recv.at[0], twin()))
+    for copy in m_line:
+        copy.wait_recv()
+    m_line += to_chips(1, w_gate.at[here])
+    up_across = [
+        begin(remote(mine_up, mine_up, ms_send.at[step], ms_recv.at[step], seq_peer(step)[0]))
+        for step in STEPS
+    ]
     swap.wait()
 
     tile = min(128, group_rows)
@@ -485,9 +628,12 @@
         device, other = chip_peer(step)
         out.append(begin(remote(att_low.at[rows_at(other, tok_rows)], attx.at[chip], a_send.at[step], a_recv.at[step], device)))
     attx[chip] = att_low[block, :]
-    for copy in out + m_line:
+    for copy in m_line[3:]:
+        copy.wait_recv()
+    for copy in out + up_across:
         copy.wait()
-    for copy in sends + line + across:
+    gather_drain(states_all, tok_rows, x_send, x_recv)
+    for copy in m_line + line + across:
         copy.wait_send()
 
 
@@ -504,7 +650,9 @@
         out_shape=[
             shape((group_rows, model_width), low),
             shape((CORES, model_width, half_cols), low),
-            shape((3, chips * CORES * rows, half_units), low),
+            shape((model_width, half_units), low),
+            shape((chips * CORES * rows, half_units), low),
+            shape((chips, CORES * rows, half_units), low),
             shape((2, heads, group_rows, HEAD_DIM), f32),
             shape((heads, group_rows, HEAD_DIM), low),
             shape((CORES, 2, heads, group_rows, HEAD_DIM), low),
@@ -513,16 +661,16 @@
             shape((chips, tok_rows, heads * HEAD_DIM), low),
         ],
         in_specs=[in_vmem(), in_hbm(), in_hbm(), in_vmem(), in_vmem(), in_vmem()],
-        out_specs=[in_vmem()] * 9,
+        out_specs=[in_vmem()] * 11,
         scratch_shapes=[
             VMEM((chips, CORES * rows, half_cols), f32),
             VMEM((chips, CORES * rows, half_cols), low),
             VMEM((3, chips, CORES * rows, half_units), f32),
-            VMEM((3, chips, CORES * rows, half_units), low),
+            VMEM((2, chips, CORES * rows, half_units), low),
             VMEM((group_rows, 3 * heads * HEAD_DIM), f32),
             VMEM((group_rows, heads * HEAD_DIM), low),
-            dma(16), dma(4), dma(4), dma(4), dma(4), dma(3, 4), dma(3, 4), dma(4), dma(4),
-            dma(4), dma(4), dma(1), dma(1), dma(3, 4), dma(3, 4), dma(1), dma(1), dma(4), dma(4),
+            dma(16), line_dma(), line_dma(), dma(4), dma(4), dma(3, 4), dma(3, 4), dma(4), dma(4),
+            dma(4), dma(4), dma(1), dma(1), dma(2, 4), dma(2, 4), dma(4), dma(4), dma(1), dma(1), dma(4), dma(4),
         ],
         compiler_params=pltpu.CompilerParams(
             collective_id=1, has_side_effects=True, vmem_limit_bytes=LIMIT
@@ -537,34 +685,42 @@
 
 
 def mlp_kernel(
-    attx, states, cotangent, w_out, alpha_attn, alpha_mlp, gain_u, gain_v, w_part,
-    out, grad_attx, grad_w_out, grad_direct, dot_a, dot_m, dot_u, dot_v, grad_half,
+    attx, states, cotangent, w_out, alpha_attn, alpha_mlp, gain_u, gain_v, w_up, w_gate, low_down,
+    out, grad_attx, grad_w_out, grad_direct, dot_a, dot_m, dot_u, dot_v, grad_half, grad_down,
     weights, mixed_one, attn_unit, factors, mixed_low, mixed_all, up, gate, hidden, part,
-    sums, grad_two, branch_low, branch_all, grad_u, grad_v, wide, turned, arrived,
+    sums, via, passed, total, grad_two, branch_low, branch_all, grad_u, grad_v, wide, turned, arrived,
+    w_down, down_half, down_got,
     local_sem, ws_send, ws_recv, wt_send, wt_recv, x_send, x_recv, r_send, r_recv,
-    g_send, g_recv, b_send, b_recv, d_send, d_recv,
+    g_send, g_recv, b_send, b_recv, d_send, d_recv, wz_send, wz_recv, ds_send, ds_recv,
 ):
     seq, chip, core = place_of()
     tok_rows, model_width = states.shape
     chip_heads = attx.shape[2]
-    seq_rows = w_part.shape[1]
-    half_units = w_part.shape[2]
+    seq_rows, half_units = w_gate.shape
+    chip_rows = low_down.shape[1]
     group_rows = CHIPS * tok_rows
     block = rows_at(chip, tok_rows)
     meet()
     seq_at = rows_at(seq, seq_rows)
-
-    def spread(which):
+    here = rows_at(chip, chip_rows)
+    swaps = [begin(remote(w_up, weights.at[0, core], wt_send.at[0], wt_recv.at[0], twin()))]
+    to_chips = [
+        begin(remote(low_down.at[chip_peer(step)[1]], w_down.at[here], wz_send.at[step], wz_recv.at[step], chip_peer(step)[0]))
+        for step in STEPS
+    ]
+
+    def spread(which, src):
         return [
-            begin(remote(w_part.at[which], weights.at[which, core, seq_at], ws_send.at[which, step], ws_recv.at[which, step], seq_peer(step)[0]))
+            begin(remote(src, weights.at[which, core, seq_at], ws_send.at[which, step], ws_recv.at[which, step], seq_peer(step)[0]))
             for step in STEPS
         ]
 
-    across = spread(0) + spread(1)
+    across = spread(1, w_gate)
     keeps = [
-        begin(pltpu.make_async_copy(w_part.at[which], weights.at[which, core, seq_at], local_sem.at[which]))
-        for which in range(3)
+        begin(pltpu.make_async_copy(w_up, weights.at[0, core], local_sem.at[0])),
+        begin(pltpu.make_async_copy(w_gate, weights.at[1, core, seq_at], local_sem.at[1])),
     ]
+    w_down[here, :] = low_down[chip]
     branch = sum(dot(attx[at], w_out[at]) for at in range(CHIPS))
     unit, factor = unit_of(branch)
     attn_unit[...] = unit
@@ -574,19 +730,20 @@
     mixed_one[...] = value
     factors[1] = factor
     mixed_low[...] = value.astype(jnp.bfloat16)
-    line = gather_line(mixed_low, mixed_all.at[block], x_send, x_recv)
+    gather_start(mixed_low, mixed_all, tok_rows, x_send, x_recv)
     mixed_all[block, :] = mixed_low[...]
     for copy in keeps:
         copy.wait()
+    for copy in to_chips:
+        copy.wait_recv()
+    gather_hop(mixed_all, tok_rows, 1, x_send, x_recv)
     for copy in across:
         copy.wait_recv()
-    swaps = [
-        begin(remote(weights.at[which, core], weights.at[which, core], wt_send.at[which], wt_recv.at[which], twin()))
-        for which in range(2)
-    ]
-    across += spread(2)
-    for copy in line:
-        copy.wait_recv()
+    across += spread(2, w_down)
+    weights[2, core, seq_at, :] = w_down[...]
+    swaps.append(begin(remote(weights.at[1, core], weights.at[1, core], wt_send.at[1], wt_recv.at[1], twin())))
+    gather_hop(mixed_all, tok_rows, 2, x_send, x_recv)
+    gather_hop(mixed_all, tok_rows, 3, x_send, x_recv)
     for copy in swaps:
         copy.wait_recv()
     for half in range(CORES):
@@ -618,23 +775,10 @@
 
     lax.fori_loop(0, model_width // tile, down, 0)
 
-    def reduce_line(which, send, recv):
-        sent = []
-        for step in STEPS:
-            device, other = chip_peer(step)
-            sent.append(begin(remote(part.at[which, rows_at(other, tok_rows)], sums.at[which, step], send.at[step], recv.at[step], device)))
-        return sent
-
-    def reduced(which):
-        total = part[which, block, :].astype(jnp.float32)
-        for step in STEPS:
-            total = total + sums[which, step].astype(jnp.float32)
-        return total
-
-    sent = reduce_line(0, r_send, r_recv)
-    for copy in sent:
-        copy.wait_recv()
-    mlp_unit, mlp_factor = unit_of(reduced(0))
+    reduce_start(part.at[0], tok_rows, sums.at[0], via.at[0], r_send, r_recv)
+    reduce_relay(part.at[0], tok_rows, sums.at[0], via.at[0], passed.at[0], r_send, r_recv)
+    reduce_wait(part.at[0], tok_rows, sums.at[0], total, r_send, r_recv)
+    mlp_unit, mlp_factor = unit_of(total[...])
     value, factor = unit_of(mixed_one[...] + alpha_mlp[...] * (mlp_unit - mixed_one[...]))
     out[...] = value.astype(jnp.bfloat16)
     above = cotangent[...].astype(jnp.float32)
@@ -644,11 +788,12 @@
     grad = grad * alpha_mlp[...]
     grad = mlp_factor * (grad - mlp_unit * jnp.sum(grad * mlp_unit, axis=-1, keepdims=True))
     branch_low[...] = grad.astype(jnp.bfloat16)
-    back = gather_line(branch_low, branch_all.at[block], g_send, g_recv)
+    gather_start(branch_low, branch_all, tok_rows, g_send, g_recv)
     branch_all[block, :] = branch_low[...]
+    gather_hop(branch_all, tok_rows, 1, g_send, g_recv)
+    gather_hop(branch_all, tok_rows, 2, g_send, g_recv)
     turned[0] = mixed_all[...].T
-    for copy in back:
-        copy.wait_recv()
+    gather_hop(branch_all, tok_rows, 3, g_send, g_recv)
     for half in range(CORES):
         wide[half] = dot(branch_all[...], weights[2, half])
     dot_u[...] = jnp.zeros_like(dot_u)
@@ -682,24 +827,35 @@
     lax.fori_loop(0, model_width // tile, back_down, 0)
     for copy in swaps:
         copy.wait_send()
-    sent += reduce_line(1, b_send, b_recv)
+    reduce_start(part.at[1], tok_rows, sums.at[1], via.at[1], b_send, b_recv)
     turned[1] = branch_all[...].T
-    pairs = ((0, grad_u), (1, grad_v), (2, hidden))
-    swaps = []
-    for which, right in pairs:
-        left = 1 if which == 2 else 0
-
-        def weight_grad(index, carry, which=which, right=right, left=left):
+    swaps = {}
+
+    def weight_grads(which, left, right):
+        def one(index, carry):
             half = index // 5
             at = rows_at(lax.rem(index, 5), tile)
             weights[which, half, at, :] = dot(turned[left, at, :], right[half]).astype(jnp.bfloat16)
             return carry
 
-        lax.fori_loop(0, CORES * 5, weight_grad, 0)
-        swaps.append(begin(remote(weights.at[which, 1 - core], arrived.at[which], d_send.at[which], d_recv.at[which], twin())))
-    for copy in sent[3:]:
-        copy.wait_recv()
-    grad = grad_two[...] * (1.0 - alpha_mlp[...]) + reduced(1)
+        lax.fori_loop(0, CORES * 5, one, 0)
+        swaps[which] = begin(remote(weights.at[which, 1 - core], arrived.at[which], d_send.at[which], d_recv.at[which], twin()))
+
+    def both_cores(which):
+        swaps[which].wait_recv()
+        return (weights[which, core].astype(jnp.float32) + arrived[which].astype(jnp.float32)).astype(jnp.bfloat16)
+
+    weight_grads(2, 1, hidden)
+    reduce_relay(part.at[1], tok_rows, sums.at[1], via.at[1], passed.at[1], b_send, b_recv)
+    down_half[...] = both_cores(2)
+    down_across = [
+        begin(remote(down_half.at[rows_at(seq_peer(step)[1], seq_rows)], down_got.at[step - 1], ds_send.at[step], ds_recv.at[step], seq_peer(step)[0]))
+        for step in STEPS
+    ]
+    weight_grads(0, 0, grad_u)
+    weight_grads(1, 0, grad_v)
+    reduce_wait(part.at[1], tok_rows, sums.at[1], total, b_send, b_recv)
+    grad = grad_two[...] * (1.0 - alpha_mlp[...]) + total[...]
     value = mixed_one[...]
     grad = factors[1] * (grad - value * jnp.sum(grad * value, axis=-1, keepdims=True))
     unit = attn_unit[...]
@@ -711,19 +867,25 @@
     for at in range(CHIPS):
         grad_attx[at] = dot_nt(low, w_out[at]).astype(jnp.bfloat16)
         grad_w_out[at] = dot_tn(attx[at], low).astype(jnp.bfloat16)
-    for which in range(3):
-        swaps[which].wait_recv()
-        grad_half[which] = (
-            weights[which, core].astype(jnp.float32) + arrived[which].astype(jnp.float32)
-        ).astype(jnp.bfloat16)
-    for copy in across + line + sent + back + swaps:
+    for which in range(2):
+        grad_half[which] = both_cores(which)
+    whole = down_half[seq_at, :].astype(jnp.float32)
+    for step in STEPS:
+        down_across[step - 1].wait_recv()
+        whole = whole + down_got[step - 1].astype(jnp.float32)
+    grad_down[...] = whole.astype(jnp.bfloat16)
+    gather_drain(mixed_all, tok_rows, x_send, x_recv)
+    gather_drain(branch_all, tok_rows, g_send, g_recv)
+    reduce_drain(part.at[0], tok_rows, sums.at[0], r_send, r_recv)
+    reduce_drain(part.at[1], tok_rows, sums.at[1], b_send, b_recv)
+    for copy in across + to_chips + down_across + [swaps[which] for which in range(3)]:
         copy.wait_send()
 
 
-def mlp_call(attx, states, cotangent, w_out, alpha_attn, alpha_mlp, gain_u, gain_v, w_part):
+def mlp_call(attx, states, cotangent, w_out, alpha_attn, alpha_mlp, gain_u, gain_v, w_up, w_gate, low_down):
     tok_rows, model_width = states.shape
     chips, _, chip_heads = attx.shape
-    half_units = w_part.shape[2]
+    seq_rows, half_units = w_gate.shape
     group_rows = chips * tok_rows
     f32, low = jnp.float32, jnp.bfloat16
     shape = jax.ShapeDtypeStruct
@@ -741,10 +903,11 @@
             shape((1, model_width), f32),
             shape((CORES, 1, half_units), f32),
             shape((CORES, 1, half_units), f32),
-            shape((3,) + matrix, low),
+            shape((2,) + matrix, low),
+            shape((seq_rows, half_units), low),
         ],
-        in_specs=[in_vmem()] * 8 + [in_hbm()],
-        out_specs=[in_vmem()] * 9,
+        in_specs=[in_vmem()] * 8 + [in_hbm(), in_vmem(), in_vmem()],
+        out_specs=[in_vmem()] * 10,
         scratch_shapes=[
             VMEM((3, CORES) + matrix, low),
             VMEM(tokens, f32),
@@ -756,7 +919,10 @@
             VMEM(wide, f32),
             VMEM(wide, low),
             VMEM((2,) + group, low),
-            VMEM((2, chips) + tokens, low),
+            VMEM((2, 3) + tokens, low),
+            VMEM((2,) + tokens, low),
+            VMEM((2,) + tokens, low),
+            VMEM(tokens, f32),
             VMEM(tokens, f32),
             VMEM(tokens, low),
             VMEM(group, low),
@@ -765,21 +931,26 @@
             VMEM(wide, f32),
             VMEM((2, model_width, group_rows), low),
             VMEM((3,) + matrix, low),
-            dma(3), dma(3, 4), dma(3, 4), dma(3), dma(3), dma(4), dma(4), dma(4), dma(4),
-            dma(4), dma(4), dma(4), dma(4), dma(3), dma(3),
+            VMEM((seq_rows, half_units), low),
+            VMEM(matrix, low),
+            VMEM((3, seq_rows, half_units), low),
+            dma(2), dma(3, 4), dma(3, 4), dma(3), dma(3), line_dma(), line_dma(), dma(4), dma(4),
+            line_dma(), line_dma(), dma(4), dma(4), dma(3), dma(3), dma(4), dma(4), dma(4), dma(4),
         ],
         compiler_params=pltpu.CompilerParams(
             collective_id=2, has_side_effects=True, vmem_limit_bytes=LIMIT
         ),
         name="mlp",
-    )(attx, states, cotangent, w_out, alpha_attn, alpha_mlp, gain_u, gain_v, w_part)
+    )(
+        attx, states, cotangent, w_out, alpha_attn, alpha_mlp, gain_u, gain_v, w_up, w_gate, low_down
+    )
 
 
 def back_kernel(
-    grad_attx, grad_half, grad_w_out, small_in, raw, query, both, att, inverse, states_all,
+    grad_attx, grad_half, grad_down, grad_w_out, small_in, raw, query, both, att, inverse, states_all,
     w_qkv, qk_gain, query_pos, key_pos, grad_direct,
     grad_states, out_mlp, out_qkv, out_proj, small_out,
-    att_low, heads_low, to_keys, swap_low, swap_kv, grad_heads, grad_sides, part, sums, turned,
+    att_low, heads_low, to_keys, swap_low, swap_kv, grad_heads, grad_sides, part, sums, via, passed, total, turned,
     grad_q, half_q, seq_q, line_q, wide_q, half_o, pair_o, seq_got, seq_low, line_got, wide,
     wide_o, small, small_pair, small_seq, dots,
     local_sem, a_send, a_recv, s_send, s_recv, o_send, o_recv, kv_send, kv_recv, r_send, r_recv,
@@ -811,13 +982,23 @@
     other_at = pl.ds(pl.multiple_of((1 - core) * half_units, 128), half_units)
     pair = begin(remote(grad_w_out.at[:, :, other_at], pair_o, o_send.at[0], o_recv.at[0], twin()))
     across = []
-    for which in range(3):
+    onward = {}
+
+    def to_chips(which, src):
+        onward[which] = [
+            begin(remote(src.at[rows_at(chip_peer(step)[1], chip_rows)], line_got.at[which, chip], z_send.at[which, step], z_recv.at[which, step], chip_peer(step)[0]))
+            for step in STEPS
+        ]
+        line_got[which, chip] = src[rows_at(chip, chip_rows), :]
+
+    to_chips(2, grad_down)
+    for which in range(2):
         for step in STEPS:
             device, other = seq_peer(step)
             across.append(begin(remote(grad_half.at[which, rows_at(other, seq_rows)], seq_got.at[which, step - 1], s_send.at[which, step], s_recv.at[which, step], device)))
     keeps = [
         begin(pltpu.make_async_copy(grad_half.at[which, rows_at(seq, seq_rows)], seq_low.at[which], local_sem.at[which]))
-        for which in range(3)
+        for which in range(2)
     ]
     to_keys[...] = jnp.zeros_like(to_keys)
     dots[...] = jnp.zeros_like(dots)
@@ -827,7 +1008,7 @@
         half_o[at] = (grad_w_out[at, :, half_at].astype(f32) + pair_o[at].astype(f32)).astype(low)
     for step in STEPS:
         device, other = seq_peer(step)
-        across.append(begin(remote(half_o.at[other], seq_got.at[3, step - 1], s_send.at[3, step], s_recv.at[3, step], device)))
+        across.append(begin(remote(half_o.at[other], seq_got.at[2, step - 1], s_send.at[2, step], s_recv.at[2, step], device)))
     for copy in line:
         copy.wait_recv()
     for head in range(heads):
@@ -892,10 +1073,7 @@
         return carry
 
     lax.fori_loop(0, 5, down, 0)
-    reduce = []
-    for step in STEPS:
-        device, other = chip_peer(step)
-        reduce.append(begin(remote(part.at[rows_at(other, tok_rows)], sums.at[step - 1], r_send.at[step], r_recv.at[step], device)))
+    reduce_start(part, tok_rows, sums, via, r_send, r_recv)
 
     def weight_grad(index, carry):
         half = index // 5
@@ -905,6 +1083,7 @@
 
     lax.fori_loop(0, CORES * 5, weight_grad, 0)
     swap_q = begin(remote(grad_q.at[1 - core], half_q, qt_send.at[0], qt_recv.at[0], twin()))
+    reduce_relay(part, tok_rows, sums, via, passed, r_send, r_recv)
     small[...] = small_in[...]
     small[4:5, :head_cols] = jnp.concatenate([dots[head] for head in range(heads)], axis=1)
     swap_s = begin(remote(small, small_pair, t_send.at[0], t_recv.at[0], twin()))
@@ -922,25 +1101,21 @@
     ]
     for copy in keeps:
         copy.wait()
-    seq_low[3] = half_o[seq]
-    onward = []
-    for which in range(4):
-        for copy in across[3 * which : 3 * which + 3]:
+    seq_low[2] = half_o[seq]
+    for at, which in enumerate((0, 1, 3)):
+        for copy in across[3 * at : 3 * at + 3]:
             copy.wait_recv()
-        total = seq_low[which].astype(f32)
+        whole = seq_low[at].astype(f32)
         for step in STEPS:
-            total = total + seq_got[which, step - 1].astype(f32)
-        seq_low[which] = total.astype(low)
-        for step in STEPS:
-            device, other = chip_peer(step)
-            onward.append(begin(remote(seq_low.at[which, rows_at(other, chip_rows)], line_got.at[which, chip], z_send.at[which, step], z_recv.at[which, step], device)))
-        line_got[which, chip] = seq_low[which, rows_at(chip, chip_rows), :]
+            whole = whole + seq_got[at, step - 1].astype(f32)
+        seq_low[at] = whole.astype(low)
+        to_chips(which, seq_low.at[at])
     for copy in across_q:
         copy.wait_recv()
-    total = half_q[rows_at(seq, seq_rows), :].astype(f32)
+    whole = half_q[rows_at(seq, seq_rows), :].astype(f32)
     for step in STEPS:
-        total = total + seq_q[step - 1].astype(f32)
-    grad_q[0, :seq_rows, :] = total.astype(low)
+        whole = whole + seq_q[step - 1].astype(f32)
+    grad_q[0, :seq_rows, :] = whole.astype(low)
     onward_q = []
     for step in STEPS:
         device, other = chip_peer(step)
@@ -950,19 +1125,15 @@
         copy.wait()
     small_pair[...] = small[...] + small_seq[0] + small_seq[1] + small_seq[2]
     small_out[chip] = small_pair[...]
-    ends = gather_line(small_pair, small_out.at[chip], p_send, p_recv)
-    for copy in reduce:
-        copy.wait_recv()
-    total = part[block, :].astype(f32) + grad_direct[...]
-    for step in STEPS:
-        total = total + sums[step - 1].astype(f32)
-    grad_states[...] = total.astype(low)
+    ends = to_line(small_pair, small_out.at[chip], p_send, p_recv)
+    reduce_wait(part, tok_rows, sums, total, r_send, r_recv)
+    grad_states[...] = (total[...] + grad_direct[...]).astype(low)
 
     mine = rows_at(core, rows)
     theirs = rows_at(1 - core, rows)
     last, lasts = [], []
-    for which in range(3):
-        for copy in onward[3 * which : 3 * which + 3]:
+    for which in (2, 0, 1):
+        for copy in onward[which]:
             copy.wait_recv()
         for at in range(CHIPS):
             wide[which, at] = line_got[which, at].astype(f32)
@@ -970,12 +1141,12 @@
             there = out_mlp.at[:, pl.ds(pl.multiple_of(start, 128), half_units)]
             last.append(begin(remote(wide.at[which, at, theirs], there, f_send.at[which, at], f_recv.at[which, at], twin())))
             lasts.append(begin(pltpu.make_async_copy(wide.at[which, at, mine], there, local_sem.at[3 + which * CHIPS + at])))
-    for copy in onward[9:]:
+    for copy in onward[3]:
         copy.wait_recv()
-    total = line_got[3, 0].astype(f32)
+    whole = line_got[3, 0].astype(f32)
     for at in range(1, CHIPS):
-        total = total + line_got[3, at].astype(f32)
-    wide_o[...] = total
+        whole = whole + line_got[3, at].astype(f32)
+    wide_o[...] = whole
     there = out_proj.at[:, half_at]
     last.append(begin(remote(wide_o.at[theirs], there, f_send.at[3, 0], f_recv.at[3, 0], twin())))
     lasts.append(begin(pltpu.make_async_copy(wide_o.at[mine], there, local_sem.at[15])))
@@ -987,12 +1158,13 @@
     lasts.append(begin(pltpu.make_async_copy(wide_q.at[:, mine], there, local_sem.at[16])))
     for copy in ends + last + lasts:
         copy.wait()
-    for copy in line + [pair] + across + reduce + across_q + onward + onward_q:
+    reduce_drain(part, tok_rows, sums, r_send, r_recv)
+    for copy in line + [pair] + across + across_q + onward_q + sum(onward.values(), []):
         copy.wait_send()
 
 
 def back_call(
-    grad_attx, grad_half, grad_w_out, small_in, raw, query, both, att, inverse, states_all,
+    grad_attx, grad_half, grad_down, grad_w_out, small_in, raw, query, both, att, inverse, states_all,
     w_qkv, qk_gain, query_pos, key_pos, grad_direct, rows,
 ):
     tok_rows, model_width = grad_direct.shape
@@ -1016,7 +1188,7 @@
             shape((rows, CORES * half_units), f32),
             shape((chips,) + small_in.shape, f32),
         ],
-        in_specs=[in_vmem(), in_hbm()] + [in_vmem()] * 13,
+        in_specs=[in_vmem(), in_hbm()] + [in_vmem()] * 14,
         out_specs=[in_vmem(), in_hbm(), in_hbm(), in_hbm(), in_vmem()],
         scratch_shapes=[
             VMEM((group_rows, head_cols), low),
@@ -1028,6 +1200,9 @@
             VMEM((CORES, group_rows, half_cols), low),
             VMEM((group_rows, model_width), low),
             VMEM((3, tok_rows, model_width), low),
+            VMEM((tok_rows, model_width), low),
+            VMEM((tok_rows, model_width), low),
+            VMEM((tok_rows, model_width), f32),
             VMEM((model_width, group_rows), low),
             VMEM((CORES, model_width, half_cols), low),
             VMEM((model_width, half_cols), low),
@@ -1036,8 +1211,8 @@
             VMEM((chips, chip_rows, half_cols), f32),
             VMEM((4, seq_rows, half_units), low),
             VMEM((4, seq_rows, half_units), low),
-            VMEM((4, 3, seq_rows, half_units), low),
-            VMEM((4, seq_rows, half_units), low),
+            VMEM((3, 3, seq_rows, half_units), low),
+            VMEM((3, seq_rows, half_units), low),
             VMEM((4, chips, chip_rows, half_units), low),
             VMEM((3, chips, chip_rows, half_units), f32),
             VMEM((chip_rows, half_units), f32),
@@ -1054,7 +1229,7 @@
         ),
         name="back",
     )(
-        grad_attx, grad_half, grad_w_out, small_in, raw, query, both, att, inverse, states_all,
+        grad_attx, grad_half, grad_down, grad_w_out, small_in, raw, query, both, att, inverse, states_all,
         w_qkv, qk_gain, query_pos, key_pos, grad_direct,
     )
 
@@ -1085,17 +1260,17 @@
     )
     query_pos = (own_places[:, None] * tok_rows + offsets).reshape(group_rows, 1)
     key_pos = (places.T[:, :, None] * tok_rows + offsets).reshape(1, CORES * group_rows)
-    states_all, w_qkv, w_part, raw, query, both, att, inverse, attx = attend_call(
+    states_all, w_qkv, w_up, w_gate, low_down, raw, query, both, att, inverse, attx = attend_call(
         states, qkv_src, mlp_weights, qk_gain, query_pos, key_pos
     )
     gain_u = lax.dynamic_slice_in_dim(unit_gains[:, 0], chip * units, units)
     gain_v = lax.dynamic_slice_in_dim(unit_gains[:, 1], chip * units, units) * math.sqrt(D)
     (
-        out_low, grad_attx, grad_w_out, grad_direct, grad_alpha_a, grad_alpha_m, grad_s_u, grad_s_v, grad_half
+        out_low, grad_attx, grad_w_out, grad_direct, grad_alpha_a, grad_alpha_m, grad_s_u, grad_s_v, grad_half, grad_down
     ) = mlp_call(
         attx, states, cotangent, w_out.reshape(chips, head_cols, model_width),
         feature_gains[:, 1].reshape(1, model_width), feature_gains[:, 2].reshape(1, model_width),
-        gain_u.reshape(CORES, 1, units // CORES), gain_v.reshape(CORES, 1, units // CORES), w_part,
+        gain_u.reshape(CORES, 1, units // CORES), gain_v.reshape(CORES, 1, units // CORES), w_up, w_gate, low_down,
     )
     small = jnp.concatenate(
         [
@@ -1104,7 +1279,7 @@
         ]
     )
     grad_states, grad_mlp, grad_qkv, grad_proj, small = back_call(
-        grad_attx, grad_half, grad_w_out, small, raw, query, both, att, inverse, states_all,
+        grad_attx, grad_half, grad_down, grad_w_out, small, raw, query, both, att, inverse, states_all,
         w_qkv, qk_gain, query_pos, key_pos, grad_direct, rows,
     )
     grad_qkv = grad_qkv.reshape(CORES, chips, rows, 3, head_cols // CORES)

time: 434 us -> 385 us (0.89)
  Pallas kernels: 393 us -> 343 us
    pallas_call x1, Pallas kernels: 129 us -> 106 us  [back_call(): pl.pallas_call(back_kernel, out_shape=[shape((tok_rows, model_width), low...]
    pallas_call x1, Pallas kernels: 163 us -> 144 us  [mlp_call(): pl.pallas_call(mlp_kernel, out_shape=[shape(tokens, low), shape(attx.shap...]
    pallas_call x1, Pallas kernels: 101 us -> 93.4 us  [attend_call(): pl.pallas_call(attend_kernel, out_shape=[shape((group_rows, model_width),...]
  transfers between devices with their start and end apart: 1 -> 1, of which waited for: 0 -> 0; matrix products, arithmetic and copies ran while one was open for 3% -> 3% of each run, Pallas kernels for 23% -> 24%
where the time goes in v4:
time: 385 us; the launch traced here: 383 us
  Pallas kernels  343 us (89%)
  local copies, waits for them, and re-layouts  19.2 us (5%)
  between operations  14.2 us (4%)
  other arithmetic  6.99 us (2%)
    pallas_call x1, Pallas kernels, mlp_call(): pl.pallas_call(mlp_kernel, out_shape=[shape(tokens, low), shape(attx.shap...  144 us
    pallas_call x1, Pallas kernels, back_call(): pl.pallas_call(back_kernel, out_shape=[shape((tok_rows, model_width), low...  106 us
    pallas_call x1, Pallas kernels, attend_call(): pl.pallas_call(attend_kernel, out_shape=[shape((group_rows, model_width),...  93.4 us
  transfers between devices with their start and end apart: 1, of which 0 were waited for; matrix products, arithmetic and copies ran while one was open for 3% of the time, Pallas kernels for 24%

profile of v4, /device:TPU:0, one launch (start us, length us, event | category | flops | bytes accessed | tf_op | source)
XLA Modules:
  0.0 383.2 jit_solution(1595578620460232496)
XLA Ops:
  7.2 0.0 all-gather.2.cloned.1.call-start
  7.2 1.6 slice.56
  8.8 0.0 all-gather.2.cloned.1.call-update
  8.8 1.1 slice.37
  10.0 0.5 broadcast.70
  10.5 1.3 reduce.9
  11.8 0.1 reshape_squeeze.9
  11.9 0.1 multiply_bitcast_fusion
  12.0 0.1 iota_add_fusion.1
  12.1 0.9 copy.22.query_pos
  13.0 1.4 slice_bitcast_fusion
  14.4 0.1 fusion.3
  14.5 0.6 reshape.132.qk_gain
  15.1 0.1 copy.21
  15.2 1.5 reshape.130
  16.7 0.5 copy.26
  17.2 0.0 copy-start.4
  17.2 1.6 reshape.131.qkv_src
  18.8 0.7 iota_add_fusion
  19.5 93.4 %attend.1 = (bf16[512,1280]{1,0:T(8,128)(2,1)}, bf16[2,1280,480]{2,1,0:T(8,128)(2,1)}, bf16[1280,640]{1,0:T(8,128)(2,1)}, bf16[320,640]{1,0:T(8,128)(2,1)}, bf16...) custom-call(bf16[128,1280]{1,0:T(8,128)(2,1)} %states.3, ...), custom_call_target="tpu_custom_call" | custom-call | tf_op jit(solution)/shard_map/attend/pallas_call | solution.py:648
  112.9 0.0 copy-done.4
  112.9 0.6 dynamic-slice_multiply_fusion
  113.5 0.0 all-gather.2.cloned.1.call-done
  113.5 143.7 %mlp.1 = (bf16[128,1280]{1,0:T(8,128)(2,1)}, bf16[4,128,320]{2,1,0:T(8,128)(2,1)}, bf16[4,320,1280]{2,1,0:T(8,128)(2,1)}, f32[128,1280]{1,0:T(8,128)}, f32[1,128...) custom-call(bf16[4,128,320]{2,1,0:T(8,128)(2,1)} %get-tuple-element., ...), custom_call_target="tpu_custom_call" | custom-call | tf_op jit(solution)/shard_map/mlp/pallas_call | solution.py:895
  257.2 0.7 broadcast_multiply_fusion
  257.9 1.4 concatenate.6.small_in
  259.3 105.7 %back.1 = (bf16[128,1280]{1,0:T(8,128)(2,1)}, f32[40,15360]{1,0:T(8,128)}, f32[2,4,40,480]{3,2,1,0:T(8,128)}, f32[40,1280]{1,0:T(8,128)}, f32[4,8,1280]{2,1,0:T(8,128)}) custom-call(bf16[4,128,320]{2,1,0:T(8,128)(2,1)} %get-tuple-element.37.grad_attx, bf16[2,1280,640]{2,1,0:T(8,128)(2,1)} %get-tuple-element.38.grad_half, ...), custom_call_target="tpu_custom_call" | custom-call | tf_op jit(solution)/shard_map/back/pallas_call | solution.py:1182
  365.0 1.2 fusion.4
  366.3 0.8 slice_reduce_fusion.2
  367.1 0.1 stack_reshape_squeeze.9
  367.2 0.0 copy-start.3
  367.2 1.9 reshape.136
  369.2 0.0 copy-start.1
  369.2 0.8 copy.24
  369.9 0.0 copy-start.2
  370.0 1.3 reshape.137
  371.2 0.0 copy-start
  371.2 0.0 copy-done.3
  371.2 0.9 pad_maximum_fusion
  372.2 0.7 fusion
  372.8 0.7 fusion.2
  373.5 0.0 copy-done.1
  373.5 0.7 copy.30
  374.2 0.0 copy-done.2
  374.2 0.7 copy.31
  374.9 0.0 copy-done
  374.9 1.4 copy.32
  (6 shorter events, 0.1 us)
Async XLA Ops:
  7.2 106.4 %all-gather.2.cloned.1.call-start = ((), (), s32[]{:S(2)}) async-start(), calls=%async_computation | async-start | bytes 3379200 | tf_op jit(solution)/shard_map/all_gather | solution.py:1251
  17.2 95.7 %copy-start.4 = (f32[5120,2]{0,1:T(2,128)S(1)}, f32[5120,2]{0,1:T(2,128)}, u32[]{:S(2)}) copy-start(f32[5120,2]{0,1:T(2,128)} %param.12) | copy-start | bytes 122884
  367.2 4.0 %copy-start.3 = (f32[40,1280]{1,0:T(8,128)S(1)}, f32[40,1280]{1,0:T(8,128)}, u32[]{:S(2)}) copy-start(f32[40,1280]{1,0:T(8,128)} %get-tuple-element.55) | copy-start | bytes 614404
  369.2 4.3 %copy-start.1 = (bf16[128,1280]{1,0:T(8,128)(2,1)S(1)}, bf16[128,1280]{1,0:T(8,128)(2,1)}, u32[]{:S(2)}) copy-start(bf16[128,1280]{1,0:T(8,128)(2,1)} %get-tuple-element.79) | copy-start | bytes 983044
  369.9 4.3 %copy-start.2 = (bf16[128,1280]{1,0:T(8,128)(2,1)S(1)}, bf16[128,1280]{1,0:T(8,128)(2,1)}, u32[]{:S(2)}) copy-start(bf16[128,1280]{1,0:T(8,128)(2,1)} %get-tuple-element.80) | copy-start | bytes 983044
  371.2 3.7 copy-start
Sparse Core Ops, SparseCore 0:
  11.4 71.1 all-gather.1

commit v5 on v4

--- a/solution.py
+++ b/solution.py
@@ -486,37 +486,54 @@
     return pl.BlockSpec(memory_space=pl.ANY)
 
 
+def key_positions(places, key_pos, tok_rows):
+    lanes = lax.broadcasted_iota(jnp.int32, (1, tok_rows), 1)
+    for at_core in range(CORES):
+        for at_chip in range(CHIPS):
+            start = (at_core * CHIPS + at_chip) * tok_rows
+            key_pos[:, start : start + tok_rows] = places[0, CORES * at_chip + at_core] * tok_rows + lanes
+
+
+def kept_pairs(places, key_pos, block, core, tok_rows):
+    down = lax.broadcasted_iota(jnp.int32, (tok_rows, 1), 0)
+    return key_pos[...] <= places[0, CORES * block + core] * tok_rows + down
+
+
 def attend_kernel(
-    states, qkv_src, mlp_src, qk_gain, query_pos, key_pos,
-    states_all, w_qkv, w_up, w_gate, low_down, raw_out, query_out, both, att_out, inv_out, attx,
-    stage_q, low_q, stage_m, low_m, raw, att_low,
+    states, attn_src, mlp_src, qk_gain, places,
+    states_all, w_qkv, w_out, w_up, w_gate, low_down, raw_out, query_out, both, att_out, inv_out, attx,
+    src_q, stage_q, low_q, stage_o, low_o, stage_m, low_m, raw, att_low, key_pos,
     local_sem, x_send, x_recv, q_send, q_recv, mt_send, mt_recv, wz_send, wz_recv,
-    ws_send, ws_recv, wt_send, wt_recv, m_send, m_recv, ms_send, ms_recv, kv_send, kv_recv, a_send, a_recv,
+    ws_send, ws_recv, wt_send, wt_recv, oz_send, oz_recv, os_send, os_recv, m_send, m_recv,
+    ms_send, ms_recv, kv_send, kv_recv, a_send, a_recv,
 ):
     seq, chip, core = place_of()
-    rows = qkv_src.shape[2]
-    half_cols = qkv_src.shape[3]
-    part_cols = half_cols // 3
-    tok_rows = states.shape[0]
+    rows = attn_src.shape[0]
+    tok_rows, model_width = states.shape
     heads = qk_gain.shape[0]
     head_cols = heads * HEAD_DIM
+    part_cols = head_cols // CORES
     group_rows = tok_rows * CHIPS
     chip_rows = CORES * rows
     seq_rows = CHIPS * chip_rows
     half_units = w_up.shape[1]
+    half_width = model_width // CORES
     ff_width = mlp_src.shape[1] // 3
+    low = jnp.bfloat16
+    for at in range(CHIPS):
+        for half in range(CORES):
+            for which in range(3):
+                start = which * model_width + at * head_cols + half * part_cols
+                src_q[at, half, :, which * part_cols : (which + 1) * part_cols] = attn_src[:, start : start + part_cols]
     meet()
     block = rows_at(chip, tok_rows)
     mine = rows_at(core, rows)
-    swaps = [
-        begin(remote(qkv_src.at[at, 1 - core], stage_q.at[at, mine], q_send.at[at], q_recv.at[at], twin()))
-        for at in range(CHIPS)
-    ]
-    keeps = [
-        begin(pltpu.make_async_copy(qkv_src.at[at, core], stage_q.at[at, mine], local_sem.at[at]))
-        for at in range(CHIPS)
-    ]
-    states_all[block, :] = states[...]
+    half_at = pl.ds(pl.multiple_of(3 * model_width + core * half_width, 128), half_width)
+    other_at = pl.ds(pl.multiple_of(3 * model_width + (1 - core) * half_width, 128), half_width)
+    swap_o = begin(remote(attn_src.at[:, other_at], stage_o.at[mine], q_send.at[1], q_recv.at[1], twin()))
+    swap_q = begin(remote(src_q.at[:, 1 - core], stage_q.at[:, mine], q_send.at[0], q_recv.at[0], twin()))
+    stage_o[mine, :] = attn_src[:, half_at]
+    stage_q[:, mine, :] = src_q[:, core]
     m_swaps, m_keeps = [], []
     for part in range(3):
         for at in range(CHIPS):
@@ -525,37 +542,41 @@
             ours = pl.ds(pl.multiple_of(start + core * half_units, 128), half_units)
             there = stage_m.at[part, at, mine]
             m_swaps.append(begin(remote(mlp_src.at[:, theirs], there, mt_send.at[part, at], mt_recv.at[part, at], twin())))
-            m_keeps.append(begin(pltpu.make_async_copy(mlp_src.at[:, ours], there, local_sem.at[CHIPS + part * CHIPS + at])))
-    for copy in keeps:
-        copy.wait()
-    for copy in swaps:
-        copy.wait()
-    low_q[...] = stage_q[...].astype(jnp.bfloat16)
+            m_keeps.append(begin(pltpu.make_async_copy(mlp_src.at[:, ours], there, local_sem.at[part * CHIPS + at])))
     my_rows = rows_at(seq * CHIPS + chip, chip_rows)
+    seq_at = rows_at(seq, seq_rows)
+    swap_o.wait()
+    low_o[...] = stage_o[...].astype(low)
+    o_line = to_line(low_o, w_out.at[core, my_rows], oz_send, oz_recv)
+    w_out[core, my_rows, :] = low_o[...]
+    swap_q.wait()
+    low_q[...] = stage_q[...].astype(low)
     line = []
     for step in STEPS:
         device, other = chip_peer(step)
         line.append(begin(remote(low_q.at[other], w_qkv.at[core, my_rows], wz_send.at[step], wz_recv.at[step], device)))
     w_qkv[core, my_rows, :] = low_q[chip]
+    states_all[block, :] = states[...]
+    key_positions(places, key_pos, tok_rows)
+    for copy in line:
+        copy.wait_recv()
+    gather_start(states, states_all, tok_rows, x_send, x_recv)
+
+    def across(part, send, recv):
+        return [begin(remote(part, part, send.at[step], recv.at[step], seq_peer(step)[0])) for step in STEPS]
+
+    q_across = across(w_qkv.at[core, seq_at], ws_send, ws_recv)
     for copy in m_keeps:
         copy.wait()
     for copy in m_swaps:
         copy.wait()
-    low_m[...] = stage_m[:2].astype(jnp.bfloat16)
-    low_down[...] = stage_m[2].astype(jnp.bfloat16)
-    for copy in line:
-        copy.wait_recv()
-    gather_start(states, states_all, tok_rows, x_send, x_recv)
-    seq_at = rows_at(seq, seq_rows)
-    seq_part = w_qkv.at[core, seq_at]
-    across = [
-        begin(remote(seq_part, seq_part, ws_send.at[step], ws_recv.at[step], seq_peer(step)[0]))
-        for step in STEPS
-    ]
+    low_m[...] = stage_m[:2].astype(low)
+    low_down[...] = stage_m[2].astype(low)
     gather_hop(states_all, tok_rows, 1, x_send, x_recv)
-    for copy in across:
+    for copy in o_line + q_across:
         copy.wait_recv()
     swap = begin(remote(w_qkv.at[core], w_qkv.at[core], wt_send.at[0], wt_recv.at[0], twin()))
+    o_across = across(w_out.at[core, seq_at], os_send, os_recv)
     gather_hop(states_all, tok_rows, 2, x_send, x_recv)
     gather_hop(states_all, tok_rows, 3, x_send, x_recv)
     here = rows_at(chip, chip_rows)
@@ -566,7 +587,6 @@
             for step in STEPS
         ]
 
-    mine_up = w_up.at[seq_at]
     m_line = to_chips(0, w_up.at[my_rows])
     w_up[my_rows, :] = low_m[0, chip]
     w_gate[here, :] = low_m[1, chip]
@@ -577,72 +597,78 @@
         for which in range(3):
             start = which * head_cols + half * part_cols
             raw[:, start : start + part_cols] = value[:, which * part_cols : (which + 1) * part_cols]
-    for head in range(heads):
-        gain = qk_gain[head]
-        for which in range(2):
-            start = which * head_cols + head * HEAD_DIM
-            value = raw[:, start : start + HEAD_DIM]
-            factor = lax.rsqrt(jnp.sum(value * value, axis=-1, keepdims=True) + EPSILON)
-            low = (value * factor * gain).astype(jnp.bfloat16)
-            raw_out[which, head] = value
-            if which == 0:
-                query_out[head] = low * math.sqrt(HEAD_DIM)
-            else:
-                both[core, 0, head] = low
-        start = 2 * head_cols + head * HEAD_DIM
-        both[core, 1, head] = raw[:, start : start + HEAD_DIM].astype(jnp.bfloat16)
-    swap = begin(remote(both.at[core], both.at[core], kv_send.at[0], kv_recv.at[0], twin()))
-    for copy in m_line:
+    for head in reversed(range(3 * heads)):
+        which, head = head // heads, head % heads
+        start = which * head_cols + head * HEAD_DIM
+        value = raw[:, start : start + HEAD_DIM]
+        if which == 2:
+            both[core, 1, head] = value.astype(low)
+            continue
+        factor = lax.rsqrt(jnp.sum(value * value, axis=-1, keepdims=True) + EPSILON)
+        scaled = (value * factor * qk_gain[head]).astype(low)
+        raw_out[which, head] = value
+        if which == 1:
+            both[core, 0, head] = scaled
+            if head == 0:
+                swap = begin(remote(both.at[core], both.at[core], kv_send.at[0], kv_recv.at[0], twin()))
+        else:
+            query_out[head] = scaled * math.sqrt(HEAD_DIM)
+    for copy in m_line + o_across:
         copy.wait_recv()
     m_line += to_chips(1, w_gate.at[here])
-    up_across = [
-        begin(remote(mine_up, mine_up, ms_send.at[step], ms_recv.at[step], seq_peer(step)[0]))
-        for step in STEPS
-    ]
+    swap_o = begin(remote(w_out.at[core], w_out.at[core], wt_send.at[1], wt_recv.at[1], twin()))
+    up_across = across(w_up.at[seq_at], ms_send, ms_recv)
     swap.wait()
 
-    tile = min(128, group_rows)
-    tiles = group_rows // tile
-
-    def one_tile(index, carry):
-        head = index // tiles
-        at = rows_at(lax.rem(index, tiles), tile)
-        query = query_out[head, at, :]
-        allowed = key_pos[...] <= query_pos[at, :]
-        scores = jnp.concatenate([dot_nt(query, both[half, 0, head]) for half in range(CORES)], axis=1)
-        powered = jnp.exp(jnp.where(allowed, scores, NEG_LARGE))
-        inverse = 1.0 / jnp.sum(powered, axis=-1, keepdims=True)
-        weights = (powered * inverse).astype(jnp.bfloat16)
-        att_out[head, at, :] = sum(
-            dot(weights[:, half * group_rows : (half + 1) * group_rows], both[half, 1, head])
-            for half in range(CORES)
-        )
-        inv_out[head, at, :] = inverse
+    def one_block(index, carry):
+        step = lax.rem(index + 1, CHIPS)
+        device, other = chip_peer(step)
+        at = rows_at(other, tok_rows)
+        allowed = kept_pairs(places, key_pos, other, core, tok_rows)
+
+        def one_head(head, carry):
+            query = query_out[head, at, :]
+            scores = jnp.concatenate([dot_nt(query, both[half, 0, head]) for half in range(CORES)], axis=1)
+            powered = jnp.exp(jnp.where(allowed, scores, NEG_LARGE))
+            inverse = 1.0 / jnp.sum(powered, axis=-1, keepdims=True)
+            weights = (powered * inverse).astype(low)
+            att_out[head, at, :] = sum(
+                dot(weights[:, half * group_rows : (half + 1) * group_rows], both[half, 1, head])
+                for half in range(CORES)
+            )
+            inv_out[head, at, :] = inverse
+            return carry
+
+        lax.fori_loop(0, heads, one_head, 0)
+        for head in range(heads):
+            att_low[at, head * HEAD_DIM : (head + 1) * HEAD_DIM] = att_out[head, at, :].astype(low)
+        when(step != 0, remote(att_low.at[at], attx.at[chip], a_send.at[step], a_recv.at[step], device).start)
         return carry
 
-    lax.fori_loop(0, heads * tiles, one_tile, 0)
-    for head in range(heads):
-        att_low[:, head * HEAD_DIM : (head + 1) * HEAD_DIM] = att_out[head].astype(jnp.bfloat16)
-    out = []
+    lax.fori_loop(0, CHIPS, one_block, 0)
+    attx[chip] = att_low[block, :]
     for step in STEPS:
-        device, other = chip_peer(step)
-        out.append(begin(remote(att_low.at[rows_at(other, tok_rows)], attx.at[chip], a_send.at[step], a_recv.at[step], device)))
-    attx[chip] = att_low[block, :]
-    for copy in m_line[3:]:
+        remote(att_low.at[block], attx.at[chip], a_send.at[step], a_recv.at[step], chip_peer(step)[0]).wait()
+    for copy in m_line[3:] + up_across:
         copy.wait_recv()
-    for copy in out + up_across:
-        copy.wait()
+    swap_o.wait()
     gather_drain(states_all, tok_rows, x_send, x_recv)
-    for copy in m_line + line + across:
+    for copy in m_line + line + o_line + q_across + o_across + up_across:
         copy.wait_send()
 
 
-def attend_call(states, qkv_src, mlp_src, qk_gain, query_pos, key_pos):
+def in_smem():
+    return pl.BlockSpec(memory_space=pltpu.SMEM)
+
+
+def attend_call(states, attn_src, mlp_src, qk_gain, places):
     tok_rows, model_width = states.shape
-    chips, _, rows, half_cols = qkv_src.shape
+    rows = attn_src.shape[0]
     heads = qk_gain.shape[0]
+    chips, chip_rows = CHIPS, CORES * rows
     group_rows = chips * tok_rows
     half_units = mlp_src.shape[1] // 3 // chips // CORES
+    half_width, half_cols = model_width // CORES, 3 * heads * HEAD_DIM // CORES
     f32, low = jnp.float32, jnp.bfloat16
     shape = jax.ShapeDtypeStruct
     return pl.pallas_call(
@@ -650,9 +676,10 @@
         out_shape=[
             shape((group_rows, model_width), low),
             shape((CORES, model_width, half_cols), low),
+            shape((CORES, model_width, half_width), low),
             shape((model_width, half_units), low),
-            shape((chips * CORES * rows, half_units), low),
-            shape((chips, CORES * rows, half_units), low),
+            shape((chips * chip_rows, half_units), low),
+            shape((chips, chip_rows, half_units), low),
             shape((2, heads, group_rows, HEAD_DIM), f32),
             shape((heads, group_rows, HEAD_DIM), low),
             shape((CORES, 2, heads, group_rows, HEAD_DIM), low),
@@ -660,23 +687,28 @@
             shape((heads, group_rows, 1), f32),
             shape((chips, tok_rows, heads * HEAD_DIM), low),
         ],
-        in_specs=[in_vmem(), in_hbm(), in_hbm(), in_vmem(), in_vmem(), in_vmem()],
-        out_specs=[in_vmem()] * 11,
+        in_specs=[in_vmem(), in_vmem(), in_hbm(), in_vmem(), in_smem()],
+        out_specs=[in_vmem()] * 12,
         scratch_shapes=[
-            VMEM((chips, CORES * rows, half_cols), f32),
-            VMEM((chips, CORES * rows, half_cols), low),
-            VMEM((3, chips, CORES * rows, half_units), f32),
-            VMEM((2, chips, CORES * rows, half_units), low),
+            VMEM((chips, CORES, rows, half_cols), f32),
+            VMEM((chips, chip_rows, half_cols), f32),
+            VMEM((chips, chip_rows, half_cols), low),
+            VMEM((chip_rows, half_width), f32),
+            VMEM((chip_rows, half_width), low),
+            VMEM((3, chips, chip_rows, half_units), f32),
+            VMEM((2, chips, chip_rows, half_units), low),
             VMEM((group_rows, 3 * heads * HEAD_DIM), f32),
             VMEM((group_rows, heads * HEAD_DIM), low),
-            dma(16), line_dma(), line_dma(), dma(4), dma(4), dma(3, 4), dma(3, 4), dma(4), dma(4),
-            dma(4), dma(4), dma(1), dma(1), dma(2, 4), dma(2, 4), dma(4), dma(4), dma(1), dma(1), dma(4), dma(4),
+            VMEM((1, CORES * group_rows), jnp.int32),
+            dma(12), line_dma(), line_dma(), dma(2), dma(2), dma(3, 4), dma(3, 4), dma(4), dma(4),
+            dma(4), dma(4), dma(2), dma(2), dma(4), dma(4), dma(4), dma(4), dma(2, 4), dma(2, 4),
+            dma(4), dma(4), dma(1), dma(1), dma(4), dma(4),
         ],
         compiler_params=pltpu.CompilerParams(
             collective_id=1, has_side_effects=True, vmem_limit_bytes=LIMIT
         ),
         name="attend",
-    )(states, qkv_src, mlp_src, qk_gain, query_pos, key_pos)
+    )(states, attn_src, mlp_src, qk_gain, places)
 
 
 def unit_of(value):
@@ -686,10 +718,10 @@
 
 def mlp_kernel(
     attx, states, cotangent, w_out, alpha_attn, alpha_mlp, gain_u, gain_v, w_up, w_gate, low_down,
-    out, grad_attx, grad_w_out, grad_direct, dot_a, dot_m, dot_u, dot_v, grad_half, grad_down,
+    out, grad_attx, grad_w_out, grad_direct, small, grad_half, grad_down,
     weights, mixed_one, attn_unit, factors, mixed_low, mixed_all, up, gate, hidden, part,
     sums, via, passed, total, grad_two, branch_low, branch_all, grad_u, grad_v, wide, turned, arrived,
-    w_down, down_half, down_got,
+    w_down, down_half, down_got, dot_u, dot_v,
     local_sem, ws_send, ws_recv, wt_send, wt_recv, x_send, x_recv, r_send, r_recv,
     g_send, g_recv, b_send, b_recv, d_send, d_recv, wz_send, wz_recv, ds_send, ds_recv,
 ):
@@ -698,6 +730,7 @@
     chip_heads = attx.shape[2]
     seq_rows, half_units = w_gate.shape
     chip_rows = low_down.shape[1]
+    half_width = w_out.shape[2]
     group_rows = CHIPS * tok_rows
     block = rows_at(chip, tok_rows)
     meet()
@@ -721,7 +754,12 @@
         begin(pltpu.make_async_copy(w_gate, weights.at[1, core, seq_at], local_sem.at[1])),
     ]
     w_down[here, :] = low_down[chip]
-    branch = sum(dot(attx[at], w_out[at]) for at in range(CHIPS))
+    part_at = [slice(at * chip_heads, (at + 1) * chip_heads) for at in range(CHIPS)]
+    half_at = [slice(half * half_width, (half + 1) * half_width) for half in range(CORES)]
+    branch = jnp.concatenate(
+        [sum(dot(attx[at], w_out[half, part_at[at], :]) for at in range(CHIPS)) for half in range(CORES)],
+        axis=1,
+    )
     unit, factor = unit_of(branch)
     attn_unit[...] = unit
     factors[0] = factor
@@ -784,7 +822,8 @@
     above = cotangent[...].astype(jnp.float32)
     grad = factor * (above - value * jnp.sum(above * value, axis=-1, keepdims=True))
     grad_two[...] = grad
-    dot_m[...] = jnp.sum(grad * (mlp_unit - mixed_one[...]), axis=0, keepdims=True)
+    small[...] = jnp.zeros_like(small)
+    small[1:2, :] = jnp.sum(grad * (mlp_unit - mixed_one[...]), axis=0, keepdims=True)
     grad = grad * alpha_mlp[...]
     grad = mlp_factor * (grad - mlp_unit * jnp.sum(grad * mlp_unit, axis=-1, keepdims=True))
     branch_low[...] = grad.astype(jnp.bfloat16)
@@ -859,14 +898,21 @@
     value = mixed_one[...]
     grad = factors[1] * (grad - value * jnp.sum(grad * value, axis=-1, keepdims=True))
     unit = attn_unit[...]
-    dot_a[...] = jnp.sum(grad * (unit - states[...].astype(jnp.float32)), axis=0, keepdims=True)
+    small[0:1, :] = jnp.sum(grad * (unit - states[...].astype(jnp.float32)), axis=0, keepdims=True)
     grad_direct[...] = grad * (1.0 - alpha_attn[...])
     grad = grad * alpha_attn[...]
     grad = factors[0] * (grad - unit * jnp.sum(grad * unit, axis=-1, keepdims=True))
     low = grad.astype(jnp.bfloat16)
     for at in range(CHIPS):
-        grad_attx[at] = dot_nt(low, w_out[at]).astype(jnp.bfloat16)
-        grad_w_out[at] = dot_tn(attx[at], low).astype(jnp.bfloat16)
+        grad_attx[at] = sum(
+            dot_nt(low[:, half_at[half]], w_out[half, part_at[at], :]) for half in range(CORES)
+        ).astype(jnp.bfloat16)
+        for half in range(CORES):
+            grad_w_out[half, at] = dot_tn(attx[at], low[:, half_at[half]]).astype(jnp.bfloat16)
+    for half in range(CORES):
+        unit_at = slice(half * half_units, (half + 1) * half_units)
+        small[2:3, unit_at] = dot_u[half]
+        small[3:4, unit_at] = dot_v[half] * math.sqrt(D)
     for which in range(2):
         grad_half[which] = both_cores(which)
     whole = down_half[seq_at, :].astype(jnp.float32)
@@ -897,17 +943,14 @@
         out_shape=[
             shape(tokens, low),
             shape(attx.shape, low),
-            shape((chips, chip_heads, model_width), low),
+            shape((CORES, chips, chip_heads, model_width // CORES), low),
             shape(tokens, f32),
-            shape((1, model_width), f32),
-            shape((1, model_width), f32),
-            shape((CORES, 1, half_units), f32),
-            shape((CORES, 1, half_units), f32),
+            shape((8, max(model_width, CORES * half_units)), f32),
             shape((2,) + matrix, low),
             shape((seq_rows, half_units), low),
         ],
         in_specs=[in_vmem()] * 8 + [in_hbm(), in_vmem(), in_vmem()],
-        out_specs=[in_vmem()] * 10,
+        out_specs=[in_vmem()] * 7,
         scratch_shapes=[
             VMEM((3, CORES) + matrix, low),
             VMEM(tokens, f32),
@@ -934,6 +977,8 @@
             VMEM((seq_rows, half_units), low),
             VMEM(matrix, low),
             VMEM((3, seq_rows, half_units), low),
+            VMEM((CORES, 1, half_units), f32),
+            VMEM((CORES, 1, half_units), f32),
             dma(2), dma(3, 4), dma(3, 4), dma(3), dma(3), line_dma(), line_dma(), dma(4), dma(4),
             line_dma(), line_dma(), dma(4), dma(4), dma(3), dma(3), dma(4), dma(4), dma(4), dma(4),
         ],
@@ -948,11 +993,11 @@
 
 def back_kernel(
     grad_attx, grad_half, grad_down, grad_w_out, small_in, raw, query, both, att, inverse, states_all,
-    w_qkv, qk_gain, query_pos, key_pos, grad_direct,
-    grad_states, out_mlp, out_qkv, out_proj, small_out,
+    w_qkv, qk_gain, places, grad_direct,
+    grad_states, out_mlp, out_attn, feature, unit,
     att_low, heads_low, to_keys, swap_low, swap_kv, grad_heads, grad_sides, part, sums, via, passed, total, turned,
     grad_q, half_q, seq_q, line_q, wide_q, half_o, pair_o, seq_got, seq_low, line_got, wide,
-    wide_o, small, small_pair, small_seq, dots,
+    wide_o, small, small_pair, small_seq, dots, small_all, flat_q, sides_q, key_pos,
     local_sem, a_send, a_recv, s_send, s_recv, o_send, o_recv, kv_send, kv_recv, r_send, r_recv,
     qt_send, qt_recv, qs_send, qs_recv, qz_send, qz_recv, z_send, z_recv, f_send, f_recv,
     p_send, p_recv, t_send, t_recv,
@@ -978,9 +1023,8 @@
         device, other = chip_peer(step)
         line.append(begin(remote(grad_attx.at[other], att_low.at[block], a_send.at[step], a_recv.at[step], device)))
     att_low[block, :] = grad_attx[chip]
-    half_at = pl.ds(pl.multiple_of(core * half_units, 128), half_units)
-    other_at = pl.ds(pl.multiple_of((1 - core) * half_units, 128), half_units)
-    pair = begin(remote(grad_w_out.at[:, :, other_at], pair_o, o_send.at[0], o_recv.at[0], twin()))
+    key_positions(places, key_pos, tok_rows)
+    pair = begin(remote(grad_w_out.at[1 - core], pair_o, o_send.at[0], o_recv.at[0], twin()))
     across = []
     onward = {}
 
@@ -1005,17 +1049,12 @@
     turned[...] = states_all[...].T
     pair.wait_recv()
     for at in range(4):
-        half_o[at] = (grad_w_out[at, :, half_at].astype(f32) + pair_o[at].astype(f32)).astype(low)
+        half_o[at] = (grad_w_out[core, at].astype(f32) + pair_o[at].astype(f32)).astype(low)
     for step in STEPS:
         device, other = seq_peer(step)
         across.append(begin(remote(half_o.at[other], seq_got.at[2, step - 1], s_send.at[2, step], s_recv.at[2, step], device)))
-    for copy in line:
-        copy.wait_recv()
-    for head in range(heads):
-        heads_low[head] = att_low[:, head * HEAD_DIM : (head + 1) * HEAD_DIM]
-
-    tile = min(128, group_rows)
-    tiles = group_rows // tile
+    tile = tok_rows
+    tiles = CHIPS
 
     def raw_back(which, head, at, upstream):
         value = raw[which, head, at, :]
@@ -1025,28 +1064,37 @@
         upstream = factor * (upstream - unit * jnp.sum(upstream * unit, axis=-1, keepdims=True))
         grad_heads[which, head, at, :] = upstream.astype(low)
 
-    def one_tile(index, carry):
-        head = index // tiles
-        at = rows_at(lax.rem(index, tiles), tile)
-        rows_q = query[head, at, :]
-        grad_att = heads_low[head, at, :]
-        allowed = key_pos[...] <= query_pos[at, :]
-        scores = jnp.concatenate([dot_nt(rows_q, both[half, 0, head]) for half in range(CORES)], axis=1)
-        probs = jnp.exp(jnp.where(allowed, scores, NEG_LARGE)) * inverse[head, at, :]
-        grad_prob = jnp.concatenate([dot_nt(grad_att, both[half, 1, head]) for half in range(CORES)], axis=1)
-        row_dot = jnp.sum(grad_att.astype(f32) * att[head, at, :], axis=-1, keepdims=True)
-        grad_scores = (probs * (grad_prob - row_dot)).astype(low)
-        weights = probs.astype(low)
-        total = jnp.zeros((tile, HEAD_DIM), f32)
-        for half in range(CORES):
-            cols = slice(half * group_rows, (half + 1) * group_rows)
-            total = total + dot(grad_scores[:, cols], both[half, 0, head])
-            to_keys[half, 0, head] += dot_tn(grad_scores[:, cols], rows_q)
-            to_keys[half, 1, head] += dot_tn(weights[:, cols], grad_att)
-        raw_back(0, head, at, total * scale)
+    def one_block(step, carry):
+        other = lax.rem(chip + CHIPS - step, CHIPS)
+        at = rows_at(other, tok_rows)
+        copy = remote(grad_attx.at[0], att_low.at[at], a_send.at[step], a_recv.at[step], device_on(other))
+        when(step > 0, copy.wait_recv)
+        for head in range(heads):
+            heads_low[head, at, :] = att_low[at, head * HEAD_DIM : (head + 1) * HEAD_DIM]
+        allowed = kept_pairs(places, key_pos, other, core, tok_rows)
+
+        def one_head(head, carry):
+            rows_q = query[head, at, :]
+            grad_att = heads_low[head, at, :]
+            scores = jnp.concatenate([dot_nt(rows_q, both[half, 0, head]) for half in range(CORES)], axis=1)
+            probs = jnp.exp(jnp.where(allowed, scores, NEG_LARGE)) * inverse[head, at, :]
+            grad_prob = jnp.concatenate([dot_nt(grad_att, both[half, 1, head]) for half in range(CORES)], axis=1)
+            row_dot = jnp.sum(grad_att.astype(f32) * att[head, at, :], axis=-1, keepdims=True)
+            grad_scores = (probs * (grad_prob - row_dot)).astype(low)
+            weights = probs.astype(low)
+            to_query = jnp.zeros((tok_rows, HEAD_DIM), f32)
+            for half in range(CORES):
+                cols = slice(half * group_rows, (half + 1) * group_rows)
+                to_query = to_query + dot(grad_scores[:, cols], both[half, 0, head])
+                to_keys[half, 0, head] += dot_tn(grad_scores[:, cols], rows_q)
+                to_keys[half, 1, head] += dot_tn(weights[:, cols], grad_att)
+            raw_back(0, head, at, to_query * scale)
+            return carry
+
+        lax.fori_loop(0, heads, one_head, 0)
         return carry
 
-    lax.fori_loop(0, heads * tiles, one_tile, 0)
+    lax.fori_loop(0, CHIPS, one_block, 0)
     swap_low[...] = to_keys[1 - core].astype(low)
     swap = begin(remote(swap_low, swap_kv, kv_send.at[0], kv_recv.at[0], twin()))
     swap.wait()
@@ -1124,8 +1172,8 @@
     for copy in spread_s:
         copy.wait()
     small_pair[...] = small[...] + small_seq[0] + small_seq[1] + small_seq[2]
-    small_out[chip] = small_pair[...]
-    ends = to_line(small_pair, small_out.at[chip], p_send, p_recv)
+    small_all[chip] = small_pair[...]
+    ends = to_line(small_pair, small_all.at[chip], p_send, p_recv)
     reduce_wait(part, tok_rows, sums, total, r_send, r_recv)
     grad_states[...] = (total[...] + grad_direct[...]).astype(low)
 
@@ -1147,16 +1195,31 @@
     for at in range(1, CHIPS):
         whole = whole + line_got[3, at].astype(f32)
     wide_o[...] = whole
-    there = out_proj.at[:, half_at]
+    start = 3 * model_width + core * half_units
+    there = out_attn.at[:, pl.ds(pl.multiple_of(start, 128), half_units)]
     last.append(begin(remote(wide_o.at[theirs], there, f_send.at[3, 0], f_recv.at[3, 0], twin())))
     lasts.append(begin(pltpu.make_async_copy(wide_o.at[mine], there, local_sem.at[15])))
     for copy in onward_q:
         copy.wait_recv()
     wide_q[...] = line_q[...].astype(f32)
-    there = out_qkv.at[core]
-    last.append(begin(remote(wide_q.at[:, theirs], there, f_send.at[3, 1], f_recv.at[3, 1], twin())))
-    lasts.append(begin(pltpu.make_async_copy(wide_q.at[:, mine], there, local_sem.at[16])))
-    for copy in ends + last + lasts:
+    sides_q[core] = wide_q[:, mine, :]
+    swap_q = begin(remote(wide_q.at[:, theirs], sides_q.at[core], f_send.at[3, 1], f_recv.at[3, 1], twin()))
+    for copy in ends:
+        copy.wait()
+    alphas = small_all[0] + small_all[1] + small_all[2] + small_all[3]
+    feature[1:3, :] = alphas[0:2, :]
+    for at in range(CHIPS):
+        feature[0:1, at * head_cols : (at + 1) * head_cols] = small_all[at, 4:5, :head_cols]
+        width = CORES * half_units
+        unit[:, at * width : (at + 1) * width] = small_all[at, 2:4, :width]
+    swap_q.wait()
+    for at in range(CHIPS):
+        for half in range(CORES):
+            for which in range(3):
+                start = which * model_width + at * head_cols + half * part_cols
+                flat_q[:, start : start + part_cols] = sides_q[half, at, :, which * part_cols : (which + 1) * part_cols]
+    lasts.append(begin(pltpu.make_async_copy(flat_q, out_attn.at[:, pl.ds(0, 3 * model_width)], local_sem.at[16])))
+    for copy in last + lasts:
         copy.wait()
     reduce_drain(part, tok_rows, sums, r_send, r_recv)
     for copy in line + [pair] + across + across_q + onward_q + sum(onward.values(), []):
@@ -1165,7 +1228,7 @@
 
 def back_call(
     grad_attx, grad_half, grad_down, grad_w_out, small_in, raw, query, both, att, inverse, states_all,
-    w_qkv, qk_gain, query_pos, key_pos, grad_direct, rows,
+    w_qkv, qk_gain, places, grad_direct, rows,
 ):
     tok_rows, model_width = grad_direct.shape
     chips = grad_attx.shape[0]
@@ -1184,12 +1247,12 @@
         out_shape=[
             shape((tok_rows, model_width), low),
             shape((rows, 3 * chips * CORES * half_units), f32),
-            shape((CORES, chips, rows, half_cols), f32),
-            shape((rows, CORES * half_units), f32),
-            shape((chips,) + small_in.shape, f32),
+            shape((rows, 4 * model_width), f32),
+            shape((3, model_width), f32),
+            shape((2, chips * CORES * half_units), f32),
         ],
-        in_specs=[in_vmem(), in_hbm()] + [in_vmem()] * 14,
-        out_specs=[in_vmem(), in_hbm(), in_hbm(), in_hbm(), in_vmem()],
+        in_specs=[in_vmem(), in_hbm()] + [in_vmem()] * 11 + [in_smem(), in_vmem()],
+        out_specs=[in_vmem(), in_hbm(), in_hbm(), in_vmem(), in_vmem()],
         scratch_shapes=[
             VMEM((group_rows, head_cols), low),
             VMEM(per_head, low),
@@ -1220,6 +1283,10 @@
             VMEM(small_in.shape, f32),
             VMEM((3,) + small_in.shape, f32),
             VMEM((heads, 1, HEAD_DIM), f32),
+            VMEM((chips,) + small_in.shape, f32),
+            VMEM((rows, 3 * model_width), f32),
+            VMEM((CORES, chips, rows, half_cols), f32),
+            VMEM((1, CORES * group_rows), jnp.int32),
             dma(17), dma(4), dma(4), dma(4, 4), dma(4, 4), dma(1), dma(1), dma(1), dma(1),
             dma(4), dma(4), dma(1), dma(1), dma(4), dma(4), dma(4), dma(4), dma(4, 4), dma(4, 4),
             dma(4, 4), dma(4, 4), dma(4), dma(4), dma(4), dma(4),
@@ -1230,7 +1297,7 @@
         name="back",
     )(
         grad_attx, grad_half, grad_down, grad_w_out, small_in, raw, query, both, att, inverse, states_all,
-        w_qkv, qk_gain, query_pos, key_pos, grad_direct,
+        w_qkv, qk_gain, places, grad_direct,
     )
 
 
@@ -1240,64 +1307,35 @@
     n_seq, n_ctx = lax.axis_size("seq"), lax.axis_size("ctx")
     chips = n_ctx // CORES
     chip = lax.axis_index("ctx") // CORES
-    core = lax.axis_index("ctx") % CORES
     heads = HEADS // chips
     head_cols = heads * HEAD_DIM
     units = ff_width // chips
-    group_rows = chips * tok_rows
     rows = attn_weights.shape[0]
-    qkv_src = attn_weights[:, : 3 * model_width].reshape(rows, 3, chips, CORES, head_cols // CORES)
-    qkv_src = qkv_src.transpose(2, 3, 0, 1, 4).reshape(chips, CORES, rows, -1)
-    w_out = lax.all_gather(
-        attn_weights[:, 3 * model_width :].astype(jnp.bfloat16), ALL, axis=0, tiled=True
-    )
     qk_gain = lax.dynamic_slice_in_dim(feature_gains[:, 0], chip * head_cols, head_cols)
     qk_gain = qk_gain.reshape(heads, 1, HEAD_DIM)
-    places = block_place[0].reshape(chips, CORES)
-    offsets = jnp.arange(tok_rows, dtype=jnp.int32)
-    own_places = jnp.sum(
-        jnp.where(jnp.arange(CORES, dtype=jnp.int32)[None, :] == core, places, 0), axis=1
-    )
-    query_pos = (own_places[:, None] * tok_rows + offsets).reshape(group_rows, 1)
-    key_pos = (places.T[:, :, None] * tok_rows + offsets).reshape(1, CORES * group_rows)
-    states_all, w_qkv, w_up, w_gate, low_down, raw, query, both, att, inverse, attx = attend_call(
-        states, qkv_src, mlp_weights, qk_gain, query_pos, key_pos
+    states_all, w_qkv, w_out, w_up, w_gate, low_down, raw, query, both, att, inverse, attx = attend_call(
+        states, attn_weights, mlp_weights, qk_gain, block_place
     )
     gain_u = lax.dynamic_slice_in_dim(unit_gains[:, 0], chip * units, units)
     gain_v = lax.dynamic_slice_in_dim(unit_gains[:, 1], chip * units, units) * math.sqrt(D)
-    (
-        out_low, grad_attx, grad_w_out, grad_direct, grad_alpha_a, grad_alpha_m, grad_s_u, grad_s_v, grad_half, grad_down
-    ) = mlp_call(
-        attx, states, cotangent, w_out.reshape(chips, head_cols, model_width),
-        feature_gains[:, 1].reshape(1, model_width), feature_gains[:, 2].reshape(1, model_width),
-        gain_u.reshape(CORES, 1, units // CORES), gain_v.reshape(CORES, 1, units // CORES), w_up, w_gate, low_down,
-    )
-    small = jnp.concatenate(
-        [
-            grad_alpha_a, grad_alpha_m, grad_s_u.reshape(1, units),
-            grad_s_v.reshape(1, units) * math.sqrt(D), jnp.zeros((4, units), jnp.float32),
-        ]
-    )
-    grad_states, grad_mlp, grad_qkv, grad_proj, small = back_call(
+    out_low, grad_attx, grad_w_out, grad_direct, small, grad_half, grad_down = mlp_call(
+        attx, states, cotangent, w_out, feature_gains[:, 1].reshape(1, model_width),
+        feature_gains[:, 2].reshape(1, model_width), gain_u.reshape(CORES, 1, units // CORES),
+        gain_v.reshape(CORES, 1, units // CORES), w_up, w_gate, low_down,
+    )
+    grad_states, grad_mlp, grad_attn, feature, unit = back_call(
         grad_attx, grad_half, grad_down, grad_w_out, small, raw, query, both, att, inverse, states_all,
-        w_qkv, qk_gain, query_pos, key_pos, grad_direct, rows,
-    )
-    grad_qkv = grad_qkv.reshape(CORES, chips, rows, 3, head_cols // CORES)
-    grad_qkv = grad_qkv.transpose(2, 3, 1, 0, 4).reshape(rows, 3 * model_width)
-    feature = jnp.stack(
-        [small[:, 4, :head_cols].reshape(-1), jnp.sum(small[:, 0], axis=0), jnp.sum(small[:, 1], axis=0)],
-        axis=1,
-    )
-    unit = jnp.stack([small[:, 2].reshape(-1), small[:, 3].reshape(-1)], axis=1)
+        w_qkv, qk_gain, block_place, grad_direct, rows,
+    )
     rank = lax.axis_index(ALL)
     unit_rows_own = ff_width // (n_seq * n_ctx)
     return (
         out_low,
         grad_states,
-        jnp.concatenate([grad_qkv, grad_proj], axis=1),
+        grad_attn,
         grad_mlp,
-        lax.dynamic_slice_in_dim(feature, rank * rows, rows),
-        lax.dynamic_slice_in_dim(unit, rank * unit_rows_own, unit_rows_own),
+        lax.dynamic_slice_in_dim(feature, rank * rows, rows, axis=1).T,
+        lax.dynamic_slice_in_dim(unit, rank * unit_rows_own, unit_rows_own, axis=1).T,
     )
 
 

time: 385 us -> 347 us (0.901)
  between operations: 14.2 us -> 0.71 us
  Pallas kernels: 343 us -> 333 us
  local copies, waits for them, and re-layouts: 19.2 us -> 11.9 us
  other arithmetic: 6.99 us -> 0.61 us
    reshape x5 -> x0, local copies, waits for them, and re-layouts: 6.73 us -> none  [the longest x2 1.97 us: shards_split(): attn_weights[:, :3 * model_width]]
    pallas_call x1, Pallas kernels: 93.4 us -> 86.7 us  [attend_call(): pl.pallas_call(attend_kernel, out_shape=[shape((group_rows, model_width),...]
  transfers between devices with their start and end apart: 1 -> 0, of which waited for: 0 -> 0; matrix products, arithmetic and copies ran while one was open for 3% -> 0% of each run, Pallas kernels for 24% -> 0%
where the time goes in v5:
time: 347 us; the launch traced here: 346 us
  Pallas kernels  333 us (96%)
  local copies, waits for them, and re-layouts  11.9 us (3%)
    pallas_call x1, Pallas kernels, mlp_call(): pl.pallas_call(mlp_kernel, out_shape=[shape(tokens, low), shape(attx.shap...  142 us
    pallas_call x1, Pallas kernels, back_call(): pl.pallas_call(back_kernel, out_shape=[shape((tok_rows, model_width), low...  104 us
    pallas_call x1, Pallas kernels, attend_call(): pl.pallas_call(attend_kernel, out_shape=[shape((group_rows, model_width),...  86.7 us

profile of v5, /device:TPU:0, one launch (start us, length us, event | category | flops | bytes accessed | tf_op | source)
XLA Modules:
  0.0 346.2 jit_solution(3068756464870437877)
XLA Ops:
  0.7 1.4 slice_bitcast_fusion
  2.1 0.1 dynamic-slice_reduce_fusion
  2.2 0.7 reshape.36.qk_gain
  2.9 0.9 fusion
  3.8 0.6 dynamic-slice_multiply_fusion
  4.4 86.7 %attend.1 = (bf16[512,1280]{1,0:T(8,128)(2,1)}, bf16[2,1280,480]{2,1,0:T(8,128)(2,1)}, bf16[2,1280,640]{2,1,0:T(8,128)(2,1)}, bf16[1280,640]{1,0:T(8,128)(2,1)},...) custom-call(bf16[128,1280]{1,0:T(8,128)(2,1)} %states.3, ...), custom_call_target="tpu_custom_call" | custom-call | tf_op jit(solution)/shard_map/attend/pallas_call | solution.py:674
  91.1 142.4 %mlp.1 = (bf16[128,1280]{1,0:T(8,128)(2,1)}, bf16[4,128,320]{2,1,0:T(8,128)(2,1)}, bf16[2,4,320,640]{3,2,1,0:T(8,128)(2,1)}, f32[128,1280]{1,0:T(8,128)}, f32[8,...) custom-call(bf16[4,128,320]{2,1,0:T(8,128)(2,1)} %get-tuple-element.30.attx, ...), custom_call_target="tpu_custom_call" | custom-call | tf_op jit(solution)/shard_map/mlp/pallas_call | solution.py:941
  233.5 0.0 copy-start.1
  233.5 103.8 %back.1 = (bf16[128,1280]{1,0:T(8,128)(2,1)}, f32[40,15360]{1,0:T(8,128)}, f32[40,5120]{1,0:T(8,128)}, f32[3,1280]{1,0:T(4,128)}, f32[2,5120]{1,0:T(2,128)}) custom-call(bf16[4,128,320]{2,1,0:T(8,128)(2,1)} %get-tuple-element.36.grad_attx, bf16[2,1280,640]{2,1,0:T(8,128)(2,1)} %get-tuple-element.37.grad_half, bf16[320,640]{1,0:T(8,128)(2,1)} %get-tuple-element.38.grad_down, ...), custom_call_target="tpu_custom_call" | custom-call | tf_op jit(solution)/shard_map/back/pallas_call | solution.py:1245
  337.4 0.0 copy-start
  337.4 1.5 dynamic-slice_bitcast_fusion.1
  338.9 1.3 dynamic-slice_bitcast_fusion
  340.2 0.0 copy-done.1
  340.2 0.7 copy.17
  340.9 1.7 copy.18
  342.6 2.1 copy.19
  344.7 0.0 copy-done
  344.7 1.4 copy.20
Async XLA Ops:
  233.5 106.7 %copy-start.1 = (bf16[128,1280]{1,0:T(8,128)(2,1)S(1)}, bf16[128,1280]{1,0:T(8,128)(2,1)}, u32[]{:S(2)}) copy-start(bf16[128,1280]{1,0:T(8,128)(2,1)} %get-tuple-element.67) | copy-start | bytes 983044
  337.4 7.3 %copy-start = (f32[40,15360]{1,0:T(8,128)S(1)}, f32[40,15360]{1,0:T(8,128)}, u32[]{:S(2)}) copy-start(f32[40,15360]{1,0:T(8,128)} %get-tuple-element.70) | copy-start | bytes 7372804

commit v6 on v5

--- a/solution.py
+++ b/solution.py
@@ -448,6 +448,68 @@
         when(jnp.logical_not(spans_line(other)), copy.wait_send)
 
 
+def side_peer(side):
+    return seq_peer(side + 1)
+
+
+def seq_rows_at(block, side, count):
+    half = count // 2
+    return pl.ds(pl.multiple_of(block * count + side * half, half), half)
+
+
+def spread_start(src, dst, count, send, recv):
+    seq = place_of()[0]
+    return [
+        begin(remote(src, dst.at[rows_at(seq, count)], send.at[side], recv.at[side], side_peer(side)[0]))
+        for side in range(2)
+    ]
+
+
+def spread_relay(dst, count, send, recv):
+    copies = []
+    for side in range(2):
+        block = side_peer(side)[1]
+        whole = dst.at[rows_at(block, count)]
+        remote(whole, whole, send.at[side], recv.at[side], side_peer(side)[0]).wait_recv()
+        part = dst.at[seq_rows_at(block, side, count)]
+        copies.append(begin(remote(part, part, send.at[2 + side], recv.at[2 + side], side_peer(1 - side)[0])))
+    return copies
+
+
+def fold_start(src, got, count, send, recv):
+    seq = place_of()[0]
+    copies = []
+    for side in range(2):
+        device, other = side_peer(side)
+        for at, block in enumerate((other, seq ^ 3)):
+            here = src.at[seq_rows_at(block, side, count)]
+            copies.append(begin(remote(here, got.at[side, at], send.at[side, at], recv.at[side, at], device)))
+    return copies
+
+
+def fold_relay(src, got, held, last, count, copies, send, recv):
+    more = []
+    for side in range(2):
+        device, other = side_peer(1 - side)
+        copies[2 * side + 1].wait_recv()
+        rows = seq_rows_at(other, side, count)
+        held[side] = (src[rows, :].astype(jnp.float32) + got[side, 1].astype(jnp.float32)).astype(held.dtype)
+        more.append(begin(remote(held.at[side], last.at[side], send.at[2, side], recv.at[2, side], device)))
+    return more
+
+
+def fold_end(src, got, last, out, count, copies, more):
+    seq = place_of()[0]
+    half = count // 2
+    for side in range(2):
+        copies[2 * side].wait_recv()
+        more[side].wait_recv()
+        rows = seq_rows_at(seq, side, count)
+        out[side * half : (side + 1) * half, :] = (
+            src[rows, :].astype(jnp.float32) + got[side, 0].astype(jnp.float32) + last[side].astype(jnp.float32)
+        ).astype(out.dtype)
+
+
 def to_line(src, there, send, recv):
     return [
         begin(remote(src, there, send.at[step], recv.at[step], chip_peer(step)[0])) for step in STEPS
@@ -501,9 +563,9 @@
 
 def attend_kernel(
     states, attn_src, mlp_src, qk_gain, places,
-    states_all, w_qkv, w_out, w_up, w_gate, low_down, raw_out, query_out, both, att_out, inv_out, attx,
-    src_q, stage_q, low_q, stage_o, low_o, stage_m, low_m, raw, att_low, key_pos,
-    local_sem, x_send, x_recv, q_send, q_recv, mt_send, mt_recv, wz_send, wz_recv,
+    to_states, to_qkv, to_out, w_up, w_gate, low_down, to_raw, to_query, to_both, to_att, to_inv, attx,
+    states_all, w_qkv, w_out, raw_out, query_out, both, att_out, inv_out, src_q, stage_q, low_q, stage_o, low_o, stage_m, low_m, raw, att_low, key_pos,
+    local_sem, keep_sem, att_sem, x_send, x_recv, q_send, q_recv, mt_send, mt_recv, wz_send, wz_recv,
     ws_send, ws_recv, wt_send, wt_recv, oz_send, oz_recv, os_send, os_recv, m_send, m_recv,
     ms_send, ms_recv, kv_send, kv_recv, a_send, a_recv,
 ):
@@ -562,10 +624,10 @@
         copy.wait_recv()
     gather_start(states, states_all, tok_rows, x_send, x_recv)
 
-    def across(part, send, recv):
-        return [begin(remote(part, part, send.at[step], recv.at[step], seq_peer(step)[0])) for step in STEPS]
-
-    q_across = across(w_qkv.at[core, seq_at], ws_send, ws_recv)
+    def across(whole, send, recv):
+        return spread_start(whole.at[seq_at], whole, seq_rows, send, recv)
+
+    q_across = across(w_qkv.at[core], ws_send, ws_recv)
     for copy in m_keeps:
         copy.wait()
     for copy in m_swaps:
@@ -573,11 +635,16 @@
     low_m[...] = stage_m[:2].astype(low)
     low_down[...] = stage_m[2].astype(low)
     gather_hop(states_all, tok_rows, 1, x_send, x_recv)
-    for copy in o_line + q_across:
+    more = spread_relay(w_qkv.at[core], seq_rows, ws_send, ws_recv)
+    for copy in o_line:
         copy.wait_recv()
+    o_across = across(w_out.at[core], os_send, os_recv)
+    for copy in more:
+        copy.wait_recv()
+    q_across += more
     swap = begin(remote(w_qkv.at[core], w_qkv.at[core], wt_send.at[0], wt_recv.at[0], twin()))
-    o_across = across(w_out.at[core, seq_at], os_send, os_recv)
     gather_hop(states_all, tok_rows, 2, x_send, x_recv)
+    o_more = spread_relay(w_out.at[core], seq_rows, os_send, os_recv)
     gather_hop(states_all, tok_rows, 3, x_send, x_recv)
     here = rows_at(chip, chip_rows)
 
@@ -591,7 +658,13 @@
     w_up[my_rows, :] = low_m[0, chip]
     w_gate[here, :] = low_m[1, chip]
     swap.wait()
-
+    kept = []
+
+    def keep(src, dst):
+        kept.append(begin(pltpu.make_async_copy(src, dst, keep_sem.at[len(kept)])))
+
+    keep(states_all, to_states)
+    keep(w_qkv, to_qkv)
     for half in range(CORES):
         value = dot(states_all[...], w_qkv[half])
         for which in range(3):
@@ -613,12 +686,15 @@
                 swap = begin(remote(both.at[core], both.at[core], kv_send.at[0], kv_recv.at[0], twin()))
         else:
             query_out[head] = scaled * math.sqrt(HEAD_DIM)
-    for copy in m_line + o_across:
+    keep(raw_out, to_raw)
+    keep(query_out, to_query)
+    for copy in m_line + o_more:
         copy.wait_recv()
     m_line += to_chips(1, w_gate.at[here])
     swap_o = begin(remote(w_out.at[core], w_out.at[core], wt_send.at[1], wt_recv.at[1], twin()))
-    up_across = across(w_up.at[seq_at], ms_send, ms_recv)
+    up_across = across(w_up, ms_send, ms_recv)
     swap.wait()
+    keep(both, to_both)
 
     def one_block(index, carry):
         step = lax.rem(index + 1, CHIPS)
@@ -643,17 +719,26 @@
         for head in range(heads):
             att_low[at, head * HEAD_DIM : (head + 1) * HEAD_DIM] = att_out[head, at, :].astype(low)
         when(step != 0, remote(att_low.at[at], attx.at[chip], a_send.at[step], a_recv.at[step], device).start)
+        pltpu.make_async_copy(att_out.at[:, at], to_att.at[:, at], att_sem.at[0, step]).start()
+        pltpu.make_async_copy(inv_out.at[:, at], to_inv.at[:, at], att_sem.at[1, step]).start()
         return carry
 
     lax.fori_loop(0, CHIPS, one_block, 0)
     attx[chip] = att_low[block, :]
+    swap_o.wait()
+    keep(w_out, to_out)
+    up_more = spread_relay(w_up, seq_rows, ms_send, ms_recv)
     for step in STEPS:
         remote(att_low.at[block], attx.at[chip], a_send.at[step], a_recv.at[step], chip_peer(step)[0]).wait()
-    for copy in m_line[3:] + up_across:
+    for copy in m_line[3:] + up_more:
         copy.wait_recv()
-    swap_o.wait()
     gather_drain(states_all, tok_rows, x_send, x_recv)
-    for copy in m_line + line + o_line + q_across + o_across + up_across:
+    for step in range(CHIPS):
+        pltpu.make_async_copy(att_out.at[:, block], to_att.at[:, block], att_sem.at[0, step]).wait()
+        pltpu.make_async_copy(inv_out.at[:, block], to_inv.at[:, block], att_sem.at[1, step]).wait()
+    for copy in kept:
+        copy.wait()
+    for copy in m_line + line + o_line + q_across + o_across + o_more + up_across + up_more:
         copy.wait_send()
 
 
@@ -688,8 +773,16 @@
             shape((chips, tok_rows, heads * HEAD_DIM), low),
         ],
         in_specs=[in_vmem(), in_vmem(), in_hbm(), in_vmem(), in_smem()],
-        out_specs=[in_vmem()] * 12,
+        out_specs=[in_hbm()] * 3 + [in_vmem()] * 3 + [in_hbm()] * 5 + [in_vmem()],
         scratch_shapes=[
+            VMEM((group_rows, model_width), low),
+            VMEM((CORES, model_width, half_cols), low),
+            VMEM((CORES, model_width, half_width), low),
+            VMEM((2, heads, group_rows, HEAD_DIM), f32),
+            VMEM((heads, group_rows, HEAD_DIM), low),
+            VMEM((CORES, 2, heads, group_rows, HEAD_DIM), low),
+            VMEM((heads, group_rows, HEAD_DIM), f32),
+            VMEM((heads, group_rows, 1), f32),
             VMEM((chips, CORES, rows, half_cols), f32),
             VMEM((chips, chip_rows, half_cols), f32),
             VMEM((chips, chip_rows, half_cols), low),
@@ -700,7 +793,7 @@
             VMEM((group_rows, 3 * heads * HEAD_DIM), f32),
             VMEM((group_rows, heads * HEAD_DIM), low),
             VMEM((1, CORES * group_rows), jnp.int32),
-            dma(12), line_dma(), line_dma(), dma(2), dma(2), dma(3, 4), dma(3, 4), dma(4), dma(4),
+            dma(12), dma(6), dma(2, 4), line_dma(), line_dma(), dma(2), dma(2), dma(3, 4), dma(3, 4), dma(4), dma(4),
             dma(4), dma(4), dma(2), dma(2), dma(4), dma(4), dma(4), dma(4), dma(2, 4), dma(2, 4),
             dma(4), dma(4), dma(1), dma(1), dma(4), dma(4),
         ],
@@ -717,9 +810,9 @@
 
 
 def mlp_kernel(
-    attx, states, cotangent, w_out, alpha_attn, alpha_mlp, gain_u, gain_v, w_up, w_gate, low_down,
-    out, grad_attx, grad_w_out, grad_direct, small, grad_half, grad_down,
-    weights, mixed_one, attn_unit, factors, mixed_low, mixed_all, up, gate, hidden, part,
+    attx, states, cotangent, from_out, alpha_attn, alpha_mlp, gain_u, gain_v, w_up, w_gate, low_down,
+    out, grad_attx, grad_w_out, grad_direct, small, to_half, grad_down,
+    w_out, grad_half, weights, mixed_one, attn_unit, factors, mixed_low, mixed_all, up, gate, hidden, part,
     sums, via, passed, total, grad_two, branch_low, branch_all, grad_u, grad_v, wide, turned, arrived,
     w_down, down_half, down_got, dot_u, dot_v,
     local_sem, ws_send, ws_recv, wt_send, wt_recv, x_send, x_recv, r_send, r_recv,
@@ -733,6 +826,7 @@
     half_width = w_out.shape[2]
     group_rows = CHIPS * tok_rows
     block = rows_at(chip, tok_rows)
+    load = begin(pltpu.make_async_copy(from_out, w_out, local_sem.at[2]))
     meet()
     seq_at = rows_at(seq, seq_rows)
     here = rows_at(chip, chip_rows)
@@ -742,18 +836,13 @@
         for step in STEPS
     ]
 
-    def spread(which, src):
-        return [
-            begin(remote(src, weights.at[which, core, seq_at], ws_send.at[which, step], ws_recv.at[which, step], seq_peer(step)[0]))
-            for step in STEPS
-        ]
-
-    across = spread(1, w_gate)
+    across = spread_start(w_gate, weights.at[1, core], seq_rows, ws_send.at[1], ws_recv.at[1])
     keeps = [
         begin(pltpu.make_async_copy(w_up, weights.at[0, core], local_sem.at[0])),
         begin(pltpu.make_async_copy(w_gate, weights.at[1, core, seq_at], local_sem.at[1])),
     ]
     w_down[here, :] = low_down[chip]
+    load.wait()
     part_at = [slice(at * chip_heads, (at + 1) * chip_heads) for at in range(CHIPS)]
     half_at = [slice(half * half_width, (half + 1) * half_width) for half in range(CORES)]
     branch = jnp.concatenate(
@@ -774,13 +863,15 @@
         copy.wait()
     for copy in to_chips:
         copy.wait_recv()
+    more = spread_relay(weights.at[1, core], seq_rows, ws_send.at[1], ws_recv.at[1])
+    across += spread_start(w_down, weights.at[2, core], seq_rows, ws_send.at[2], ws_recv.at[2])
+    weights[2, core, seq_at, :] = w_down[...]
     gather_hop(mixed_all, tok_rows, 1, x_send, x_recv)
-    for copy in across:
+    for copy in more:
         copy.wait_recv()
-    across += spread(2, w_down)
-    weights[2, core, seq_at, :] = w_down[...]
     swaps.append(begin(remote(weights.at[1, core], weights.at[1, core], wt_send.at[1], wt_recv.at[1], twin())))
     gather_hop(mixed_all, tok_rows, 2, x_send, x_recv)
+    down_more = spread_relay(weights.at[2, core], seq_rows, ws_send.at[2], ws_recv.at[2])
     gather_hop(mixed_all, tok_rows, 3, x_send, x_recv)
     for copy in swaps:
         copy.wait_recv()
@@ -799,7 +890,7 @@
         return carry
 
     lax.fori_loop(0, CORES * slabs, activate, 0)
-    for copy in across[-3:]:
+    for copy in down_more:
         copy.wait_recv()
     swap = begin(remote(weights.at[2, core], weights.at[2, core], wt_send.at[2], wt_recv.at[2], twin()))
     swaps.append(swap)
@@ -864,7 +955,7 @@
         return carry
 
     lax.fori_loop(0, model_width // tile, back_down, 0)
-    for copy in swaps:
+    for copy in swaps + more + down_more:
         copy.wait_send()
     reduce_start(part.at[1], tok_rows, sums.at[1], via.at[1], b_send, b_recv)
     turned[1] = branch_all[...].T
@@ -893,6 +984,10 @@
     ]
     weight_grads(0, 0, grad_u)
     weight_grads(1, 0, grad_v)
+    kept = []
+    for which in range(2):
+        grad_half[which] = both_cores(which)
+        kept.append(begin(pltpu.make_async_copy(grad_half.at[which], to_half.at[which], local_sem.at[which])))
     reduce_wait(part.at[1], tok_rows, sums.at[1], total, b_send, b_recv)
     grad = grad_two[...] * (1.0 - alpha_mlp[...]) + total[...]
     value = mixed_one[...]
@@ -913,13 +1008,13 @@
         unit_at = slice(half * half_units, (half + 1) * half_units)
         small[2:3, unit_at] = dot_u[half]
         small[3:4, unit_at] = dot_v[half] * math.sqrt(D)
-    for which in range(2):
-        grad_half[which] = both_cores(which)
     whole = down_half[seq_at, :].astype(jnp.float32)
     for step in STEPS:
         down_across[step - 1].wait_recv()
         whole = whole + down_got[step - 1].astype(jnp.float32)
     grad_down[...] = whole.astype(jnp.bfloat16)
+    for copy in kept:
+        copy.wait()
     gather_drain(mixed_all, tok_rows, x_send, x_recv)
     gather_drain(branch_all, tok_rows, g_send, g_recv)
     reduce_drain(part.at[0], tok_rows, sums.at[0], r_send, r_recv)
@@ -949,9 +1044,11 @@
             shape((2,) + matrix, low),
             shape((seq_rows, half_units), low),
         ],
-        in_specs=[in_vmem()] * 8 + [in_hbm(), in_vmem(), in_vmem()],
-        out_specs=[in_vmem()] * 7,
+        in_specs=[in_vmem()] * 3 + [in_hbm()] + [in_vmem()] * 4 + [in_hbm(), in_vmem(), in_vmem()],
+        out_specs=[in_vmem()] * 5 + [in_hbm(), in_vmem()],
         scratch_shapes=[
+            VMEM(w_out.shape, low),
+            VMEM((2,) + matrix, low),
             VMEM((3, CORES) + matrix, low),
             VMEM(tokens, f32),
             VMEM(tokens, f32),
@@ -979,7 +1076,7 @@
             VMEM((3, seq_rows, half_units), low),
             VMEM((CORES, 1, half_units), f32),
             VMEM((CORES, 1, half_units), f32),
-            dma(2), dma(3, 4), dma(3, 4), dma(3), dma(3), line_dma(), line_dma(), dma(4), dma(4),
+            dma(3), dma(3, 4), dma(3, 4), dma(3), dma(3), line_dma(), line_dma(), dma(4), dma(4),
             line_dma(), line_dma(), dma(4), dma(4), dma(3), dma(3), dma(4), dma(4), dma(4), dma(4),
         ],
         compiler_params=pltpu.CompilerParams(
@@ -992,13 +1089,13 @@
 
 
 def back_kernel(
-    grad_attx, grad_half, grad_down, grad_w_out, small_in, raw, query, both, att, inverse, states_all,
-    w_qkv, qk_gain, places, grad_direct,
+    grad_attx, from_half, grad_down, from_grad_out, small_in, from_raw, from_query, from_both, from_att,
+    from_inv, from_states, from_qkv, qk_gain, places, grad_direct,
     grad_states, out_mlp, out_attn, feature, unit,
-    att_low, heads_low, to_keys, swap_low, swap_kv, grad_heads, grad_sides, part, sums, via, passed, total, turned,
-    grad_q, half_q, seq_q, line_q, wide_q, half_o, pair_o, seq_got, seq_low, line_got, wide,
+    grad_half, grad_w_out, raw, query, both, att, inverse, states_all, w_qkv, att_low, heads_low, to_keys, swap_low, swap_kv, grad_heads, grad_sides, part, sums, via, passed, total, turned,
+    grad_q, half_q, seq_q, line_q, wide_q, half_o, pair_o, seq_got, seq_held, seq_last, seq_low, q_got, q_held, q_last, line_got, wide,
     wide_o, small, small_pair, small_seq, dots, small_all, flat_q, sides_q, key_pos,
-    local_sem, a_send, a_recv, s_send, s_recv, o_send, o_recv, kv_send, kv_recv, r_send, r_recv,
+    local_sem, load_sem, a_send, a_recv, s_send, s_recv, o_send, o_recv, kv_send, kv_recv, r_send, r_recv,
     qt_send, qt_recv, qs_send, qs_recv, qz_send, qz_recv, z_send, z_recv, f_send, f_recv,
     p_send, p_recv, t_send, t_recv,
 ):
@@ -1008,7 +1105,7 @@
     head_cols = heads * HEAD_DIM
     group_rows = CHIPS * tok_rows
     half_units = grad_half.shape[2]
-    seq_rows = seq_got.shape[2]
+    seq_rows = seq_low.shape[1]
     chip_rows = seq_rows // CHIPS
     rows = chip_rows // CORES
     part_cols = head_cols // CORES
@@ -1016,6 +1113,15 @@
     scale = math.sqrt(HEAD_DIM)
     block = rows_at(chip, tok_rows)
     f32, low = jnp.float32, jnp.bfloat16
+    loads = [
+        begin(pltpu.make_async_copy(src, dst, load_sem.at[at]))
+        for at, (src, dst) in enumerate(
+            (
+                (from_query, query), (from_both, both), (from_inv, inverse), (from_att, att), (from_raw, raw),
+                (from_grad_out, grad_w_out), (from_states, states_all), (from_half, grad_half), (from_qkv, w_qkv),
+            )
+        )
+    ]
     meet()
     waits = []
     line = []
@@ -1024,8 +1130,7 @@
         line.append(begin(remote(grad_attx.at[other], att_low.at[block], a_send.at[step], a_recv.at[step], device)))
     att_low[block, :] = grad_attx[chip]
     key_positions(places, key_pos, tok_rows)
-    pair = begin(remote(grad_w_out.at[1 - core], pair_o, o_send.at[0], o_recv.at[0], twin()))
-    across = []
+    pair = begin(remote(from_grad_out.at[1 - core], pair_o, o_send.at[0], o_recv.at[0], twin()))
     onward = {}
 
     def to_chips(which, src):
@@ -1035,24 +1140,27 @@
         ]
         line_got[which, chip] = src[rows_at(chip, chip_rows), :]
 
-    to_chips(2, grad_down)
-    for which in range(2):
-        for step in STEPS:
-            device, other = seq_peer(step)
-            across.append(begin(remote(grad_half.at[which, rows_at(other, seq_rows)], seq_got.at[which, step - 1], s_send.at[which, step], s_recv.at[which, step], device)))
-    keeps = [
-        begin(pltpu.make_async_copy(grad_half.at[which, rows_at(seq, seq_rows)], seq_low.at[which], local_sem.at[which]))
-        for which in range(2)
-    ]
+    def cross(which, src):
+        return fold_start(src, seq_got.at[which], seq_rows, s_send.at[which], s_recv.at[which])
+
+    def cross_on(which, src, copies):
+        return fold_relay(src, seq_got.at[which], seq_held.at[which], seq_last.at[which], seq_rows, copies, s_send.at[which], s_recv.at[which])
+
+    def cross_end(which, src, copies, more):
+        fold_end(src, seq_got.at[which], seq_last.at[which], seq_low.at[which], seq_rows, copies, more)
+
+    crossing = [cross(which, from_half.at[which]) for which in range(2)]
     to_keys[...] = jnp.zeros_like(to_keys)
     dots[...] = jnp.zeros_like(dots)
+    for copy in loads:
+        copy.wait()
     turned[...] = states_all[...].T
     pair.wait_recv()
     for at in range(4):
-        half_o[at] = (grad_w_out[core, at].astype(f32) + pair_o[at].astype(f32)).astype(low)
-    for step in STEPS:
-        device, other = seq_peer(step)
-        across.append(begin(remote(half_o.at[other], seq_got.at[2, step - 1], s_send.at[2, step], s_recv.at[2, step], device)))
+        half_o[at * seq_rows : (at + 1) * seq_rows, :] = (
+            grad_w_out[core, at].astype(f32) + pair_o[at].astype(f32)
+        ).astype(low)
+    crossing.append(cross(2, half_o))
     tile = tok_rows
     tiles = CHIPS
 
@@ -1095,6 +1203,9 @@
         return carry
 
     lax.fori_loop(0, CHIPS, one_block, 0)
+    to_chips(2, grad_down)
+    sources = (grad_half.at[0], grad_half.at[1], half_o)
+    onwards = [cross_on(which, sources[which], crossing[which]) for which in range(2)]
     swap_low[...] = to_keys[1 - core].astype(low)
     swap = begin(remote(swap_low, swap_kv, kv_send.at[0], kv_recv.at[0], twin()))
     swap.wait()
@@ -1113,6 +1224,9 @@
         full = jnp.concatenate([grad_heads[which, head] for head in range(heads)], axis=1)
         for half in range(CORES):
             grad_sides[half, :, which * part_cols : (which + 1) * part_cols] = full[:, half * part_cols : (half + 1) * part_cols]
+    onwards.append(cross_on(2, half_o, crossing[2]))
+    cross_end(0, sources[0], crossing[0], onwards[0])
+    to_chips(0, seq_low.at[0])
     wide_tile = model_width // 5
 
     def down(index, carry):
@@ -1131,44 +1245,30 @@
 
     lax.fori_loop(0, CORES * 5, weight_grad, 0)
     swap_q = begin(remote(grad_q.at[1 - core], half_q, qt_send.at[0], qt_recv.at[0], twin()))
+    cross_end(1, sources[1], crossing[1], onwards[1])
+    to_chips(1, seq_low.at[1])
     reduce_relay(part, tok_rows, sums, via, passed, r_send, r_recv)
     small[...] = small_in[...]
     small[4:5, :head_cols] = jnp.concatenate([dots[head] for head in range(heads)], axis=1)
     swap_s = begin(remote(small, small_pair, t_send.at[0], t_recv.at[0], twin()))
     swap_q.wait()
     half_q[...] = (grad_q[core].astype(f32) + half_q[...].astype(f32)).astype(low)
-    across_q = []
-    for step in STEPS:
-        device, other = seq_peer(step)
-        across_q.append(begin(remote(half_q.at[rows_at(other, seq_rows)], seq_q.at[step - 1], qs_send.at[step], qs_recv.at[step], device)))
+    crossing_q = fold_start(half_q, q_got, seq_rows, qs_send, qs_recv)
+    cross_end(2, half_o, crossing[2], onwards[2])
+    to_chips(3, seq_low.at[2])
     swap_s.wait()
     small[...] = small[...] + small_pair[...]
     spread_s = [
         begin(remote(small, small_seq.at[step - 1], t_send.at[step], t_recv.at[step], seq_peer(step)[0]))
         for step in STEPS
     ]
-    for copy in keeps:
-        copy.wait()
-    seq_low[2] = half_o[seq]
-    for at, which in enumerate((0, 1, 3)):
-        for copy in across[3 * at : 3 * at + 3]:
-            copy.wait_recv()
-        whole = seq_low[at].astype(f32)
-        for step in STEPS:
-            whole = whole + seq_got[at, step - 1].astype(f32)
-        seq_low[at] = whole.astype(low)
-        to_chips(which, seq_low.at[at])
-    for copy in across_q:
-        copy.wait_recv()
-    whole = half_q[rows_at(seq, seq_rows), :].astype(f32)
-    for step in STEPS:
-        whole = whole + seq_q[step - 1].astype(f32)
-    grad_q[0, :seq_rows, :] = whole.astype(low)
+    more_q = fold_relay(half_q, q_got, q_held, q_last, seq_rows, crossing_q, qs_send, qs_recv)
+    fold_end(half_q, q_got, q_last, seq_q, seq_rows, crossing_q, more_q)
     onward_q = []
     for step in STEPS:
         device, other = chip_peer(step)
-        onward_q.append(begin(remote(grad_q.at[0, rows_at(other, chip_rows)], line_q.at[chip], qz_send.at[step], qz_recv.at[step], device)))
-    line_q[chip] = grad_q[0, rows_at(chip, chip_rows), :]
+        onward_q.append(begin(remote(seq_q.at[rows_at(other, chip_rows)], line_q.at[chip], qz_send.at[step], qz_recv.at[step], device)))
+    line_q[chip] = seq_q[rows_at(chip, chip_rows), :]
     for copy in spread_s:
         copy.wait()
     small_pair[...] = small[...] + small_seq[0] + small_seq[1] + small_seq[2]
@@ -1222,7 +1322,7 @@
     for copy in last + lasts:
         copy.wait()
     reduce_drain(part, tok_rows, sums, r_send, r_recv)
-    for copy in line + [pair] + across + across_q + onward_q + sum(onward.values(), []):
+    for copy in line + [pair] + sum(crossing + onwards + list(onward.values()), crossing_q + more_q + onward_q):
         copy.wait_send()
 
 
@@ -1251,9 +1351,10 @@
             shape((3, model_width), f32),
             shape((2, chips * CORES * half_units), f32),
         ],
-        in_specs=[in_vmem(), in_hbm()] + [in_vmem()] * 11 + [in_smem(), in_vmem()],
+        in_specs=[in_vmem(), in_hbm(), in_vmem(), in_hbm(), in_vmem()] + [in_hbm()] * 7 + [in_vmem(), in_smem(), in_vmem()],
         out_specs=[in_vmem(), in_hbm(), in_hbm(), in_vmem(), in_vmem()],
         scratch_shapes=[
+            *(VMEM(value.shape, value.dtype) for value in (grad_half, grad_w_out, raw, query, both, att, inverse, states_all, w_qkv)),
             VMEM((group_rows, head_cols), low),
             VMEM(per_head, low),
             VMEM((CORES, 2) + per_head, f32),
@@ -1269,13 +1370,18 @@
             VMEM((model_width, group_rows), low),
             VMEM((CORES, model_width, half_cols), low),
             VMEM((model_width, half_cols), low),
-            VMEM((3, seq_rows, half_cols), low),
+            VMEM((seq_rows, half_cols), low),
             VMEM((chips, chip_rows, half_cols), low),
             VMEM((chips, chip_rows, half_cols), f32),
+            VMEM((4 * seq_rows, half_units), low),
             VMEM((4, seq_rows, half_units), low),
-            VMEM((4, seq_rows, half_units), low),
-            VMEM((3, 3, seq_rows, half_units), low),
+            VMEM((3, 2, 2, seq_rows // 2, half_units), low),
+            VMEM((3, 2, seq_rows // 2, half_units), low),
+            VMEM((3, 2, seq_rows // 2, half_units), low),
             VMEM((3, seq_rows, half_units), low),
+            VMEM((2, 2, seq_rows // 2, half_cols), low),
+            VMEM((2, seq_rows // 2, half_cols), low),
+            VMEM((2, seq_rows // 2, half_cols), low),
             VMEM((4, chips, chip_rows, half_units), low),
             VMEM((3, chips, chip_rows, half_units), f32),
             VMEM((chip_rows, half_units), f32),
@@ -1287,8 +1393,8 @@
             VMEM((rows, 3 * model_width), f32),
             VMEM((CORES, chips, rows, half_cols), f32),
             VMEM((1, CORES * group_rows), jnp.int32),
-            dma(17), dma(4), dma(4), dma(4, 4), dma(4, 4), dma(1), dma(1), dma(1), dma(1),
-            dma(4), dma(4), dma(1), dma(1), dma(4), dma(4), dma(4), dma(4), dma(4, 4), dma(4, 4),
+            dma(17), dma(9), dma(4), dma(4), dma(3, 3, 2), dma(3, 3, 2), dma(1), dma(1), dma(1), dma(1),
+            dma(4), dma(4), dma(1), dma(1), dma(3, 2), dma(3, 2), dma(4), dma(4), dma(4, 4), dma(4, 4),
             dma(4, 4), dma(4, 4), dma(4), dma(4), dma(4), dma(4),
         ],
         compiler_params=pltpu.CompilerParams(

time: 347 us -> 331 us (0.954)
  Pallas kernels: 333 us -> 318 us
    pallas_call x1, Pallas kernels: 86.7 us -> 78.5 us  [attend_call(): pl.pallas_call(attend_kernel, out_shape=[shape((group_rows, model_width),...]
    pallas_call x1, Pallas kernels: 142 us -> 138 us  [mlp_call(): pl.pallas_call(mlp_kernel, out_shape=[shape(tokens, low), shape(attx.shap...]
where the time goes in v6:
time: 331 us
  Pallas kernels  318 us (96%)
  local copies, waits for them, and re-layouts  11.9 us (4%)
    pallas_call x1, Pallas kernels, mlp_call(): pl.pallas_call(mlp_kernel, out_shape=[shape(tokens, low), shape(attx.shap...  138 us
    pallas_call x1, Pallas kernels, back_call(): pl.pallas_call(back_kernel, out_shape=[shape((tok_rows, model_width), low...  101 us
    pallas_call x1, Pallas kernels, attend_call(): pl.pallas_call(attend_kernel, out_shape=[shape((group_rows, model_width),...  78.5 us

profile of v6, /device:TPU:0, one launch (start us, length us, event | category | flops | bytes accessed | tf_op | source)
XLA Modules:
  0.0 330.8 jit_solution(13909209156176528076)
XLA Ops:
  0.7 1.4 slice_bitcast_fusion
  2.1 0.1 dynamic-slice_reduce_fusion
  2.2 0.7 reshape.36.qk_gain
  2.9 0.9 fusion
  3.8 0.6 dynamic-slice_multiply_fusion
  4.4 78.5 %attend.1 = (bf16[512,1280]{1,0:T(8,128)(2,1)}, bf16[2,1280,480]{2,1,0:T(8,128)(2,1)}, bf16[2,1280,640]{2,1,0:T(8,128)(2,1)}, bf16[1280,640]{1,0:T(8,128)(2,1)},...) custom-call(bf16[128,1280]{1,0:T(8,128)(2,1)} %states.3, ...), custom_call_target="tpu_custom_call" | custom-call | tf_op jit(solution)/shard_map/attend/pallas_call | solution.py:759
  82.9 138.2 %mlp.1 = (bf16[128,1280]{1,0:T(8,128)(2,1)}, bf16[4,128,320]{2,1,0:T(8,128)(2,1)}, bf16[2,4,320,640]{3,2,1,0:T(8,128)(2,1)}, f32[128,1280]{1,0:T(8,128)}, f32[8,...) custom-call(bf16[4,128,320]{2,1,0:T(8,128)(2,1)} %get-tuple-element.30.attx, ...), custom_call_target="tpu_custom_call" | custom-call | tf_op jit(solution)/shard_map/mlp/pallas_call | solution.py:1036
  221.1 0.0 copy-start.1
  221.1 100.8 %back.1 = (bf16[128,1280]{1,0:T(8,128)(2,1)}, f32[40,15360]{1,0:T(8,128)}, f32[40,5120]{1,0:T(8,128)}, f32[3,1280]{1,0:T(4,128)}, f32[2,5120]{1,0:T(2,128)}) custom-call(bf16[4,128,320]{2,1,0:T(8,128)(2,1)} %get-tuple-element.36.grad_attx, bf16[2,1280,640]{2,1,0:T(8,128)(2,1)} %get-tuple-element.37.from_half, bf16[320,640]{1,0:T(8,128)(2,1)} %get-tuple-element.38.grad_down, ...), custom_call_target="tpu_custom_call" | custom-call | tf_op jit(solution)/shard_map/back/pallas_call | solution.py:1345
  322.0 0.0 copy-start
  322.0 1.5 dynamic-slice_bitcast_fusion.1
  323.5 1.3 dynamic-slice_bitcast_fusion
  324.8 0.0 copy-done.1
  324.8 0.7 copy.17
  325.5 1.7 copy.18
  327.2 2.1 copy.19
  329.3 0.0 copy-done
  329.3 1.4 copy.20
Async XLA Ops:
  221.1 103.7 %copy-start.1 = (bf16[128,1280]{1,0:T(8,128)(2,1)S(1)}, bf16[128,1280]{1,0:T(8,128)(2,1)}, u32[]{:S(2)}) copy-start(bf16[128,1280]{1,0:T(8,128)(2,1)} %get-tuple-element.67) | copy-start | bytes 983044
  322.0 7.3 %copy-start = (f32[40,15360]{1,0:T(8,128)S(1)}, f32[40,15360]{1,0:T(8,128)}, u32[]{:S(2)}) copy-start(f32[40,15360]{1,0:T(8,128)} %get-tuple-element.70) | copy-start | bytes 7372804

commit v7 on v6

--- a/solution.py
+++ b/solution.py
@@ -392,16 +392,17 @@
     return abs(place_of()[1] - other) == CHIPS - 1
 
 
-def reduce_start(part, count, sums, via, send, recv):
+def reduce_start(part, count, sums, via, send, recv, ahead=True):
     chip = place_of()[1]
     near = jnp.where(chip == 0, 1, CHIPS - 2)
     first = remote(part.at[rows_at(CHIPS - 1 - chip, count)], via, send.at[0], recv.at[0], device_on(near))
 
-    def ahead():
+    def begin_far():
         first.start()
-        first.wait_send()
-
-    when(jnp.logical_not(inside_line()), ahead)
+        if ahead:
+            first.wait_send()
+
+    when(jnp.logical_not(inside_line()), begin_far)
     for step in STEPS:
         device, other = chip_peer(step)
         copy = remote(part.at[rows_at(other, count)], sums.at[step - 1], send.at[step], recv.at[step], device)
@@ -440,12 +441,15 @@
         when(jnp.logical_not(spans_line(source)), add)
 
 
-def reduce_drain(part, count, sums, send, recv):
+def reduce_drain(part, count, sums, send, recv, ahead=True):
     rows = part.at[rows_at(0, count)]
     for step in STEPS:
         device, other = chip_peer(step)
         copy = remote(rows, sums.at[step - 1], send.at[step], recv.at[step], device)
         when(jnp.logical_not(spans_line(other)), copy.wait_send)
+    if not ahead:
+        copy = remote(rows, sums.at[0], send.at[0], recv.at[0], device_on(place_of()[1]))
+        when(jnp.logical_not(inside_line()), copy.wait_send)
 
 
 def side_peer(side):
@@ -620,9 +624,9 @@
     w_qkv[core, my_rows, :] = low_q[chip]
     states_all[block, :] = states[...]
     key_positions(places, key_pos, tok_rows)
+    gather_start(states, states_all, tok_rows, x_send, x_recv)
     for copy in line:
         copy.wait_recv()
-    gather_start(states, states_all, tok_rows, x_send, x_recv)
 
     def across(whole, send, recv):
         return spread_start(whole.at[seq_at], whole, seq_rows, send, recv)
@@ -870,26 +874,35 @@
     for copy in more:
         copy.wait_recv()
     swaps.append(begin(remote(weights.at[1, core], weights.at[1, core], wt_send.at[1], wt_recv.at[1], twin())))
+    slab = min(64, group_rows)
+    slabs = group_rows // slab
+    half_slabs = slabs // 2
+    half_rows = group_rows // 2
+    mine = chip // 2
+
+    def forward(group):
+        rows = rows_at(group, half_rows)
+        for half in range(CORES):
+            up[half, rows, :] = dot(mixed_all[rows, :], weights[0, half])
+            gate[half, rows, :] = dot(mixed_all[rows, :], weights[1, half])
+
+        def activate(index, carry):
+            half = index // half_slabs
+            at = rows_at(group * half_slabs + lax.rem(index, half_slabs), slab)
+            gated = gate[half, at, :] * gain_v[half]
+            scaled = up[half, at, :] * gain_u[half]
+            hidden[half, at, :] = (gated * jax.nn.sigmoid(gated) * scaled).astype(jnp.bfloat16)
+            return carry
+
+        lax.fori_loop(0, CORES * half_slabs, activate, 0)
+
+    for copy in swaps:
+        copy.wait_recv()
+    forward(mine)
     gather_hop(mixed_all, tok_rows, 2, x_send, x_recv)
     down_more = spread_relay(weights.at[2, core], seq_rows, ws_send.at[2], ws_recv.at[2])
     gather_hop(mixed_all, tok_rows, 3, x_send, x_recv)
-    for copy in swaps:
-        copy.wait_recv()
-    for half in range(CORES):
-        up[half] = dot(mixed_all[...], weights[0, half])
-        gate[half] = dot(mixed_all[...], weights[1, half])
-    slab = min(64, group_rows)
-    slabs = group_rows // slab
-
-    def activate(index, carry):
-        half = index // slabs
-        at = rows_at(lax.rem(index, slabs), slab)
-        gated = gate[half, at, :] * gain_v[half]
-        scaled = up[half, at, :] * gain_u[half]
-        hidden[half, at, :] = (gated * jax.nn.sigmoid(gated) * scaled).astype(jnp.bfloat16)
-        return carry
-
-    lax.fori_loop(0, CORES * slabs, activate, 0)
+    forward(1 - mine)
     for copy in down_more:
         copy.wait_recv()
     swap = begin(remote(weights.at[2, core], weights.at[2, core], wt_send.at[2], wt_recv.at[2], twin()))
@@ -957,7 +970,7 @@
     lax.fori_loop(0, model_width // tile, back_down, 0)
     for copy in swaps + more + down_more:
         copy.wait_send()
-    reduce_start(part.at[1], tok_rows, sums.at[1], via.at[1], b_send, b_recv)
+    reduce_start(part.at[1], tok_rows, sums.at[1], via.at[1], b_send, b_recv, False)
     turned[1] = branch_all[...].T
     swaps = {}
 
@@ -977,12 +990,12 @@
 
     weight_grads(2, 1, hidden)
     reduce_relay(part.at[1], tok_rows, sums.at[1], via.at[1], passed.at[1], b_send, b_recv)
+    weight_grads(0, 0, grad_u)
     down_half[...] = both_cores(2)
     down_across = [
         begin(remote(down_half.at[rows_at(seq_peer(step)[1], seq_rows)], down_got.at[step - 1], ds_send.at[step], ds_recv.at[step], seq_peer(step)[0]))
         for step in STEPS
     ]
-    weight_grads(0, 0, grad_u)
     weight_grads(1, 0, grad_v)
     kept = []
     for which in range(2):
@@ -1018,7 +1031,7 @@
     gather_drain(mixed_all, tok_rows, x_send, x_recv)
     gather_drain(branch_all, tok_rows, g_send, g_recv)
     reduce_drain(part.at[0], tok_rows, sums.at[0], r_send, r_recv)
-    reduce_drain(part.at[1], tok_rows, sums.at[1], b_send, b_recv)
+    reduce_drain(part.at[1], tok_rows, sums.at[1], b_send, b_recv, False)
     for copy in across + to_chips + down_across + [swaps[which] for which in range(3)]:
         copy.wait_send()
 
@@ -1224,19 +1237,7 @@
         full = jnp.concatenate([grad_heads[which, head] for head in range(heads)], axis=1)
         for half in range(CORES):
             grad_sides[half, :, which * part_cols : (which + 1) * part_cols] = full[:, half * part_cols : (half + 1) * part_cols]
-    onwards.append(cross_on(2, half_o, crossing[2]))
-    cross_end(0, sources[0], crossing[0], onwards[0])
-    to_chips(0, seq_low.at[0])
     wide_tile = model_width // 5
-
-    def down(index, carry):
-        at = rows_at(index, wide_tile)
-        part[:, at] = sum(dot_nt(grad_sides[half], w_qkv[half, at, :]) for half in range(CORES)).astype(low)
-        return carry
-
-    lax.fori_loop(0, 5, down, 0)
-    reduce_start(part, tok_rows, sums, via, r_send, r_recv)
-
     def weight_grad(index, carry):
         half = index // 5
         at = rows_at(lax.rem(index, 5), wide_tile)
@@ -1245,24 +1246,35 @@
 
     lax.fori_loop(0, CORES * 5, weight_grad, 0)
     swap_q = begin(remote(grad_q.at[1 - core], half_q, qt_send.at[0], qt_recv.at[0], twin()))
+    onwards.append(cross_on(2, half_o, crossing[2]))
+    cross_end(0, sources[0], crossing[0], onwards[0])
+    to_chips(0, seq_low.at[0])
+
+    def down(index, carry):
+        at = rows_at(index, wide_tile)
+        part[:, at] = sum(dot_nt(grad_sides[half], w_qkv[half, at, :]) for half in range(CORES)).astype(low)
+        return carry
+
+    lax.fori_loop(0, 5, down, 0)
+    reduce_start(part, tok_rows, sums, via, r_send, r_recv, False)
+    swap_q.wait()
+    half_q[...] = (grad_q[core].astype(f32) + half_q[...].astype(f32)).astype(low)
+    crossing_q = fold_start(half_q, q_got, seq_rows, qs_send, qs_recv)
     cross_end(1, sources[1], crossing[1], onwards[1])
     to_chips(1, seq_low.at[1])
-    reduce_relay(part, tok_rows, sums, via, passed, r_send, r_recv)
+    cross_end(2, half_o, crossing[2], onwards[2])
+    to_chips(3, seq_low.at[2])
     small[...] = small_in[...]
     small[4:5, :head_cols] = jnp.concatenate([dots[head] for head in range(heads)], axis=1)
     swap_s = begin(remote(small, small_pair, t_send.at[0], t_recv.at[0], twin()))
-    swap_q.wait()
-    half_q[...] = (grad_q[core].astype(f32) + half_q[...].astype(f32)).astype(low)
-    crossing_q = fold_start(half_q, q_got, seq_rows, qs_send, qs_recv)
-    cross_end(2, half_o, crossing[2], onwards[2])
-    to_chips(3, seq_low.at[2])
+    more_q = fold_relay(half_q, q_got, q_held, q_last, seq_rows, crossing_q, qs_send, qs_recv)
+    reduce_relay(part, tok_rows, sums, via, passed, r_send, r_recv)
     swap_s.wait()
     small[...] = small[...] + small_pair[...]
     spread_s = [
         begin(remote(small, small_seq.at[step - 1], t_send.at[step], t_recv.at[step], seq_peer(step)[0]))
         for step in STEPS
     ]
-    more_q = fold_relay(half_q, q_got, q_held, q_last, seq_rows, crossing_q, qs_send, qs_recv)
     fold_end(half_q, q_got, q_last, seq_q, seq_rows, crossing_q, more_q)
     onward_q = []
     for step in STEPS:
@@ -1274,8 +1286,6 @@
     small_pair[...] = small[...] + small_seq[0] + small_seq[1] + small_seq[2]
     small_all[chip] = small_pair[...]
     ends = to_line(small_pair, small_all.at[chip], p_send, p_recv)
-    reduce_wait(part, tok_rows, sums, total, r_send, r_recv)
-    grad_states[...] = (total[...] + grad_direct[...]).astype(low)
 
     mine = rows_at(core, rows)
     theirs = rows_at(1 - core, rows)
@@ -1319,9 +1329,11 @@
                 start = which * model_width + at * head_cols + half * part_cols
                 flat_q[:, start : start + part_cols] = sides_q[half, at, :, which * part_cols : (which + 1) * part_cols]
     lasts.append(begin(pltpu.make_async_copy(flat_q, out_attn.at[:, pl.ds(0, 3 * model_width)], local_sem.at[16])))
+    reduce_wait(part, tok_rows, sums, total, r_send, r_recv)
+    grad_states[...] = (total[...] + grad_direct[...]).astype(low)
     for copy in last + lasts:
         copy.wait()
-    reduce_drain(part, tok_rows, sums, r_send, r_recv)
+    reduce_drain(part, tok_rows, sums, r_send, r_recv, False)
     for copy in line + [pair] + sum(crossing + onwards + list(onward.values()), crossing_q + more_q + onward_q):
         copy.wait_send()
 

time: 331 us -> 319 us (0.964)
  Pallas kernels: 318 us -> 305 us
    pallas_call x1, Pallas kernels: 138 us -> 127 us  [mlp_call(): pl.pallas_call(mlp_kernel, out_shape=[shape(tokens, low), shape(attx.shap...]
where the time goes in v7:
time: 319 us; the launch traced here: 318 us
  Pallas kernels  305 us (96%)
  local copies, waits for them, and re-layouts  11.9 us (4%)
    pallas_call x1, Pallas kernels, mlp_call(): pl.pallas_call(mlp_kernel, out_shape=[shape(tokens, low), shape(attx.shap...  127 us
    pallas_call x1, Pallas kernels, back_call(): pl.pallas_call(back_kernel, out_shape=[shape((tok_rows, model_width), low...  98.7 us
    pallas_call x1, Pallas kernels, attend_call(): pl.pallas_call(attend_kernel, out_shape=[shape((group_rows, model_width),...  78.8 us

profile of v7, /device:TPU:0, one launch (start us, length us, event | category | flops | bytes accessed | tf_op | source)
XLA Modules:
  0.0 318.2 jit_solution(16276673229105870668)
XLA Ops:
  0.7 1.4 slice_bitcast_fusion
  2.1 0.1 dynamic-slice_reduce_fusion
  2.2 0.7 reshape.36.qk_gain
  2.9 0.9 fusion
  3.8 0.6 dynamic-slice_multiply_fusion
  4.4 78.8 %attend.1 = (bf16[512,1280]{1,0:T(8,128)(2,1)}, bf16[2,1280,480]{2,1,0:T(8,128)(2,1)}, bf16[2,1280,640]{2,1,0:T(8,128)(2,1)}, bf16[1280,640]{1,0:T(8,128)(2,1)},...) custom-call(bf16[128,1280]{1,0:T(8,128)(2,1)} %states.3, ...), custom_call_target="tpu_custom_call" | custom-call | tf_op jit(solution)/shard_map/attend/pallas_call | solution.py:763
  83.2 127.4 %mlp.1 = (bf16[128,1280]{1,0:T(8,128)(2,1)}, bf16[4,128,320]{2,1,0:T(8,128)(2,1)}, bf16[2,4,320,640]{3,2,1,0:T(8,128)(2,1)}, f32[128,1280]{1,0:T(8,128)}, f32[8,...) custom-call(bf16[4,128,320]{2,1,0:T(8,128)(2,1)} %get-tuple-element.30.attx, ...), custom_call_target="tpu_custom_call" | custom-call | tf_op jit(solution)/shard_map/mlp/pallas_call | solution.py:1049
  210.6 0.0 copy-start.1
  210.6 98.7 %back.1 = (bf16[128,1280]{1,0:T(8,128)(2,1)}, f32[40,15360]{1,0:T(8,128)}, f32[40,5120]{1,0:T(8,128)}, f32[3,1280]{1,0:T(4,128)}, f32[2,5120]{1,0:T(2,128)}) custom-call(bf16[4,128,320]{2,1,0:T(8,128)(2,1)} %get-tuple-element.36.grad_attx, bf16[2,1280,640]{2,1,0:T(8,128)(2,1)} %get-tuple-element.37.from_half, bf16[320,640]{1,0:T(8,128)(2,1)} %get-tuple-element.38.grad_down, ...), custom_call_target="tpu_custom_call" | custom-call | tf_op jit(solution)/shard_map/back/pallas_call | solution.py:1357
  309.4 0.0 copy-start
  309.4 1.5 dynamic-slice_bitcast_fusion.1
  310.9 1.3 dynamic-slice_bitcast_fusion
  312.2 0.0 copy-done.1
  312.2 0.7 copy.17
  312.9 1.7 copy.18
  314.6 2.1 copy.19
  316.7 0.0 copy-done
  316.7 1.4 copy.20
Async XLA Ops:
  210.6 101.6 %copy-start.1 = (bf16[128,1280]{1,0:T(8,128)(2,1)S(1)}, bf16[128,1280]{1,0:T(8,128)(2,1)}, u32[]{:S(2)}) copy-start(bf16[128,1280]{1,0:T(8,128)(2,1)} %get-tuple-element.67) | copy-start | bytes 983044
  309.4 7.3 %copy-start = (f32[40,15360]{1,0:T(8,128)S(1)}, f32[40,15360]{1,0:T(8,128)}, u32[]{:S(2)}) copy-start(f32[40,15360]{1,0:T(8,128)} %get-tuple-element.70) | copy-start | bytes 7372804

commit v8 on v7

--- a/solution.py
+++ b/solution.py
@@ -1153,6 +1153,8 @@
         ]
         line_got[which, chip] = src[rows_at(chip, chip_rows), :]
 
+    to_chips(2, grad_down)
+
     def cross(which, src):
         return fold_start(src, seq_got.at[which], seq_rows, s_send.at[which], s_recv.at[which])
 
@@ -1162,18 +1164,20 @@
     def cross_end(which, src, copies, more):
         fold_end(src, seq_got.at[which], seq_last.at[which], seq_low.at[which], seq_rows, copies, more)
 
-    crossing = [cross(which, from_half.at[which]) for which in range(2)]
+    crossing = [cross(0, from_half.at[0])]
     to_keys[...] = jnp.zeros_like(to_keys)
     dots[...] = jnp.zeros_like(dots)
     for copy in loads:
         copy.wait()
     turned[...] = states_all[...].T
+    sources = (grad_half.at[0], grad_half.at[1], half_o)
+    onwards = [cross_on(0, sources[0], crossing[0])]
+    crossing.append(cross(1, from_half.at[1]))
     pair.wait_recv()
     for at in range(4):
         half_o[at * seq_rows : (at + 1) * seq_rows, :] = (
             grad_w_out[core, at].astype(f32) + pair_o[at].astype(f32)
         ).astype(low)
-    crossing.append(cross(2, half_o))
     tile = tok_rows
     tiles = CHIPS
 
@@ -1189,7 +1193,8 @@
         other = lax.rem(chip + CHIPS - step, CHIPS)
         at = rows_at(other, tok_rows)
         copy = remote(grad_attx.at[0], att_low.at[at], a_send.at[step], a_recv.at[step], device_on(other))
-        when(step > 0, copy.wait_recv)
+        if step > 0:
+            copy.wait_recv()
         for head in range(heads):
             heads_low[head, at, :] = att_low[at, head * HEAD_DIM : (head + 1) * HEAD_DIM]
         allowed = kept_pairs(places, key_pos, other, core, tok_rows)
@@ -1215,10 +1220,16 @@
         lax.fori_loop(0, heads, one_head, 0)
         return carry
 
-    lax.fori_loop(0, CHIPS, one_block, 0)
-    to_chips(2, grad_down)
-    sources = (grad_half.at[0], grad_half.at[1], half_o)
-    onwards = [cross_on(which, sources[which], crossing[which]) for which in range(2)]
+    one_block(0, 0)
+    cross_end(0, sources[0], crossing[0], onwards[0])
+    to_chips(0, seq_low.at[0])
+    one_block(1, 0)
+    onwards.append(cross_on(1, sources[1], crossing[1]))
+    crossing.append(cross(2, half_o))
+    one_block(2, 0)
+    one_block(3, 0)
+    cross_end(1, sources[1], crossing[1], onwards[1])
+    to_chips(1, seq_low.at[1])
     swap_low[...] = to_keys[1 - core].astype(low)
     swap = begin(remote(swap_low, swap_kv, kv_send.at[0], kv_recv.at[0], twin()))
     swap.wait()
@@ -1238,6 +1249,16 @@
         for half in range(CORES):
             grad_sides[half, :, which * part_cols : (which + 1) * part_cols] = full[:, half * part_cols : (half + 1) * part_cols]
     wide_tile = model_width // 5
+    onwards.append(cross_on(2, half_o, crossing[2]))
+
+    def down(index, carry):
+        at = rows_at(index, wide_tile)
+        part[:, at] = sum(dot_nt(grad_sides[half], w_qkv[half, at, :]) for half in range(CORES)).astype(low)
+        return carry
+
+    lax.fori_loop(0, 5, down, 0)
+    reduce_start(part, tok_rows, sums, via, r_send, r_recv, False)
+
     def weight_grad(index, carry):
         half = index // 5
         at = rows_at(lax.rem(index, 5), wide_tile)
@@ -1246,49 +1267,31 @@
 
     lax.fori_loop(0, CORES * 5, weight_grad, 0)
     swap_q = begin(remote(grad_q.at[1 - core], half_q, qt_send.at[0], qt_recv.at[0], twin()))
-    onwards.append(cross_on(2, half_o, crossing[2]))
-    cross_end(0, sources[0], crossing[0], onwards[0])
-    to_chips(0, seq_low.at[0])
-
-    def down(index, carry):
-        at = rows_at(index, wide_tile)
-        part[:, at] = sum(dot_nt(grad_sides[half], w_qkv[half, at, :]) for half in range(CORES)).astype(low)
-        return carry
-
-    lax.fori_loop(0, 5, down, 0)
-    reduce_start(part, tok_rows, sums, via, r_send, r_recv, False)
     swap_q.wait()
     half_q[...] = (grad_q[core].astype(f32) + half_q[...].astype(f32)).astype(low)
     crossing_q = fold_start(half_q, q_got, seq_rows, qs_send, qs_recv)
-    cross_end(1, sources[1], crossing[1], onwards[1])
-    to_chips(1, seq_low.at[1])
     cross_end(2, half_o, crossing[2], onwards[2])
     to_chips(3, seq_low.at[2])
+    reduce_relay(part, tok_rows, sums, via, passed, r_send, r_recv)
     small[...] = small_in[...]
     small[4:5, :head_cols] = jnp.concatenate([dots[head] for head in range(heads)], axis=1)
     swap_s = begin(remote(small, small_pair, t_send.at[0], t_recv.at[0], twin()))
     more_q = fold_relay(half_q, q_got, q_held, q_last, seq_rows, crossing_q, qs_send, qs_recv)
-    reduce_relay(part, tok_rows, sums, via, passed, r_send, r_recv)
+    fold_end(half_q, q_got, q_last, seq_q, seq_rows, crossing_q, more_q)
+    onward_q = []
+    for step in STEPS:
+        device, other = chip_peer(step)
+        onward_q.append(begin(remote(seq_q.at[rows_at(other, chip_rows)], line_q.at[chip], qz_send.at[step], qz_recv.at[step], device)))
+    line_q[chip] = seq_q[rows_at(chip, chip_rows), :]
+
+    mine = rows_at(core, rows)
+    theirs = rows_at(1 - core, rows)
     swap_s.wait()
     small[...] = small[...] + small_pair[...]
     spread_s = [
         begin(remote(small, small_seq.at[step - 1], t_send.at[step], t_recv.at[step], seq_peer(step)[0]))
         for step in STEPS
     ]
-    fold_end(half_q, q_got, q_last, seq_q, seq_rows, crossing_q, more_q)
-    onward_q = []
-    for step in STEPS:
-        device, other = chip_peer(step)
-        onward_q.append(begin(remote(seq_q.at[rows_at(other, chip_rows)], line_q.at[chip], qz_send.at[step], qz_recv.at[step], device)))
-    line_q[chip] = seq_q[rows_at(chip, chip_rows), :]
-    for copy in spread_s:
-        copy.wait()
-    small_pair[...] = small[...] + small_seq[0] + small_seq[1] + small_seq[2]
-    small_all[chip] = small_pair[...]
-    ends = to_line(small_pair, small_all.at[chip], p_send, p_recv)
-
-    mine = rows_at(core, rows)
-    theirs = rows_at(1 - core, rows)
     last, lasts = [], []
     for which in (2, 0, 1):
         for copy in onward[which]:
@@ -1299,6 +1302,11 @@
             there = out_mlp.at[:, pl.ds(pl.multiple_of(start, 128), half_units)]
             last.append(begin(remote(wide.at[which, at, theirs], there, f_send.at[which, at], f_recv.at[which, at], twin())))
             lasts.append(begin(pltpu.make_async_copy(wide.at[which, at, mine], there, local_sem.at[3 + which * CHIPS + at])))
+    for copy in spread_s:
+        copy.wait()
+    small_pair[...] = small[...] + small_seq[0] + small_seq[1] + small_seq[2]
+    small_all[chip] = small_pair[...]
+    ends = to_line(small_pair, small_all.at[chip], p_send, p_recv)
     for copy in onward[3]:
         copy.wait_recv()
     whole = line_got[3, 0].astype(f32)

time: 319 us -> 311 us (0.975)
  Pallas kernels: 305 us -> 297 us
    pallas_call x1, Pallas kernels: 98.7 us -> 90.9 us  [back_call(): pl.pallas_call(back_kernel, out_shape=[shape((tok_rows, model_width), low...]
where the time goes in v8:
time: 311 us; the launch traced here: 310 us
  Pallas kernels  297 us (95%)
  local copies, waits for them, and re-layouts  11.9 us (4%)
    pallas_call x1, Pallas kernels, mlp_call(): pl.pallas_call(mlp_kernel, out_shape=[shape(tokens, low), shape(attx.shap...  127 us
    pallas_call x1, Pallas kernels, back_call(): pl.pallas_call(back_kernel, out_shape=[shape((tok_rows, model_width), low...  90.9 us
    pallas_call x1, Pallas kernels, attend_call(): pl.pallas_call(attend_kernel, out_shape=[shape((group_rows, model_width),...  78.8 us

profile of v8, /device:TPU:0, one launch (start us, length us, event | category | flops | bytes accessed | tf_op | source)
XLA Modules:
  0.0 310.3 jit_solution(16750635279657401211)
XLA Ops:
  0.7 1.4 slice_bitcast_fusion
  2.1 0.1 dynamic-slice_reduce_fusion
  2.2 0.7 reshape.36.qk_gain
  2.9 0.9 fusion
  3.8 0.6 dynamic-slice_multiply_fusion
  4.4 78.8 %attend.1 = (bf16[512,1280]{1,0:T(8,128)(2,1)}, bf16[2,1280,480]{2,1,0:T(8,128)(2,1)}, bf16[2,1280,640]{2,1,0:T(8,128)(2,1)}, bf16[1280,640]{1,0:T(8,128)(2,1)},...) custom-call(bf16[128,1280]{1,0:T(8,128)(2,1)} %states.3, ...), custom_call_target="tpu_custom_call" | custom-call | tf_op jit(solution)/shard_map/attend/pallas_call | solution.py:763
  83.2 127.4 %mlp.1 = (bf16[128,1280]{1,0:T(8,128)(2,1)}, bf16[4,128,320]{2,1,0:T(8,128)(2,1)}, bf16[2,4,320,640]{3,2,1,0:T(8,128)(2,1)}, f32[128,1280]{1,0:T(8,128)}, f32[8,...) custom-call(bf16[4,128,320]{2,1,0:T(8,128)(2,1)} %get-tuple-element.30.attx, ...), custom_call_target="tpu_custom_call" | custom-call | tf_op jit(solution)/shard_map/mlp/pallas_call | solution.py:1049
  210.6 0.0 copy-start.1
  210.6 90.9 %back.1 = (bf16[128,1280]{1,0:T(8,128)(2,1)}, f32[40,15360]{1,0:T(8,128)}, f32[40,5120]{1,0:T(8,128)}, f32[3,1280]{1,0:T(4,128)}, f32[2,5120]{1,0:T(2,128)}) custom-call(bf16[4,128,320]{2,1,0:T(8,128)(2,1)} %get-tuple-element.36.grad_attx, bf16[2,1280,640]{2,1,0:T(8,128)(2,1)} %get-tuple-element.37.from_half, bf16[320,640]{1,0:T(8,128)(2,1)} %get-tuple-element.38.grad_down, ...), custom_call_target="tpu_custom_call" | custom-call | tf_op jit(solution)/shard_map/back/pallas_call | solution.py:1365
  301.5 0.0 copy-start
  301.6 1.5 dynamic-slice_bitcast_fusion.1
  303.0 1.3 dynamic-slice_bitcast_fusion
  304.4 0.0 copy-done.1
  304.4 0.7 copy.17
  305.1 1.7 copy.18
  306.8 2.1 copy.19
  308.9 0.0 copy-done
  308.9 1.4 copy.20
Async XLA Ops:
  210.6 93.7 %copy-start.1 = (bf16[128,1280]{1,0:T(8,128)(2,1)S(1)}, bf16[128,1280]{1,0:T(8,128)(2,1)}, u32[]{:S(2)}) copy-start(bf16[128,1280]{1,0:T(8,128)(2,1)} %get-tuple-element.67) | copy-start | bytes 983044
  301.5 7.3 %copy-start = (f32[40,15360]{1,0:T(8,128)S(1)}, f32[40,15360]{1,0:T(8,128)}, u32[]{:S(2)}) copy-start(f32[40,15360]{1,0:T(8,128)} %get-tuple-element.70) | copy-start | bytes 7372804

commit v9 on v8

--- a/solution.py
+++ b/solution.py
@@ -1427,6 +1427,31 @@
     )
 
 
+def finish_kernel(*refs):
+    count = len(refs) // 3
+    sources, results, held = refs[:count], refs[count : 2 * count], refs[2 * count : 3 * count]
+    sem = refs[-1]
+    copies = [begin(pltpu.make_async_copy(sources[at], held[at], sem.at[0, at])) for at in range(count)]
+    leaving = []
+    for at in range(count):
+        copies[at].wait()
+        leaving.append(begin(pltpu.make_async_copy(held[at], results[at], sem.at[1, at])))
+    for copy in leaving:
+        copy.wait()
+
+
+def finish_call(*arrays):
+    return pl.pallas_call(
+        finish_kernel,
+        out_shape=[jax.ShapeDtypeStruct(array.shape, array.dtype) for array in arrays],
+        in_specs=[in_hbm()] * len(arrays),
+        out_specs=[in_hbm()] * len(arrays),
+        scratch_shapes=[VMEM(array.shape, array.dtype) for array in arrays] + [dma(2, len(arrays))],
+        compiler_params=pltpu.CompilerParams(vmem_limit_bytes=LIMIT),
+        name="finish",
+    )(*arrays)
+
+
 def shards_split(states, cotangent, attn_weights, mlp_weights, feature_gains, unit_gains, block_place):
     tok_rows, model_width = states.shape
     ff_width = unit_gains.shape[0]
@@ -1453,6 +1478,7 @@
         grad_attx, grad_half, grad_down, grad_w_out, small, raw, query, both, att, inverse, states_all,
         w_qkv, qk_gain, block_place, grad_direct, rows,
     )
+    out_low, grad_states, grad_mlp, grad_attn = finish_call(out_low, grad_states, grad_mlp, grad_attn)
     rank = lax.axis_index(ALL)
     unit_rows_own = ff_width // (n_seq * n_ctx)
     return (

time: 311 us -> 308 us (level)
  local copies, waits for them, and re-layouts: 11.9 us -> 5.77 us
  Pallas kernels: 297 us -> 301 us
    unnamed x8 -> x0, local copies, waits for them, and re-layouts: 5.97 us -> none
    pallas_call x0 -> x1, Pallas kernels: none -> 3.68 us  [finish_call(): pl.pallas_call(finish_kernel, out_shape=[jax.ShapeDtypeStruct(array.shape...]
where the time goes in v9:
time: 308 us
  Pallas kernels  301 us (98%)
  local copies, waits for them, and re-layouts  5.77 us (2%)
    pallas_call x1, Pallas kernels, mlp_call(): pl.pallas_call(mlp_kernel, out_shape=[shape(tokens, low), shape(attx.shap...  127 us
    pallas_call x1, Pallas kernels, back_call(): pl.pallas_call(back_kernel, out_shape=[shape((tok_rows, model_width), low...  90.9 us
    pallas_call x1, Pallas kernels, attend_call(): pl.pallas_call(attend_kernel, out_shape=[shape((group_rows, model_width),...  78.8 us

profile of v9, /device:TPU:0, one launch (start us, length us, event | category | flops | bytes accessed | tf_op | source)
XLA Modules:
  0.0 307.9 jit_solution(559396944862050809)
XLA Ops:
  0.7 1.4 slice_bitcast_fusion
  2.1 0.1 dynamic-slice_reduce_fusion
  2.2 0.7 reshape.36.qk_gain
  2.9 0.9 fusion
  3.8 0.6 dynamic-slice_multiply_fusion
  4.4 78.8 %attend.1 = (bf16[512,1280]{1,0:T(8,128)(2,1)}, bf16[2,1280,480]{2,1,0:T(8,128)(2,1)}, bf16[2,1280,640]{2,1,0:T(8,128)(2,1)}, bf16[1280,640]{1,0:T(8,128)(2,1)},...) custom-call(bf16[128,1280]{1,0:T(8,128)(2,1)} %states.3, ...), custom_call_target="tpu_custom_call" | custom-call | tf_op jit(solution)/shard_map/attend/pallas_call | solution.py:763
  83.2 127.4 %mlp.1 = (bf16[128,1280]{1,0:T(8,128)(2,1)}, bf16[4,128,320]{2,1,0:T(8,128)(2,1)}, bf16[2,4,320,640]{3,2,1,0:T(8,128)(2,1)}, f32[128,1280]{1,0:T(8,128)}, f32[8,...) custom-call(bf16[4,128,320]{2,1,0:T(8,128)(2,1)} %get-tuple-element.34.attx, ...), custom_call_target="tpu_custom_call" | custom-call | tf_op jit(solution)/shard_map/mlp/pallas_call | solution.py:1049
  210.6 90.9 %back.1 = (bf16[128,1280]{1,0:T(8,128)(2,1)}, f32[40,15360]{1,0:T(8,128)}, f32[40,5120]{1,0:T(8,128)}, f32[3,1280]{1,0:T(4,128)}, f32[2,5120]{1,0:T(2,128)}) custom-call(bf16[4,128,320]{2,1,0:T(8,128)(2,1)} %get-tuple-element.40.grad_attx, bf16[2,1280,640]{2,1,0:T(8,128)(2,1)} %get-tuple-element.41.from_half, bf16[320,640]{1,0:T(8,128)(2,1)} %get-tuple-element.42.grad_down, ...), custom_call_target="tpu_custom_call" | custom-call | tf_op jit(solution)/shard_map/back/pallas_call | solution.py:1365
  301.5 3.7 %finish.1 = (bf16[128,1280]{1,0:T(8,128)(2,1)}, bf16[128,1280]{1,0:T(8,128)(2,1)}, f32[40,15360]{1,0:T(8,128)}, f32[40,5120]{1,0:T(8,128)}) custom-call(bf16[128,1280]{1,0:T(8,128)(2,1)} %get-tuple-element.39.refs_0_, bf16[128,1280]{1,0:T(8,128)(2,1)} %get-tuple-element.53.refs_1_, f32[40,15360]{1,0:T(8,128)} %get-tuple-element.54.refs_2_, ...), custom_call_target="tpu_custom_call" | custom-call | tf_op jit(solution)/shard_map/finish/pallas_call | solution.py:1444
  305.2 1.3 dynamic-slice_bitcast_fusion.1
  306.6 1.3 dynamic-slice_bitcast_fusion

commit v10 on v9

--- a/solution.py
+++ b/solution.py
@@ -989,8 +989,8 @@
         return (weights[which, core].astype(jnp.float32) + arrived[which].astype(jnp.float32)).astype(jnp.bfloat16)
 
     weight_grads(2, 1, hidden)
+    weight_grads(0, 0, grad_u)
     reduce_relay(part.at[1], tok_rows, sums.at[1], via.at[1], passed.at[1], b_send, b_recv)
-    weight_grads(0, 0, grad_u)
     down_half[...] = both_cores(2)
     down_across = [
         begin(remote(down_half.at[rows_at(seq_peer(step)[1], seq_rows)], down_got.at[step - 1], ds_send.at[step], ds_recv.at[step], seq_peer(step)[0]))
@@ -1243,13 +1243,13 @@
         grad_heads[2, head, at, :] = value.astype(low)
         return carry
 
+    onwards.append(cross_on(2, half_o, crossing[2]))
     lax.fori_loop(0, heads * tiles, one_key, 0)
     for which in range(3):
         full = jnp.concatenate([grad_heads[which, head] for head in range(heads)], axis=1)
         for half in range(CORES):
             grad_sides[half, :, which * part_cols : (which + 1) * part_cols] = full[:, half * part_cols : (half + 1) * part_cols]
     wide_tile = model_width // 5
-    onwards.append(cross_on(2, half_o, crossing[2]))
 
     def down(index, carry):
         at = rows_at(index, wide_tile)

time: 308 us -> 308 us (level)
  no operation moved by 1% of the time
where the time goes in v10:
time: 308 us
  Pallas kernels  301 us (98%)
  local copies, waits for them, and re-layouts  5.77 us (2%)
    pallas_call x1, Pallas kernels, mlp_call(): pl.pallas_call(mlp_kernel, out_shape=[shape(tokens, low), shape(attx.shap...  127 us
    pallas_call x1, Pallas kernels, back_call(): pl.pallas_call(back_kernel, out_shape=[shape((tok_rows, model_width), low...  90.9 us
    pallas_call x1, Pallas kernels, attend_call(): pl.pallas_call(attend_kernel, out_shape=[shape((group_rows, model_width),...  78.8 us

profile of v10, /device:TPU:0, one launch (start us, length us, event | category | flops | bytes accessed | tf_op | source)
XLA Modules:
  0.0 307.8 jit_solution(17965014362930885113)
XLA Ops:
  0.7 1.4 slice_bitcast_fusion
  2.1 0.1 dynamic-slice_reduce_fusion
  2.2 0.7 reshape.36.qk_gain
  2.9 0.9 fusion
  3.8 0.6 dynamic-slice_multiply_fusion
  4.4 78.8 %attend.1 = (bf16[512,1280]{1,0:T(8,128)(2,1)}, bf16[2,1280,480]{2,1,0:T(8,128)(2,1)}, bf16[2,1280,640]{2,1,0:T(8,128)(2,1)}, bf16[1280,640]{1,0:T(8,128)(2,1)},...) custom-call(bf16[128,1280]{1,0:T(8,128)(2,1)} %states.3, ...), custom_call_target="tpu_custom_call" | custom-call | tf_op jit(solution)/shard_map/attend/pallas_call | solution.py:763
  83.2 127.4 %mlp.1 = (bf16[128,1280]{1,0:T(8,128)(2,1)}, bf16[4,128,320]{2,1,0:T(8,128)(2,1)}, bf16[2,4,320,640]{3,2,1,0:T(8,128)(2,1)}, f32[128,1280]{1,0:T(8,128)}, f32[8,...) custom-call(bf16[4,128,320]{2,1,0:T(8,128)(2,1)} %get-tuple-element.34.attx, ...), custom_call_target="tpu_custom_call" | custom-call | tf_op jit(solution)/shard_map/mlp/pallas_call | solution.py:1049
  210.6 90.9 %back.1 = (bf16[128,1280]{1,0:T(8,128)(2,1)}, f32[40,15360]{1,0:T(8,128)}, f32[40,5120]{1,0:T(8,128)}, f32[3,1280]{1,0:T(4,128)}, f32[2,5120]{1,0:T(2,128)}) custom-call(bf16[4,128,320]{2,1,0:T(8,128)(2,1)} %get-tuple-element.40.grad_attx, bf16[2,1280,640]{2,1,0:T(8,128)(2,1)} %get-tuple-element.41.from_half, bf16[320,640]{1,0:T(8,128)(2,1)} %get-tuple-element.42.grad_down, ...), custom_call_target="tpu_custom_call" | custom-call | tf_op jit(solution)/shard_map/back/pallas_call | solution.py:1365
  301.5 3.7 %finish.1 = (bf16[128,1280]{1,0:T(8,128)(2,1)}, bf16[128,1280]{1,0:T(8,128)(2,1)}, f32[40,15360]{1,0:T(8,128)}, f32[40,5120]{1,0:T(8,128)}) custom-call(bf16[128,1280]{1,0:T(8,128)(2,1)} %get-tuple-element.39.refs_0_, bf16[128,1280]{1,0:T(8,128)(2,1)} %get-tuple-element.53.refs_1_, f32[40,15360]{1,0:T(8,128)} %get-tuple-element.54.refs_2_, ...), custom_call_target="tpu_custom_call" | custom-call | tf_op jit(solution)/shard_map/finish/pallas_call | solution.py:1444
  305.2 1.3 dynamic-slice_bitcast_fusion.1
  306.5 1.3 dynamic-slice_bitcast_fusion
